TPU v7x, 32 devices: a whole 2x2x4 slice. The times are simulated.
32 devices in a mesh: tm: 8 (over z, y), space: 4 (over x, core).
Axes of the slice: x: 2, y: 2, z: 4, core: 2. Of those that a mesh axis runs over, the one named last changes fastest.
Arguments:
- volume: float32 [8, 16, 256, 256], P('tm', 'space'), may hold values from -6 to 6
- prior_image: float32 [8, 16, 256, 256], P('tm', 'space'), may hold values from -6 to 6
- dual_pairs: float32 [8, 4, 16, 256, 256], P('tm', None, 'space'), may hold values from -0.3 to 0.3
- pair_cycle: int32 [8, 4], P('tm'), may hold values from -2 to 2, as said below
- pair_offset: int32 [8, 4], P('tm'), may hold values from -3 to 3
Outputs:
- volume_next: float32 [8, 16, 256, 256], P('tm', 'space')
- dual_next: float32 [8, 4, 16, 256, 256], P('tm', None, 'space')
Inputs may be any that keep to these rules, and one draw needn't show every extreme that they name: `pair_cycle`: each frame has at least one filled slot; filled slots come first, name distinct cycle offsets, and always name a partner frame inside 0 .. 7.
All inputs are finite; a program needn't handle non-finite values.
Results may differ from a plain program's by a relative error of at most 0.0003.
Values sent between devices are 32-bit elements; how exact they have to be, the bound alone decides.
No kernel may reach another device: no remote copies, remote signals or barrier semaphores. Data moves between devices by JAX's collectives and lax.ppermute only.
A program may use at most 64 MiB of HBM per device.

v0:
```python
import functools

import jax
import jax.numpy as jnp
from jax import lax
from jax.experimental import pallas as pl
from jax.experimental.pallas import tpu as pltpu
from jax.sharding import PartitionSpec as P


CYCLES = 8
HOPS = (-2, -1, 1, 2)

dual_step = 0.5
primal_step = 0.25
dual_bound = 0.3
fidelity = 1.0
scale = 1.0 / (1.0 + primal_step * fidelity)
flow = primal_step * scale
patch = -1.0 / (27.0 * 4.0)

KEPT = jax.ShapeDtypeStruct


LANES = 128
STEP = 16
EDGE = 16
RIM = 8


def chosen(table, hop):
    slot = jnp.int32(0)
    filled = table[0] == hop
    for k in range(1, 4):
        hit = table[k] == hop
        slot = jnp.where(hit, k, slot)
        filled = filled | hit
    return slot, filled


def offset_of(table, hop):
    offset = jnp.int32(0)
    for k in range(4):
        offset = jnp.where(table[k] == hop, table[4 + k], offset)
    return offset


def home_slot(table, hop):
    slot, filled = chosen(table, hop)
    count = jnp.int32(0)
    for k in range(4):
        count = count + (table[k] != 0).astype(jnp.int32)
    for other in HOPS:
        _, other_filled = chosen(table, other)
        count = count + ((other < hop) & jnp.logical_not(other_filled)).astype(jnp.int32)
    return jnp.where(filled, slot, count), filled


def pack_kernel(table, hops, *refs):
    sources, outs, (held,) = refs[:4], refs[4:8], refs[8:]
    rows = sources[0].shape[2]
    for half in range(2):
        held[half, pl.ds(0, RIM), :] = jnp.zeros((RIM, LANES), jnp.float32)
        held[half, pl.ds(RIM + rows, RIM), :] = jnp.zeros((RIM, LANES), jnp.float32)
    for j in range(4):
        offset = offset_of(table, hops[j])
        for half in range(2):
            lanes = pl.ds(half * LANES, LANES)
            held[half, pl.ds(RIM, rows), :] = sources[j][0, 0, :, lanes]
            outs[j][0, :, lanes] = held[half, pl.ds(RIM + offset, rows), :]


def pack(table, hops, dual):
    _, depth, rows, columns = dual.shape
    spec = lambda j: pl.BlockSpec(
        (1, 1, rows, columns), lambda z, t, h: (chosen(t, h[j])[0], z, 0, 0)
    )
    return pl.pallas_call(
        pack_kernel,
        name="pack",
        grid_spec=pltpu.PrefetchScalarGridSpec(
            num_scalar_prefetch=2,
            grid=(depth,),
            in_specs=[spec(j) for j in range(4)],
            out_specs=[pl.BlockSpec((1, rows, columns), lambda z, t, h: (z, 0, 0))] * 4,
            scratch_shapes=[pltpu.VMEM((2, rows + 2 * RIM, LANES), jnp.float32)],
        ),
        out_shape=[jax.ShapeDtypeStruct((depth, rows, columns), jnp.float32)] * 4,
        cost_estimate=pl.CostEstimate(flops=0, bytes_accessed=8 * 4 * depth * rows * columns, transcendentals=0),
    )(table, hops, dual, dual, dual, dual)


def box_rows(sums, z, half, start):
    return (
        sums[z, half, pl.ds(start - 1, STEP), :]
        + sums[z, half, pl.ds(start, STEP), :]
        + sums[z, half, pl.ds(start + 1, STEP), :]
    )


def box_lanes(left, right, lane):
    zero = jnp.zeros_like(left)
    left_up, right_up = pltpu.roll(left, 1, 1), pltpu.roll(right, 1, 1)
    left_down, right_down = pltpu.roll(left, LANES - 1, 1), pltpu.roll(right, LANES - 1, 1)
    first, last = lane == 0, lane == LANES - 1
    return (
        left + jnp.where(first, zero, left_up) + jnp.where(last, right_down, left_down),
        right + jnp.where(first, left_up, right_up) + jnp.where(last, zero, right_down),
    )


def pair_kernel(places, first, depth, hops, table, *refs):
    count = len(places)
    refs = list(refs)
    take = lambda k: [refs.pop(0) for _ in range(k)]
    tables = take(count)
    image, above, below, dual, start = take(5)
    partners, tails, heads = take(count), take(count), take(count)
    if not first:
        take(1)
    fresh_out, total = take(2)
    weights, gains = take(count), take(count)
    own, held, own_sums, in_sums, dual_in, fresh, sems, out_sems = refs
    rows, columns = image.shape[1:]
    per = 7

    def copies(i):
        place, stacked = places[i]
        slot, _ = chosen(table, hops[place])
        moves = []
        for half in range(2):
            lanes = pl.ds(half * LANES, LANES)
            moves.append((partners[i].at[:, :, lanes], held.at[i, pl.ds(1, depth), half, pl.ds(EDGE, rows), :]))
            moves.append((tails[i].at[stacked, :, lanes], held.at[i, 0, half, pl.ds(EDGE, rows), :]))
            moves.append((heads[i].at[stacked, :, lanes], held.at[i, depth + 1, half, pl.ds(EDGE, rows), :]))
        moves.append((dual.at[slot], dual_in.at[i]))
        return [pltpu.make_async_copy(a, b, sems.at[per * i + j]) for j, (a, b) in enumerate(moves)]

    base = per * count
    common = [
        pltpu.make_async_copy(image, own.at[pl.ds(1, depth), pl.ds(RIM, rows), :], sems.at[base]),
        pltpu.make_async_copy(above.at[0], own.at[0, pl.ds(RIM, rows), :], sems.at[base + 1]),
        pltpu.make_async_copy(below.at[0], own.at[depth + 1, pl.ds(RIM, rows), :], sems.at[base + 2]),
        pltpu.make_async_copy(start, total, sems.at[base + 3]),
    ]
    for c in common:
        c.start()
    incoming_copies = [copies(i) for i in range(count)]
    for group in incoming_copies:
        for c in group:
            c.start()

    for z in range(depth + 2):
        own[z, pl.ds(0, RIM), :] = jnp.zeros((RIM, columns), jnp.float32)
        own[z, pl.ds(RIM + rows, RIM), :] = jnp.zeros((RIM, columns), jnp.float32)
        for half in range(2):
            for i in range(count):
                held[i, z, half, pl.ds(0, EDGE), :] = jnp.zeros((EDGE, LANES), jnp.float32)
                held[i, z, half, pl.ds(EDGE + rows, EDGE), :] = jnp.zeros((EDGE, LANES), jnp.float32)
    for z in range(depth):
        for half in range(2):
            own_sums[z, half, pl.ds(0, RIM), :] = jnp.zeros((RIM, LANES), jnp.float32)
            own_sums[z, half, pl.ds(RIM + rows, RIM), :] = jnp.zeros((RIM, LANES), jnp.float32)

    row = lax.broadcasted_iota(jnp.int32, (STEP, LANES), 0)
    lane = lax.broadcasted_iota(jnp.int32, (STEP, LANES), 1)

    for c in common:
        c.wait()

    out_copies = []
    for i in range(count):
        place, _ = places[i]
        hop = hops[place]
        own_offset = offset_of(table, hop)
        slot, filled = home_slot(table, hop)
        bound = jnp.where(filled, jnp.float32(dual_bound), jnp.float32(0.0))
        for c in incoming_copies[i]:
            c.wait()
        _, in_filled = chosen(tables[i], -hop)
        in_offset = offset_of(tables[i], -hop)
        low = jnp.where(in_filled, -in_offset, 4 * rows)
        high = rows - 1 - in_offset

        def own_contrast(z, half, y):
            return held[i, z, half, pl.ds(EDGE + y - own_offset, STEP), :] - own[
                z, pl.ds(pl.multiple_of(RIM + y, 8), STEP), pl.ds(half * LANES, LANES)
            ]

        def in_contrast(z, half, y, inside):
            mine = own[z, pl.ds(pl.multiple_of(RIM + y, 8), STEP), pl.ds(half * LANES, LANES)]
            if inside is not None:
                mine = jnp.where(inside, mine, 0.0)
            return mine - held[i, z, half, pl.ds(EDGE + y + in_offset, STEP), :]

        def add_slices(sums, contrast, y):
            for half in range(2):
                squares = []
                for z in range(depth + 2):
                    value = contrast(z, half)
                    squares.append(value * value)
                for z in range(depth):
                    sums[z, half, pl.ds(pl.multiple_of(RIM + y, 8), STEP), :] = squares[z] + squares[z + 1] + squares[z + 2]

        def gather(step, carry):
            y = step * STEP
            add_slices(own_sums, lambda z, half: own_contrast(z, half, y), y)
            return carry

        def gather_in(step, carry):
            y = step * STEP - RIM
            inside = (row + y >= low) & (row + y <= high)
            add_slices(in_sums, lambda z, half: in_contrast(z, half, y, inside), y)
            return carry

        def apply(step, carry):
            y = pl.multiple_of(step * STEP, STEP)
            inside = (row + y >= low) & (row + y <= high)
            here = pl.ds(y, STEP)
            for z in range(depth):
                own_box = box_lanes(
                    box_rows(own_sums, z, 0, RIM + y), box_rows(own_sums, z, 1, RIM + y), lane
                )
                in_box = box_lanes(
                    box_rows(in_sums, z, 0, RIM + y), box_rows(in_sums, z, 1, RIM + y), lane
                )
                for half in range(2):
                    lanes = pl.ds(half * LANES, LANES)
                    weight = jnp.exp(own_box[half] * patch)
                    value = dual_in[i, z, here, lanes] + (dual_step * weight) * own_contrast(z + 1, half, y)
                    value = jnp.minimum(jnp.maximum(value, -bound), bound)
                    fresh[i, z, here, lanes] = value
                    flux = (weight * value) * flow
                    if first and i == 0:
                        mine = own[z + 1, pl.ds(pl.multiple_of(RIM + y, 8), STEP), lanes]
                        flux = flux + (scale * mine)
                        total[z, here, lanes] = (flow * fidelity) * total[z, here, lanes] + flux
                    else:
                        total[z, here, lanes] = total[z, here, lanes] + flux
                    weight = jnp.exp(in_box[half] * patch)
                    gain = (dual_step * weight) * in_contrast(z + 1, half, y, None)
                    weights[i][z, here, lanes] = jnp.where(inside, weight, 0.0)
                    gains[i][z, here, lanes] = gain
            return carry

        lax.fori_loop(0, rows // STEP, gather, 0)
        lax.fori_loop(0, (rows + 2 * RIM) // STEP, gather_in, 0)
        lax.fori_loop(0, rows // STEP, apply, 0)

        done = pltpu.make_async_copy(fresh.at[i], fresh_out.at[slot], out_sems.at[i])
        done.start()
        out_copies.append(done)
    for c in out_copies:
        c.wait()


def pairs(places, hops, table, tables, image, above, below, dual, start, partners, tails, heads, fresh=None):
    count = len(places)
    depth, rows, columns = image.shape
    first = fresh is None
    f32 = jnp.float32
    block = KEPT(image.shape, f32)
    any_spec = pl.BlockSpec(memory_space=pl.ANY)
    vmem_spec = pl.BlockSpec(memory_space=pltpu.VMEM)
    smem = pl.BlockSpec(memory_space=pltpu.SMEM)
    operands = [hops, table, *tables, image, above, below, dual, start, *partners, *tails, *heads]
    specs = [smem] * (2 + count) + [any_spec] * (len(operands) - 2 - count)
    aliases = {}
    if not first:
        aliases = {len(operands): 0}
        operands.append(fresh)
        specs.append(any_spec)
    cells = depth * rows * columns
    return pl.pallas_call(
        functools.partial(pair_kernel, places, first, depth),
        name="pairs_first" if first else "pairs_last",
        in_specs=specs,
        out_specs=[any_spec] + [vmem_spec] * (1 + 2 * count),
        out_shape=[jax.ShapeDtypeStruct(dual.shape, f32)] + [block] * (1 + 2 * count),
        input_output_aliases=aliases,
        scratch_shapes=[
            pltpu.VMEM((depth + 2, rows + 2 * RIM, columns), f32),
            pltpu.VMEM((count, depth + 2, 2, rows + 2 * EDGE, LANES), f32),
            pltpu.VMEM((depth, 2, rows + 2 * RIM, LANES), f32),
            pltpu.VMEM((depth, 2, rows + 2 * RIM, LANES), f32),
            pltpu.VMEM((count, depth, rows, columns), f32),
            pltpu.VMEM((count, depth, rows, columns), f32),
            pltpu.SemaphoreType.DMA((7 * count + 4,)),
            pltpu.SemaphoreType.DMA((count,)),
        ],
        compiler_params=pltpu.CompilerParams(vmem_limit_bytes=28 << 20),
        cost_estimate=pl.CostEstimate(
            flops=count * 60 * cells, bytes_accessed=4 * (3 + 7 * count) * cells, transcendentals=2 * count * cells
        ),
    )(*operands)


def settle_kernel(count, total, *refs):
    duals, weights, gains, out = refs[:count], refs[count : 2 * count], refs[2 * count : 3 * count], refs[-1]
    depth, rows, _ = total.shape

    def body(step, carry):
        here = pl.ds(pl.multiple_of(step * STEP, STEP), STEP)
        for z in range(depth):
            arriving = None
            for i in range(count):
                value = duals[i][z, here, :] + gains[i][z, here, :]
                value = weights[i][z, here, :] * jnp.minimum(jnp.maximum(value, -dual_bound), dual_bound)
                arriving = value if arriving is None else arriving + value
            out[z, here, :] = total[z, here, :] - flow * arriving
        return carry

    lax.fori_loop(0, rows // STEP, body, 0)


def settle(total, duals, weights, gains, last):
    count = len(duals)
    vmem_spec = pl.BlockSpec(memory_space=pltpu.VMEM)
    return pl.pallas_call(
        functools.partial(settle_kernel, count),
        in_specs=[vmem_spec] * (1 + 3 * count),
        out_specs=vmem_spec,
        out_shape=(jax.ShapeDtypeStruct if last else KEPT)(total.shape, jnp.float32),
        compiler_params=pltpu.CompilerParams(vmem_limit_bytes=20 << 20),
        cost_estimate=pl.CostEstimate(
            flops=5 * count * total.size, bytes_accessed=4 * (2 + 3 * count) * total.size, transcendentals=0
        ),
    )(total, *duals, *weights, *gains)


def shards(volume, prior_image, dual_pairs, pair_cycle, pair_offset):
    frames = lax.axis_size("tm")
    spaces = lax.axis_size("space")
    stride = frames // CYCLES
    image = volume[0]
    dual = dual_pairs[0]
    cycle_of = lambda t: t // stride
    every = range(frames)
    swap = [(t, t + stride if cycle_of(t) % 2 == 0 else t - stride) for t in every]
    cross = [(t, t - stride if cycle_of(t) % 2 == 0 else t + stride) for t in every]
    cross = [(a, b) for a, b in cross if 0 <= b < frames]
    later = [(t, t + 2 * stride) for t in every if t + 2 * stride < frames]
    sooner = [(t, t - 2 * stride) for t in every if t - 2 * stride >= 0]
    relay = [(t, t + 2 * stride if cycle_of(t) % 2 == 0 else t - 2 * stride) for t in every]
    relay = [(a, b) for a, b in relay if 0 <= b < frames]
    onward = [(s, s + 1) for s in range(spaces - 1)]
    backward = [(s + 1, s) for s in range(spaces - 1)]

    def send(x, pairs_, axis="tm"):
        return lax.ppermute(x, axis, pairs_)

    parity = (lax.axis_index("tm") // stride) % 2
    near = (1 - 2 * parity).astype(jnp.int32)
    hops = jnp.stack([near, -near, jnp.int32(2), jnp.int32(-2)])
    table = jnp.concatenate([pair_cycle[0], pair_offset[0]])

    near_image = send(image, swap)
    before_image = send(image, later)
    after_image = send(image, sooner)
    near_dual, far_dual, later_dual, sooner_dual = pack(table, hops, dual)
    near_dual = send(near_dual, swap)
    far_dual = send(far_dual, cross)
    far_image = send(near_image, relay)
    near_table = send(table, swap)
    far_table = send(table, cross)
    before_table = send(table, later)
    after_table = send(table, sooner)

    stack = (image, near_image, after_image, before_image)
    bottoms = jnp.stack([x[-1] for x in stack])
    tops = jnp.stack([x[0] for x in stack])
    tails = send(bottoms, onward, "space")
    heads = send(tops, backward, "space")
    before_dual = send(later_dual, later)
    after_dual = send(sooner_dual, sooner)
    fresh, total, wn, wa, gn, ga = pairs(
        ((0, 1), (2, 2)), hops, table, (near_table, after_table), image, tails, heads, dual, prior_image[0],
        (near_image, after_image), (tails,) * 2, (heads,) * 2,
    )
    far_tail = send(far_image[-1:], onward, "space")
    far_head = send(far_image[:1], backward, "space")
    fresh, total, wb, wf, gb, gf = pairs(
        ((3, 3), (1, 0)), hops, table, (before_table, far_table), image, tails, heads, dual, total,
        (before_image, far_image), (tails, far_tail), (heads, far_head), fresh,
    )
    volume_next = settle(
        total, (near_dual, after_dual, before_dual, far_dual), (wn, wa, wb, wf), (gn, ga, gb, gf), True
    )
    return (volume_next[None], fresh[None])


def solution(mesh):
    return jax.shard_map(
        shards,
        mesh=mesh,
        in_specs=(
            P("tm", "space", None, None),
            P("tm", "space", None, None),
            P("tm", None, "space", None, None),
            P("tm", None),
            P("tm", None),
        ),
        out_specs=(P("tm", "space", None, None), P("tm", None, "space", None, None)),
        check_vma=False,
    )
```

profile of v0, /device:TPU:24, one launch (start us, length us, event | category | flops | bytes accessed | tf_op | source)
XLA Modules:
  0.0 121.4 jit_solution(11500966352411425943)
XLA Ops:
  0.6 1.6 %collective-permute-start.2 = (f32[4,256,256]{2,1,0:T(8,128)}, f32[4,256,256]{2,1,0:T(8,128)}, u32[]{:S(2)}, u32[]{:S(2)}) collective-permute-start(f32[4,256,256]{2,1,0:T(8,128)} %bitcast.19), channel_id=1, source_target_pairs={{0,4},{4,0},{8,12},{12,8},{16,20},{20,16},{24,28},{28,24},{1,5},{5... | collective-permute-start | bytes 3145736 | tf_op jit(solution)/shard_map/ppermute | solution.py:350
  2.2 2.4 %collective-permute-start.3 = (f32[4,256,256]{2,1,0:T(8,128)}, f32[4,256,256]{2,1,0:T(8,128)S(1)}, u32[]{:S(2)}, u32[]{:S(2)}) collective-permute-start(f32[4,256,256]{2,1,0:T(8,128)} %bitcast.20), channel_id=1, source_target_pairs={{8,0},{12,4},{16,8},{20,12},{24,16},{28,20},{9,1},{13,5},{17,9},{2... | collective-permute-start | bytes 3145736 | tf_op jit(solution)/shard_map/ppermute | solution.py:350
  4.7 1.3 %collective-permute-start.4 = (f32[4,256,256]{2,1,0:T(8,128)}, f32[4,256,256]{2,1,0:T(8,128)S(1)}, u32[]{:S(2)}, u32[]{:S(2)}) collective-permute-start(f32[4,256,256]{2,1,0:T(8,128)} %bitcast.21), channel_id=1, source_target_pairs={{0,8},{4,12},{8,16},{12,20},{16,24},{20,28},{1,9},{5,13},{9,17},{1... | collective-permute-start | bytes 3145736 | tf_op jit(solution)/shard_map/ppermute | solution.py:350
  6.0 1.1 slice_bitcast_fusion
  7.0 18.9 %collective-permute-done.2.refs_7_ = f32[4,256,256]{2,1,0:T(8,128)} collective-permute-done((f32[4,256,256]{2,1,0:T(8,128)}, f32[4,256,256]{2,1,0:T(8,128)}, u32[]{:S(2)}, u32[]{:S(2)}) %collective-permute-start.2) | collective-permute-done | bytes 1048608 | tf_op jit(solution)/shard_map/ppermute | solution.py:350
  25.9 1.1 fusion.1
  27.1 4.0 %collective-permute-done.4.refs_7_ = f32[4,256,256]{2,1,0:T(8,128)S(1)} collective-permute-done((f32[4,256,256]{2,1,0:T(8,128)}, f32[4,256,256]{2,1,0:T(8,128)S(1)}, u32[]{:S(2)}, u32[]{:S(2)}) %collective-permute-start.4) | collective-permute-done | bytes 1048608 | tf_op jit(solution)/shard_map/ppermute | solution.py:350
  32.1 1.0 pad_maximum_fusion
  33.1 1.3 %collective-permute-start.5 = (f32[4,256,256]{2,1,0:T(8,128)}, f32[4,256,256]{2,1,0:T(8,128)S(1)}, u32[]{:S(2)}, u32[]{:S(2)}) collective-permute-start(f32[4,256,256]{2,1,0:T(8,128)} %pad_maximum_fusion), channel_id=1, source_target_pairs={{0,1},{1,2},{2,3},{4,5},{5,6},{6,7},{8,9},{9,10},{10,11},{12,13},{... | collective-permute-start | bytes 3145736 | tf_op jit(solution)/shard_map/ppermute | solution.py:350
  34.5 1.3 %collective-permute-start.9 = (f32[4,256,256]{2,1,0:T(8,128)}, f32[4,256,256]{2,1,0:T(8,128)}, u32[]{:S(2)}, u32[]{:S(2)}) collective-permute-start(f32[4,256,256]{2,1,0:T(8,128)} %collective-permute-done.2.refs_7_), channel_id=1, source_target_pairs={{0,8},{8,16},{12,4},{16,24},{20,12},{28,20},{1,9},{9,17},{13,5},{1... | collective-permute-start | bytes 3145736 | tf_op jit(solution)/shard_map/ppermute | solution.py:350
  35.8 1.0 pad_maximum_fusion.1
  36.8 1.3 %collective-permute-start.6 = (f32[4,256,256]{2,1,0:T(8,128)}, f32[4,256,256]{2,1,0:T(8,128)S(1)}, u32[]{:S(2)}, u32[]{:S(2)}) collective-permute-start(f32[4,256,256]{2,1,0:T(8,128)} %pad_maximum_fusion.1), channel_id=1, source_target_pairs={{1,0},{2,1},{3,2},{5,4},{6,5},{7,6},{9,8},{10,9},{11,10},{13,12},{... | collective-permute-start | bytes 3145736 | tf_op jit(solution)/shard_map/ppermute | solution.py:350
  38.2 2.5 %collective-permute-start.7 = (s32[8]{0:T(128)S(1)}, s32[8]{0:T(128)S(1)}, u32[]{:S(2)}, u32[]{:S(2)}) collective-permute-start(s32[8]{0:T(128)S(1)} %pad_add_fusion.1.table), channel_id=1, source_target_pairs={{0,4},{4,0},{8,12},{12,8},{16,20},{20,16},{24,28},{28,24},{1,5},{5... | collective-permute-start | bytes 104 | tf_op jit(solution)/shard_map/ppermute | solution.py:350
  40.7 2.1 %collective-permute-start.8 = (s32[8]{0:T(128)S(1)}, s32[8]{0:T(128)S(1)}, u32[]{:S(2)}, u32[]{:S(2)}) collective-permute-start(s32[8]{0:T(128)S(1)} %pad_add_fusion.1.table), channel_id=1, source_target_pairs={{8,0},{12,4},{16,8},{20,12},{24,16},{28,20},{9,1},{13,5},{17,9},{2... | collective-permute-start | bytes 104 | tf_op jit(solution)/shard_map/ppermute | solution.py:350
  43.4 5.5 %pack.1 = (f32[4,256,256]{2,1,0:T(8,128)}, f32[4,256,256]{2,1,0:T(8,128)}, f32[4,256,256]{2,1,0:T(8,128)}, f32[4,256,256]{2,1,0:T(8,128)}) custom-call(s32[8]{0:T(128)} %copy-done.9, s32[4]{0:T(128)} %pad_add_fusion.hops, f32[4,4,256,256]{3,2,1,0:T(8,128)} %bitcast.13, f32[4,4,256,256]{3,2,1,0:T(8,128)} %bitcast.14, f32[4,4,256,256]{3,2,1,0:T(8,128)} %bitcast.15, ...), custom_call_target="tpu_custom_call" | custom-call | bytes 8388608 | tf_op jit(solution)/shard_map/pack/pallas_call | solution.py:78
  48.9 1.3 %collective-permute-start = (s32[8]{0:T(128)}, s32[8]{0:T(128)S(1)}, u32[]{:S(2)}, u32[]{:S(2)}) collective-permute-start(s32[8]{0:T(128)} %copy-done.9), channel_id=1, source_target_pairs={{0,8},{4,12},{8,16},{12,20},{16,24},{20,28},{1,9},{5,13},{9,17},{1... | collective-permute-start | bytes 104 | tf_op jit(solution)/shard_map/ppermute | solution.py:350
  50.2 13.6 %collective-permute-start.1 = (s32[8]{0:T(128)}, s32[8]{0:T(128)S(1)}, u32[]{:S(2)}, u32[]{:S(2)}) collective-permute-start(s32[8]{0:T(128)} %copy-done.9), channel_id=1, source_target_pairs={{4,8},{8,4},{12,16},{16,12},{20,24},{24,20},{5,9},{9,5},{13,17},{1... | collective-permute-start | bytes 104 | tf_op jit(solution)/shard_map/ppermute | solution.py:350
  63.9 1.7 %collective-permute-done.1.refs_1_ = s32[8]{0:T(128)S(1)} collective-permute-done((s32[8]{0:T(128)}, s32[8]{0:T(128)S(1)}, u32[]{:S(2)}, u32[]{:S(2)}) %collective-permute-start.1) | collective-permute-done | bytes 64 | tf_op jit(solution)/shard_map/ppermute | solution.py:350
  65.5 2.1 %collective-permute-start.13 = (f32[4,256,256]{2,1,0:T(8,128)}, f32[4,256,256]{2,1,0:T(8,128)S(1)}, u32[]{:S(2)}, u32[]{:S(2)}) collective-permute-start(f32[4,256,256]{2,1,0:T(8,128)} %get-tuple-element.22), channel_id=1, source_target_pairs={{8,0},{12,4},{16,8},{20,12},{24,16},{28,20},{9,1},{13,5},{17,9},{2... | collective-permute-start | bytes 3145736 | tf_op jit(solution)/shard_map/ppermute | solution.py:350
  67.6 1.3 %collective-permute-start.14 = (f32[4,256,256]{2,1,0:T(8,128)}, f32[4,256,256]{2,1,0:T(8,128)S(1)}, u32[]{:S(2)}, u32[]{:S(2)}) collective-permute-start(f32[4,256,256]{2,1,0:T(8,128)} %get-tuple-element.23), channel_id=1, source_target_pairs={{0,8},{4,12},{8,16},{12,20},{16,24},{20,28},{1,9},{5,13},{9,17},{1... | collective-permute-start | bytes 3145736 | tf_op jit(solution)/shard_map/ppermute | solution.py:350
  68.9 7.3 %collective-permute-start.15 = (f32[4,256,256]{2,1,0:T(8,128)}, f32[4,256,256]{2,1,0:T(8,128)S(1)}, u32[]{:S(2)}, u32[]{:S(2)}) collective-permute-start(f32[4,256,256]{2,1,0:T(8,128)} %get-tuple-element.24), channel_id=1, source_target_pairs={{4,8},{8,4},{12,16},{16,12},{20,24},{24,20},{5,9},{9,5},{13,17},{1... | collective-permute-start | bytes 3145736 | tf_op jit(solution)/shard_map/ppermute | solution.py:350
  76.3 1.1 fusion
  77.4 1.3 %collective-permute-start.10 = (f32[1,256,256]{2,1,0:T(8,128)S(1)}, f32[1,256,256]{2,1,0:T(8,128)S(1)}, u32[]{:S(2)}, u32[]{:S(2)}) collective-permute-start(f32[1,256,256]{2,1,0:T(8,128)S(1)} %get-tuple-element.35), channel_id=1, source_target_pairs={{0,1},{1,2},{2,3},{4,5},{5,6},{6,7},{8,9},{9,10},{10,11},{12,13},{... | collective-permute-start | bytes 786440 | tf_op jit(solution)/shard_map/ppermute | solution.py:350
  78.7 1.1 collective-permute-done.10.refs_10_
  79.8 1.3 %collective-permute-start.11 = (f32[1,256,256]{2,1,0:T(8,128)S(1)}, f32[1,256,256]{2,1,0:T(8,128)S(1)}, u32[]{:S(2)}, u32[]{:S(2)}) collective-permute-start(f32[1,256,256]{2,1,0:T(8,128)S(1)} %get-tuple-element.34), channel_id=1, source_target_pairs={{1,0},{2,1},{3,2},{5,4},{6,5},{7,6},{9,8},{10,9},{11,10},{13,12},{... | collective-permute-start | bytes 786440 | tf_op jit(solution)/shard_map/ppermute | solution.py:350
  81.1 2.2 %copy-done = f32[1,4,4,256,256]{4,3,2,1,0:T(8,128)S(1)} copy-done((f32[1,4,4,256,256]{4,3,2,1,0:T(8,128)S(1)}, f32[1,4,4,256,256]{4,3,2,1,0:T(8,128)}, u32[]{:S(2)}) %copy-start) | copy-done | bytes 4194328
  83.3 1.2 %copy-done.6 = f32[4,256,256]{2,1,0:T(8,128)S(1)} copy-done((f32[4,256,256]{2,1,0:T(8,128)S(1)}, f32[4,256,256]{2,1,0:T(8,128)}, u32[]{:S(2)}) %copy-start.6) | copy-done | bytes 1048600
  84.5 1.2 %copy-done.7 = f32[1,4,256,256]{3,2,1,0:T(8,128)S(1)} copy-done((f32[1,4,256,256]{3,2,1,0:T(8,128)S(1)}, f32[1,4,256,256]{3,2,1,0:T(8,128)}, u32[]{:S(2)}) %copy-start.7) | copy-done | bytes 1048600
  86.3 9.9 %pairs_first.1 = (f32[4,4,256,256]{3,2,1,0:T(8,128)}, f32[4,256,256]{2,1,0:T(8,128)S(1)}, f32[4,256,256]{2,1,0:T(8,128)S(1)}, f32[4,256,256]{2,1,0:T(8,128)S(1)}...) custom-call(s32[4]{0:T(128)S(1)} %copy-done.8, s32[8]{0:T(128)S(1)} %copy-done.10, ...), custom_call_target="tpu_custom_call" | custom-call | flops 31457280 | bytes 17825792 | tf_op jit(solution)/shard_map/pairs_first/pallas_call | solution.py:274
  96.2 8.8 %pairs_last.1 = (f32[4,4,256,256]{3,2,1,0:T(8,128)}, f32[4,256,256]{2,1,0:T(8,128)S(1)}, f32[4,256,256]{2,1,0:T(8,128)S(1)}, f32[4,256,256]{2,1,0:T(8,128)S(1)},...) custom-call(s32[4]{0:T(128)S(1)} %copy-done.8, s32[8]{0:T(128)S(1)} %copy-done.10, ...), custom_call_target="tpu_custom_call", output_to_operand_aliasing={{0}: (15, {})} | custom-call | flops 31457280 | bytes 17825792 | tf_op jit(solution)/shard_map/pairs_last/pallas_call | solution.py:274
  105.1 14.4 %collective-permute-done.15.refs_3_ = f32[4,256,256]{2,1,0:T(8,128)S(1)} collective-permute-done((f32[4,256,256]{2,1,0:T(8,128)}, f32[4,256,256]{2,1,0:T(8,128)S(1)}, u32[]{:S(2)}, u32[]{:S(2)}) %collective-permute-start.15) | collective-permute-done | bytes 1048608 | tf_op jit(solution)/shard_map/ppermute | solution.py:350
  119.5 2.0 %shard_map.68 = f32[4,256,256]{2,1,0:T(8,128)} custom-call(f32[4,256,256]{2,1,0:T(8,128)S(1)} %get-tuple-element.20.total, f32[4,256,256]{2,1,0:T(8,128)S(1)} %collective-permute-done.12.refs_0_, f32[4,256,256]{2,1,0:T(8,128)S(1)} %collective-permute-done.13.refs_1_, f32[4,256,256]{2,1,0:T(8,128)S(1)} %collective-permute-done.14.refs_2_, ...), custom_call_target="tpu_custom_call" | custom-call | flops 5242880 | bytes 14680064 | tf_op jit(solution)/shard_map/pallas_call | solution.py:319
  (39 shorter events, 2.4 us)
Async XLA Ops:
  0.6 37.5 %copy-start.11 = (s32[1,4]{1,0:T(1,128)S(1)}, s32[1,4]{1,0:T(1,128)}, u32[]{:S(2)}) copy-start(s32[1,4]{1,0:T(1,128)} %param.9) | copy-start | bytes 52
  0.6 37.5 %copy-start.12 = (s32[1,4]{1,0:T(1,128)S(1)}, s32[1,4]{1,0:T(1,128)}, u32[]{:S(2)}) copy-start(s32[1,4]{1,0:T(1,128)} %param.8) | copy-start | bytes 52
  0.6 25.3 %collective-permute-start.2 = (f32[4,256,256]{2,1,0:T(8,128)}, f32[4,256,256]{2,1,0:T(8,128)}, u32[]{:S(2)}, u32[]{:S(2)}) collective-permute-start(f32[4,256,256]{2,1,0:T(8,128)} %bitcast.19), channel_id=1, source_target_pairs={{0,4},{4,0},{8,12},{12,8},{16,20},{20,16},{24,28},{28,24},{1,5},{5... | collective-permute-start | bytes 3145736 | tf_op jit(solution)/shard_map/ppermute | solution.py:350
  2.2 24.8 %collective-permute-start.3 = (f32[4,256,256]{2,1,0:T(8,128)}, f32[4,256,256]{2,1,0:T(8,128)S(1)}, u32[]{:S(2)}, u32[]{:S(2)}) collective-permute-start(f32[4,256,256]{2,1,0:T(8,128)} %bitcast.20), channel_id=1, source_target_pairs={{8,0},{12,4},{16,8},{20,12},{24,16},{28,20},{9,1},{13,5},{17,9},{2... | collective-permute-start | bytes 3145736 | tf_op jit(solution)/shard_map/ppermute | solution.py:350
  4.7 26.4 %collective-permute-start.4 = (f32[4,256,256]{2,1,0:T(8,128)}, f32[4,256,256]{2,1,0:T(8,128)S(1)}, u32[]{:S(2)}, u32[]{:S(2)}) collective-permute-start(f32[4,256,256]{2,1,0:T(8,128)} %bitcast.21), channel_id=1, source_target_pairs={{0,8},{4,12},{8,16},{12,20},{16,24},{20,28},{1,9},{5,13},{9,17},{1... | collective-permute-start | bytes 3145736 | tf_op jit(solution)/shard_map/ppermute | solution.py:350
  27.0 4.1 %copy-start.5 = (f32[4,256,256]{2,1,0:T(8,128)}, f32[4,256,256]{2,1,0:T(8,128)S(1)}, u32[]{:S(2)}) copy-start(f32[4,256,256]{2,1,0:T(8,128)S(1)} %collective-permute-done.3.refs_8_) | copy-start | bytes 3145732
  31.1 1.0 copy-start.3
  33.1 34.5 %collective-permute-start.5 = (f32[4,256,256]{2,1,0:T(8,128)}, f32[4,256,256]{2,1,0:T(8,128)S(1)}, u32[]{:S(2)}, u32[]{:S(2)}) collective-permute-start(f32[4,256,256]{2,1,0:T(8,128)} %pad_maximum_fusion), channel_id=1, source_target_pairs={{0,1},{1,2},{2,3},{4,5},{5,6},{6,7},{8,9},{9,10},{10,11},{12,13},{... | collective-permute-start | bytes 3145736 | tf_op jit(solution)/shard_map/ppermute | solution.py:350
  34.5 34.4 %collective-permute-start.9 = (f32[4,256,256]{2,1,0:T(8,128)}, f32[4,256,256]{2,1,0:T(8,128)}, u32[]{:S(2)}, u32[]{:S(2)}) collective-permute-start(f32[4,256,256]{2,1,0:T(8,128)} %collective-permute-done.2.refs_7_), channel_id=1, source_target_pairs={{0,8},{8,16},{12,4},{16,24},{20,12},{28,20},{1,9},{9,17},{13,5},{1... | collective-permute-start | bytes 3145736 | tf_op jit(solution)/shard_map/ppermute | solution.py:350
  36.8 40.5 %collective-permute-start.6 = (f32[4,256,256]{2,1,0:T(8,128)}, f32[4,256,256]{2,1,0:T(8,128)S(1)}, u32[]{:S(2)}, u32[]{:S(2)}) collective-permute-start(f32[4,256,256]{2,1,0:T(8,128)} %pad_maximum_fusion.1), channel_id=1, source_target_pairs={{1,0},{2,1},{3,2},{5,4},{6,5},{7,6},{9,8},{10,9},{11,10},{13,12},{... | collective-permute-start | bytes 3145736 | tf_op jit(solution)/shard_map/ppermute | solution.py:350
  38.2 5.2 %copy-start.9 = (s32[8]{0:T(128)}, s32[8]{0:T(128)S(1)}, u32[]{:S(2)}) copy-start(s32[8]{0:T(128)S(1)} %pad_add_fusion.1.table) | copy-start | bytes 100
  38.2 10.7 %collective-permute-start.7 = (s32[8]{0:T(128)S(1)}, s32[8]{0:T(128)S(1)}, u32[]{:S(2)}, u32[]{:S(2)}) collective-permute-start(s32[8]{0:T(128)S(1)} %pad_add_fusion.1.table), channel_id=1, source_target_pairs={{0,4},{4,0},{8,12},{12,8},{16,20},{20,16},{24,28},{28,24},{1,5},{5... | collective-permute-start | bytes 104 | tf_op jit(solution)/shard_map/ppermute | solution.py:350
  40.7 9.5 %collective-permute-start.8 = (s32[8]{0:T(128)S(1)}, s32[8]{0:T(128)S(1)}, u32[]{:S(2)}, u32[]{:S(2)}) collective-permute-start(s32[8]{0:T(128)S(1)} %pad_add_fusion.1.table), channel_id=1, source_target_pairs={{8,0},{12,4},{16,8},{20,12},{24,16},{28,20},{9,1},{13,5},{17,9},{2... | collective-permute-start | bytes 104 | tf_op jit(solution)/shard_map/ppermute | solution.py:350
  43.4 37.7 %copy-start.2 = (f32[1,4,256,256]{3,2,1,0:T(8,128)S(1)}, f32[1,4,256,256]{3,2,1,0:T(8,128)}, u32[]{:S(2)}) copy-start(f32[1,4,256,256]{3,2,1,0:T(8,128)} %param.5) | copy-start | bytes 3145732
  43.4 37.7 %copy-start.8 = (s32[4]{0:T(128)S(1)}, s32[4]{0:T(128)}, u32[]{:S(2)}) copy-start(s32[4]{0:T(128)} %pad_add_fusion.hops) | copy-start | bytes 52
  48.9 14.9 %collective-permute-start = (s32[8]{0:T(128)}, s32[8]{0:T(128)S(1)}, u32[]{:S(2)}, u32[]{:S(2)}) collective-permute-start(s32[8]{0:T(128)} %copy-done.9), channel_id=1, source_target_pairs={{0,8},{4,12},{8,16},{12,20},{16,24},{20,28},{1,9},{5,13},{9,17},{1... | collective-permute-start | bytes 104 | tf_op jit(solution)/shard_map/ppermute | solution.py:350
  50.2 15.3 %collective-permute-start.1 = (s32[8]{0:T(128)}, s32[8]{0:T(128)S(1)}, u32[]{:S(2)}, u32[]{:S(2)}) collective-permute-start(s32[8]{0:T(128)} %copy-done.9), channel_id=1, source_target_pairs={{4,8},{8,4},{12,16},{16,12},{20,24},{24,20},{5,9},{9,5},{13,17},{1... | collective-permute-start | bytes 104 | tf_op jit(solution)/shard_map/ppermute | solution.py:350
  63.8 41.3 %collective-permute-start.12 = (f32[4,256,256]{2,1,0:T(8,128)}, f32[4,256,256]{2,1,0:T(8,128)S(1)}, u32[]{:S(2)}, u32[]{:S(2)}) collective-permute-start(f32[4,256,256]{2,1,0:T(8,128)} %get-tuple-element.21), channel_id=1, source_target_pairs={{0,4},{4,0},{8,12},{12,8},{16,20},{20,16},{24,28},{28,24},{1,5},{5... | collective-permute-start | bytes 3145736 | tf_op jit(solution)/shard_map/ppermute | solution.py:350
  65.5 39.6 %collective-permute-start.13 = (f32[4,256,256]{2,1,0:T(8,128)}, f32[4,256,256]{2,1,0:T(8,128)S(1)}, u32[]{:S(2)}, u32[]{:S(2)}) collective-permute-start(f32[4,256,256]{2,1,0:T(8,128)} %get-tuple-element.22), channel_id=1, source_target_pairs={{8,0},{12,4},{16,8},{20,12},{24,16},{28,20},{9,1},{13,5},{17,9},{2... | collective-permute-start | bytes 3145736 | tf_op jit(solution)/shard_map/ppermute | solution.py:350
  67.6 37.5 %collective-permute-start.14 = (f32[4,256,256]{2,1,0:T(8,128)}, f32[4,256,256]{2,1,0:T(8,128)S(1)}, u32[]{:S(2)}, u32[]{:S(2)}) collective-permute-start(f32[4,256,256]{2,1,0:T(8,128)} %get-tuple-element.23), channel_id=1, source_target_pairs={{0,8},{4,12},{8,16},{12,20},{16,24},{20,28},{1,9},{5,13},{9,17},{1... | collective-permute-start | bytes 3145736 | tf_op jit(solution)/shard_map/ppermute | solution.py:350
  68.9 50.5 %collective-permute-start.15 = (f32[4,256,256]{2,1,0:T(8,128)}, f32[4,256,256]{2,1,0:T(8,128)S(1)}, u32[]{:S(2)}, u32[]{:S(2)}) collective-permute-start(f32[4,256,256]{2,1,0:T(8,128)} %get-tuple-element.24), channel_id=1, source_target_pairs={{4,8},{8,4},{12,16},{16,12},{20,24},{24,20},{5,9},{9,5},{13,17},{1... | collective-permute-start | bytes 3145736 | tf_op jit(solution)/shard_map/ppermute | solution.py:350
  77.4 2.4 %collective-permute-start.10 = (f32[1,256,256]{2,1,0:T(8,128)S(1)}, f32[1,256,256]{2,1,0:T(8,128)S(1)}, u32[]{:S(2)}, u32[]{:S(2)}) collective-permute-start(f32[1,256,256]{2,1,0:T(8,128)S(1)} %get-tuple-element.35), channel_id=1, source_target_pairs={{0,1},{1,2},{2,3},{4,5},{5,6},{6,7},{8,9},{9,10},{10,11},{12,13},{... | collective-permute-start | bytes 786440 | tf_op jit(solution)/shard_map/ppermute | solution.py:350
  79.8 16.4 %collective-permute-start.11 = (f32[1,256,256]{2,1,0:T(8,128)S(1)}, f32[1,256,256]{2,1,0:T(8,128)S(1)}, u32[]{:S(2)}, u32[]{:S(2)}) collective-permute-start(f32[1,256,256]{2,1,0:T(8,128)S(1)} %get-tuple-element.34), channel_id=1, source_target_pairs={{1,0},{2,1},{3,2},{5,4},{6,5},{7,6},{9,8},{10,9},{11,10},{13,12},{... | collective-permute-start | bytes 786440 | tf_op jit(solution)/shard_map/ppermute | solution.py:350
  81.1 2.2 %copy-start = (f32[1,4,4,256,256]{4,3,2,1,0:T(8,128)S(1)}, f32[1,4,4,256,256]{4,3,2,1,0:T(8,128)}, u32[]{:S(2)}) copy-start(f32[1,4,4,256,256]{4,3,2,1,0:T(8,128)} %param.7) | copy-start | bytes 12582916
  83.3 1.2 %copy-start.6 = (f32[4,256,256]{2,1,0:T(8,128)S(1)}, f32[4,256,256]{2,1,0:T(8,128)}, u32[]{:S(2)}) copy-start(f32[4,256,256]{2,1,0:T(8,128)} %copy-done.5) | copy-start | bytes 3145732
  84.5 1.2 %copy-start.7 = (f32[1,4,256,256]{3,2,1,0:T(8,128)S(1)}, f32[1,4,256,256]{3,2,1,0:T(8,128)}, u32[]{:S(2)}) copy-start(f32[1,4,256,256]{3,2,1,0:T(8,128)} %param.6) | copy-start | bytes 3145732
  85.8 0.6 copy-start.10
  86.3 9.9 %copy-start.1 = (f32[1,4,4,256,256]{4,3,2,1,0:T(8,128)S(1)}, f32[1,4,4,256,256]{4,3,2,1,0:T(8,128)}, u32[]{:S(2)}) copy-start(f32[1,4,4,256,256]{4,3,2,1,0:T(8,128)} %param.7) | copy-start | bytes 12582916
  86.3 9.9 %copy-start.4 = (f32[4,256,256]{2,1,0:T(8,128)S(1)}, f32[4,256,256]{2,1,0:T(8,128)}, u32[]{:S(2)}) copy-start(f32[4,256,256]{2,1,0:T(8,128)} %copy-done.3) | copy-start | bytes 3145732
where the time goes:
time: 122 us; the launch traced here: 121 us
  starting transfers between devices  42 us (34%)
  waiting for transfers between devices  40.2 us (33%)
  Pallas kernels  26.1 us (21%)
  local copies, waits for them, and re-layouts  9.45 us (8%)
  other arithmetic  2.74 us (2%)
    ppermute x16, starting transfers between devices, send(): return lax.ppermute(x, axis, pairs_)  42 us
    ppermute x16, waiting for transfers between devices, send(): return lax.ppermute(x, axis, pairs_)  40.2 us
    pallas_call x2, Pallas kernels, pairs(): pl.pallas_call(functools.partial(pair_kernel, places, first, depth), name...  18.7 us
    unnamed x26, local copies, waits for them, and re-layouts  6.18 us
    pallas_call x1, Pallas kernels, pack(): pl.pallas_call(pack_kernel, name='pack', grid_spec=pltpu.PrefetchScalarGr...  5.49 us
  transfers between devices with their start and end apart: 16, of which 5 were waited for; matrix products, arithmetic and copies ran while one was open for 4% of the time, Pallas kernels for 20%

commit v1 on v0

v1 whole, which is shorter than its diff:
```python
import functools

import jax
import jax.numpy as jnp
from jax import lax
from jax.experimental import pallas as pl
from jax.experimental.pallas import tpu as pltpu
from jax.sharding import PartitionSpec as P


CYCLES = 8
HOPS = (-2, -1, 1, 2)

dual_step = 0.5
primal_step = 0.25
dual_bound = 0.3
fidelity = 1.0
scale = 1.0 / (1.0 + primal_step * fidelity)
flow = primal_step * scale
patch = -1.0 / (27.0 * 4.0)


LANES = 128
STEP = 32
PARTS = 2
EDGE = 16
RIM = 8


def chosen(table, hop):
    slot = jnp.int32(0)
    filled = table[0] == hop
    for k in range(1, 4):
        hit = table[k] == hop
        slot = jnp.where(hit, k, slot)
        filled = filled | hit
    return slot, filled


def offset_of(table, hop):
    offset = jnp.int32(0)
    for k in range(4):
        offset = jnp.where(table[k] == hop, table[4 + k], offset)
    return offset


def home_slot(table, hop):
    slot, filled = chosen(table, hop)
    count = jnp.int32(0)
    for k in range(4):
        count = count + (table[k] != 0).astype(jnp.int32)
    for other in HOPS:
        _, other_filled = chosen(table, other)
        count = count + ((other < hop) & jnp.logical_not(other_filled)).astype(jnp.int32)
    return jnp.where(filled, slot, count), filled


def hop_of(place, stride):
    if place > 1:
        return jnp.int32(2 if place == 2 else -2)
    parity = (lax.axis_index("tm") // stride) % 2
    near = (1 - 2 * parity).astype(jnp.int32)
    return near if place == 0 else -near


def pack_kernel(places, stride, table, dual, *refs):
    count = len(places)
    outs, (held, sems) = refs[:count], refs[count:]
    depth, rows = dual.shape[1:3]
    moves = []
    for j, place in enumerate(places):
        slot, _ = chosen(table, hop_of(place, stride))
        for half in range(2):
            source = dual.at[slot, :, :, pl.ds(half * LANES, LANES)]
            moves.append(
                pltpu.make_async_copy(source, held.at[j, :, half, pl.ds(RIM, rows), :], sems.at[2 * j + half])
            )
    for m in moves:
        m.start()
    for j in range(count):
        for z in range(depth):
            for half in range(2):
                held[j, z, half, pl.ds(0, RIM), :] = jnp.zeros((RIM, LANES), jnp.float32)
                held[j, z, half, pl.ds(RIM + rows, RIM), :] = jnp.zeros((RIM, LANES), jnp.float32)
    for j, place in enumerate(places):
        offset = offset_of(table, hop_of(place, stride))
        moves[2 * j].wait()
        moves[2 * j + 1].wait()

        def body(step, carry):
            y = pl.multiple_of(step * STEP, STEP)
            for z in range(depth):
                for half in range(2):
                    outs[j][z, pl.ds(y, STEP), pl.ds(half * LANES, LANES)] = held[
                        j, z, half, pl.ds(RIM + y + offset, STEP), :
                    ]
            return carry

        lax.fori_loop(0, rows // STEP, body, 0)


def pack(places, stride, table, dual):
    _, depth, rows, columns = dual.shape
    count = len(places)
    return pl.pallas_call(
        functools.partial(pack_kernel, places, stride),
        in_specs=[pl.BlockSpec(memory_space=pltpu.SMEM), pl.BlockSpec(memory_space=pltpu.HBM)],
        out_specs=[pl.BlockSpec(memory_space=pltpu.VMEM)] * count,
        out_shape=[jax.ShapeDtypeStruct((depth, rows, columns), jnp.float32)] * count,
        scratch_shapes=[
            pltpu.VMEM((count, depth, 2, rows + 2 * RIM, LANES), jnp.float32),
            pltpu.SemaphoreType.DMA((2 * count,)),
        ],
        compiler_params=pltpu.CompilerParams(vmem_limit_bytes=8 << 20),
        cost_estimate=pl.CostEstimate(
            flops=0, bytes_accessed=2 * count * 4 * depth * rows * columns, transcendentals=0
        ),
    )(table, dual)


def box_rows(sums, z, half, start):
    return (
        sums[z, half, pl.ds(start - 1, STEP), :]
        + sums[z, half, pl.ds(start, STEP), :]
        + sums[z, half, pl.ds(start + 1, STEP), :]
    )


def box_lanes(left, right, lane):
    zero = jnp.zeros_like(left)
    left_up, right_up = pltpu.roll(left, 1, 1), pltpu.roll(right, 1, 1)
    left_down, right_down = pltpu.roll(left, LANES - 1, 1), pltpu.roll(right, LANES - 1, 1)
    first, last = lane == 0, lane == LANES - 1
    return (
        left + jnp.where(first, zero, left_up) + jnp.where(last, right_down, left_down),
        right + jnp.where(first, left_up, right_up) + jnp.where(last, zero, right_down),
    )


def pair_kernel(places, first, stride, table, *refs):
    count = len(places)
    refs = list(refs)
    take = lambda k: [refs.pop(0) for _ in range(k)]
    tables = take(count)
    image, above, below, dual, start = take(5)
    partners, tails, heads = take(count), take(count), take(count)
    if not first:
        take(1)
    fresh_out, total = take(2)
    weights, gains = take(count), take(count)
    held, own_sums, in_sums, fresh, sems, out_sems = refs
    depth, rows, _ = image.shape
    f32 = jnp.float32

    def copies(i):
        stacked = places[i][1]
        moves = []
        for half in range(2):
            lanes = pl.ds(half * LANES, LANES)
            moves.append((partners[i].at[:, :, lanes], held.at[i, pl.ds(1, depth), half, pl.ds(EDGE, rows), :]))
            moves.append((tails[i].at[stacked, :, lanes], held.at[i, 0, half, pl.ds(EDGE, rows), :]))
            moves.append((heads[i].at[stacked, :, lanes], held.at[i, depth + 1, half, pl.ds(EDGE, rows), :]))
        return [pltpu.make_async_copy(a, b, sems.at[6 * i + j]) for j, (a, b) in enumerate(moves)]

    in_copies = [copies(i) for i in range(count)]
    for group in in_copies:
        for c in group:
            c.start()
    for i in range(count):
        for z in range(depth + 2):
            for half in range(2):
                held[i, z, half, pl.ds(0, EDGE), :] = jnp.zeros((EDGE, LANES), f32)
                held[i, z, half, pl.ds(EDGE + rows, EDGE), :] = jnp.zeros((EDGE, LANES), f32)
    for z in range(depth):
        for half in range(2):
            own_sums[z, half, pl.ds(0, RIM), :] = jnp.zeros((RIM, LANES), f32)
            own_sums[z, half, pl.ds(RIM + rows, RIM), :] = jnp.zeros((RIM, LANES), f32)

    row = lax.broadcasted_iota(jnp.int32, (STEP, LANES), 0)
    lane = lax.broadcasted_iota(jnp.int32, (STEP, LANES), 1)

    def mine(z, half, y):
        here, lanes = pl.ds(pl.multiple_of(y, 8), STEP), pl.ds(half * LANES, LANES)
        if z == 0:
            return above[0, here, lanes]
        if z == depth + 1:
            return below[0, here, lanes]
        return image[z - 1, here, lanes]

    def store_sums(sums, half, y, size, squares):
        for z in range(depth):
            sums[z, half, pl.ds(pl.multiple_of(RIM + y, 8), size), :] = squares[z] + squares[z + 1] + squares[z + 2]

    out_copies = []
    for i in range(count):
        hop = hop_of(places[i][0], stride)
        source, _ = chosen(table, hop)
        own_offset = offset_of(table, hop)
        slot, filled = home_slot(table, hop)
        bound = jnp.where(filled, f32(dual_bound), f32(0.0))
        _, in_filled = chosen(tables[i], -hop)
        in_offset = offset_of(tables[i], -hop)
        low = jnp.where(in_filled, -in_offset, 4 * rows)
        high = rows - 1 - in_offset
        for c in in_copies[i]:
            c.wait()

        def theirs(z, half, y, shift, size=STEP):
            return held[i, z, half, pl.ds(EDGE + y + shift, size), :]

        for y in (-RIM, rows):
            for half in range(2):
                values = [theirs(z, half, y, in_offset, RIM) for z in range(depth + 2)]
                store_sums(in_sums, half, y, RIM, [v * v for v in values])

        def gather(step, carry):
            y = pl.multiple_of(step * STEP, STEP)
            inside = (row + y >= low) & (row + y <= high)
            for half in range(2):
                own_squares, in_squares = [], []
                for z in range(depth + 2):
                    value = mine(z, half, y)
                    own_square = theirs(z, half, y, -own_offset) - value
                    own_squares.append(own_square * own_square)
                    in_square = jnp.where(inside, value, 0.0) - theirs(z, half, y, in_offset)
                    in_squares.append(in_square * in_square)
                store_sums(own_sums, half, y, STEP, own_squares)
                store_sums(in_sums, half, y, STEP, in_squares)
            return carry

        def apply(step, carry):
            y = pl.multiple_of(step * STEP, STEP)
            inside = (row + y >= low) & (row + y <= high)
            here = pl.ds(y, STEP)
            for z in range(depth):
                own_box = box_lanes(box_rows(own_sums, z, 0, RIM + y), box_rows(own_sums, z, 1, RIM + y), lane)
                in_box = box_lanes(box_rows(in_sums, z, 0, RIM + y), box_rows(in_sums, z, 1, RIM + y), lane)
                for half in range(2):
                    lanes = pl.ds(half * LANES, LANES)
                    value = mine(z + 1, half, y)
                    weight = jnp.exp(own_box[half] * patch)
                    contrast = theirs(z + 1, half, y, -own_offset) - value
                    step_to = dual[source, z, here, lanes] + (dual_step * weight) * contrast
                    step_to = jnp.minimum(jnp.maximum(step_to, -bound), bound)
                    fresh[i, z, here, lanes] = step_to
                    flux = (weight * step_to) * flow
                    if i > 0:
                        total[z, here, lanes] = total[z, here, lanes] + flux
                    elif first:
                        total[z, here, lanes] = scale * value + (flow * fidelity) * start[z, here, lanes] + flux
                    else:
                        total[z, here, lanes] = start[z, here, lanes] + flux
                    weight = jnp.exp(in_box[half] * patch)
                    weights[i][z, here, lanes] = jnp.where(inside, weight, 0.0)
                    gains[i][z, here, lanes] = (dual_step * weight) * (value - theirs(z + 1, half, y, in_offset))
            return carry

        steps = rows // STEP
        lax.fori_loop(0, steps, gather, 0)
        for part in range(PARTS):
            lax.fori_loop(part * steps // PARTS, (part + 1) * steps // PARTS, apply, 0)
            some = pl.ds(part * rows // PARTS, rows // PARTS)
            done = pltpu.make_async_copy(
                fresh.at[i, :, some, :], fresh_out.at[slot, :, some, :], out_sems.at[PARTS * i + part]
            )
            done.start()
            out_copies.append(done)
    for c in out_copies:
        c.wait()


def pairs(places, stride, table, tables, image, above, below, dual, start, partners, tails, heads, fresh=None):
    count = len(places)
    depth, rows, columns = image.shape
    first = fresh is None
    f32 = jnp.float32
    block = jax.ShapeDtypeStruct(image.shape, f32)
    any_spec = pl.BlockSpec(memory_space=pl.ANY)
    vmem_spec = pl.BlockSpec(memory_space=pltpu.VMEM)
    smem = pl.BlockSpec(memory_space=pltpu.SMEM)
    operands = [table, *tables, image, above, below, dual, start, *partners, *tails, *heads]
    specs = [smem] * (1 + count) + [vmem_spec] * 5 + [any_spec] * (3 * count)
    aliases = {}
    if not first:
        aliases = {len(operands): 0}
        operands.append(fresh)
        specs.append(any_spec)
    cells = depth * rows * columns
    return pl.pallas_call(
        functools.partial(pair_kernel, places, first, stride),
        in_specs=specs,
        out_specs=[any_spec] + [vmem_spec] * (1 + 2 * count),
        out_shape=[jax.ShapeDtypeStruct(dual.shape, f32)] + [block] * (1 + 2 * count),
        input_output_aliases=aliases,
        scratch_shapes=[
            pltpu.VMEM((count, depth + 2, 2, rows + 2 * EDGE, LANES), f32),
            pltpu.VMEM((depth, 2, rows + 2 * RIM, LANES), f32),
            pltpu.VMEM((depth, 2, rows + 2 * RIM, LANES), f32),
            pltpu.VMEM((count, depth, rows, columns), f32),
            pltpu.SemaphoreType.DMA((6 * count,)),
            pltpu.SemaphoreType.DMA((PARTS * count,)),
        ],
        compiler_params=pltpu.CompilerParams(vmem_limit_bytes=24 << 20),
        cost_estimate=pl.CostEstimate(
            flops=count * 60 * cells, bytes_accessed=4 * (3 + 7 * count) * cells, transcendentals=2 * count * cells
        ),
    )(*operands)


def settle_kernel(count, total, *refs):
    duals, weights, gains, out = refs[:count], refs[count : 2 * count], refs[2 * count : 3 * count], refs[-1]
    depth, rows, _ = total.shape

    def body(step, carry):
        here = pl.ds(pl.multiple_of(step * STEP, STEP), STEP)
        for z in range(depth):
            arriving = None
            for i in range(count):
                value = duals[i][z, here, :] + gains[i][z, here, :]
                value = weights[i][z, here, :] * jnp.minimum(jnp.maximum(value, -dual_bound), dual_bound)
                arriving = value if arriving is None else arriving + value
            out[z, here, :] = total[z, here, :] - flow * arriving
        return carry

    lax.fori_loop(0, rows // STEP, body, 0)


def settle(total, duals, weights, gains):
    count = len(duals)
    vmem_spec = pl.BlockSpec(memory_space=pltpu.VMEM)
    return pl.pallas_call(
        functools.partial(settle_kernel, count),
        in_specs=[vmem_spec] * (1 + 3 * count),
        out_specs=vmem_spec,
        out_shape=jax.ShapeDtypeStruct(total.shape, jnp.float32),
        compiler_params=pltpu.CompilerParams(vmem_limit_bytes=20 << 20),
        cost_estimate=pl.CostEstimate(
            flops=5 * count * total.size, bytes_accessed=4 * (2 + 3 * count) * total.size, transcendentals=0
        ),
    )(total, *duals, *weights, *gains)


def shards(volume, prior_image, dual_pairs, pair_cycle, pair_offset):
    frames = lax.axis_size("tm")
    spaces = lax.axis_size("space")
    stride = frames // CYCLES
    image = volume[0]
    dual = dual_pairs[0]
    cycle_of = lambda t: t // stride
    every = range(frames)
    swap = [(t, t + stride if cycle_of(t) % 2 == 0 else t - stride) for t in every]
    cross = [(t, t - stride if cycle_of(t) % 2 == 0 else t + stride) for t in every]
    cross = [(a, b) for a, b in cross if 0 <= b < frames]
    later = [(t, t + 2 * stride) for t in every if t + 2 * stride < frames]
    sooner = [(t, t - 2 * stride) for t in every if t - 2 * stride >= 0]
    relay = [(t, t + 2 * stride if cycle_of(t) % 2 == 0 else t - 2 * stride) for t in every]
    relay = [(a, b) for a, b in relay if 0 <= b < frames]
    onward = [(s, s + 1) for s in range(spaces - 1)]
    backward = [(s + 1, s) for s in range(spaces - 1)]

    def send(x, pairs_, axis="tm"):
        return lax.ppermute(x, axis, pairs_)

    table = jnp.concatenate([pair_cycle[0], pair_offset[0]])

    near_image = send(image, swap)
    before_image = send(image, later)
    after_image = send(image, sooner)
    near_dual, far_dual = pack((0, 1), stride, table, dual)
    near_dual = send(near_dual, swap)
    far_dual = send(far_dual, cross)
    far_image = send(near_image, relay)
    near_table = send(table, swap)
    far_table = send(table, cross)
    before_table = send(table, later)
    after_table = send(table, sooner)

    stack = (image, near_image, after_image, before_image)
    bottoms = jnp.stack([x[-1] for x in stack])
    tops = jnp.stack([x[0] for x in stack])
    tails = send(bottoms, onward, "space")
    heads = send(tops, backward, "space")
    later_dual, sooner_dual = pack((2, 3), stride, table, dual)
    before_dual = send(later_dual, later)
    after_dual = send(sooner_dual, sooner)
    fresh, total, wn, wa, gn, ga = pairs(
        ((0, 1), (2, 2)), stride, table, (near_table, after_table), image, tails, heads, dual, prior_image[0],
        (near_image, after_image), (tails,) * 2, (heads,) * 2,
    )
    far_tail = send(far_image[-1:], onward, "space")
    far_head = send(far_image[:1], backward, "space")
    fresh, total, wb, wf, gb, gf = pairs(
        ((3, 3), (1, 0)), stride, table, (before_table, far_table), image, tails, heads, dual, total,
        (before_image, far_image), (tails, far_tail), (heads, far_head), fresh,
    )
    volume_next = settle(
        total, (near_dual, after_dual, before_dual, far_dual), (wn, wa, wb, wf), (gn, ga, gb, gf)
    )
    return (volume_next[None], fresh[None])


def solution(mesh):
    return jax.shard_map(
        shards,
        mesh=mesh,
        in_specs=(
            P("tm", "space", None, None),
            P("tm", "space", None, None),
            P("tm", None, "space", None, None),
            P("tm", None),
            P("tm", None),
        ),
        out_specs=(P("tm", "space", None, None), P("tm", None, "space", None, None)),
        check_vma=False,
    )
```

time: 122 us -> 120 us (0.984)
  waiting for transfers between devices: 40.2 us -> 52.9 us
  Pallas kernels: 26.1 us -> 16.5 us
  local copies, waits for them, and re-layouts: 9.45 us -> 1.23 us
  starting transfers between devices: 42 us -> 47.2 us
  other arithmetic: 2.74 us -> 0.24 us
    ppermute x16, waiting for transfers between devices: 40.2 us -> 52.9 us  [send(): return lax.ppermute(x, axis, pairs_)]
    pallas_call x3 -> x4, Pallas kernels: 24.2 us -> 14.8 us  [the longest x2 13 us: pairs(): pl.pallas_call(functools.partial(pair_kernel, places, first, stride), in_...]
    unnamed x26 -> x10, local copies, waits for them, and re-layouts: 6.18 us -> 0.03 us
    ppermute x16, starting transfers between devices: 42 us -> 47.2 us  [send(): return lax.ppermute(x, axis, pairs_)]
  transfers between devices with their start and end apart: 16 -> 16, of which waited for: 5 -> 7; matrix products, arithmetic and copies ran while one was open for 4% -> 1% of each run, Pallas kernels for 20% -> 12%
where the time goes in v1:
time: 120 us; the launch traced here: 119 us
  waiting for transfers between devices  52.9 us (44%)
  starting transfers between devices  47.2 us (39%)
  Pallas kernels  16.5 us (14%)
  local copies, waits for them, and re-layouts  1.23 us (1%)
    ppermute x16, waiting for transfers between devices, send(): return lax.ppermute(x, axis, pairs_)  52.9 us
    ppermute x16, starting transfers between devices, send(): return lax.ppermute(x, axis, pairs_)  47.2 us
    pallas_call x2, Pallas kernels, pairs(): pl.pallas_call(functools.partial(pair_kernel, places, first, stride), in_...  13 us
  transfers between devices with their start and end apart: 16, of which 7 were waited for; matrix products, arithmetic and copies ran while one was open for 1% of the time, Pallas kernels for 12%

profile of v1, /device:TPU:24, one launch (start us, length us, event | category | flops | bytes accessed | tf_op | source)
XLA Modules:
  0.0 119.1 jit_solution(10188925236689216864)
XLA Ops:
  0.7 1.6 %collective-permute-start.2 = (f32[4,256,256]{2,1,0:T(8,128)}, f32[4,256,256]{2,1,0:T(8,128)S(1)}, u32[]{:S(2)}, u32[]{:S(2)}) collective-permute-start(f32[4,256,256]{2,1,0:T(8,128)} %bitcast.15), channel_id=1, source_target_pairs={{0,4},{4,0},{8,12},{12,8},{16,20},{20,16},{24,28},{28,24},{1,5},{5... | collective-permute-start | bytes 3145736 | tf_op jit(solution)/shard_map/ppermute | solution.py:362
  2.2 2.4 %collective-permute-start.3 = (f32[4,256,256]{2,1,0:T(8,128)}, f32[4,256,256]{2,1,0:T(8,128)S(1)}, u32[]{:S(2)}, u32[]{:S(2)}) collective-permute-start(f32[4,256,256]{2,1,0:T(8,128)} %bitcast.16), channel_id=1, source_target_pairs={{8,0},{12,4},{16,8},{20,12},{24,16},{28,20},{9,1},{13,5},{17,9},{2... | collective-permute-start | bytes 3145736 | tf_op jit(solution)/shard_map/ppermute | solution.py:362
  4.7 1.3 %collective-permute-start.4 = (f32[4,256,256]{2,1,0:T(8,128)}, f32[4,256,256]{2,1,0:T(8,128)S(1)}, u32[]{:S(2)}, u32[]{:S(2)}) collective-permute-start(f32[4,256,256]{2,1,0:T(8,128)} %bitcast.17), channel_id=1, source_target_pairs={{0,8},{4,12},{8,16},{12,20},{16,24},{20,28},{1,9},{5,13},{9,17},{1... | collective-permute-start | bytes 3145736 | tf_op jit(solution)/shard_map/ppermute | solution.py:362
  6.0 1.1 slice_bitcast_fusion
  7.0 18.8 %collective-permute-done.2.refs_7_ = f32[4,256,256]{2,1,0:T(8,128)S(1)} collective-permute-done((f32[4,256,256]{2,1,0:T(8,128)}, f32[4,256,256]{2,1,0:T(8,128)S(1)}, u32[]{:S(2)}, u32[]{:S(2)}) %collective-permute-start.2) | collective-permute-done | bytes 1048608 | tf_op jit(solution)/shard_map/ppermute | solution.py:362
  25.9 1.2 collective-permute-done.3.refs_8_
  27.1 4.0 %collective-permute-done.4.refs_7_ = f32[4,256,256]{2,1,0:T(8,128)S(1)} collective-permute-done((f32[4,256,256]{2,1,0:T(8,128)}, f32[4,256,256]{2,1,0:T(8,128)S(1)}, u32[]{:S(2)}, u32[]{:S(2)}) %collective-permute-start.4) | collective-permute-done | bytes 1048608 | tf_op jit(solution)/shard_map/ppermute | solution.py:362
  31.1 0.1 pad_maximum_fusion
  31.2 1.4 %collective-permute-start.5 = (f32[4,256,256]{2,1,0:T(8,128)S(1)}, f32[4,256,256]{2,1,0:T(8,128)S(1)}, u32[]{:S(2)}, u32[]{:S(2)}) collective-permute-start(f32[4,256,256]{2,1,0:T(8,128)S(1)} %pad_maximum_fusion), channel_id=1, source_target_pairs={{0,1},{1,2},{2,3},{4,5},{5,6},{6,7},{8,9},{9,10},{10,11},{12,13},{... | collective-permute-start | bytes 3145736 | tf_op jit(solution)/shard_map/ppermute | solution.py:362
  32.6 1.3 %collective-permute-start.9 = (f32[4,256,256]{2,1,0:T(8,128)S(1)}, f32[4,256,256]{2,1,0:T(8,128)S(1)}, u32[]{:S(2)}, u32[]{:S(2)}) collective-permute-start(f32[4,256,256]{2,1,0:T(8,128)S(1)} %collective-permute-done.2.refs_7_), channel_id=1, source_target_pairs={{0,8},{8,16},{12,4},{16,24},{20,12},{28,20},{1,9},{9,17},{13,5},{1... | collective-permute-start | bytes 3145736 | tf_op jit(solution)/shard_map/ppermute | solution.py:362
  33.9 0.1 pad_maximum_fusion.1
  34.0 1.3 %collective-permute-start.6 = (f32[4,256,256]{2,1,0:T(8,128)S(1)}, f32[4,256,256]{2,1,0:T(8,128)S(1)}, u32[]{:S(2)}, u32[]{:S(2)}) collective-permute-start(f32[4,256,256]{2,1,0:T(8,128)S(1)} %pad_maximum_fusion.1), channel_id=1, source_target_pairs={{1,0},{2,1},{3,2},{5,4},{6,5},{7,6},{9,8},{10,9},{11,10},{13,12},{... | collective-permute-start | bytes 3145736 | tf_op jit(solution)/shard_map/ppermute | solution.py:362
  35.3 0.1 pad_add_fusion.table
  35.4 1.8 %collective-permute-start.7 = (s32[8]{0:T(128)S(1)}, s32[8]{0:T(128)S(1)}, u32[]{:S(2)}, u32[]{:S(2)}) collective-permute-start(s32[8]{0:T(128)S(1)} %pad_add_fusion.table), channel_id=1, source_target_pairs={{0,4},{4,0},{8,12},{12,8},{16,20},{20,16},{24,28},{28,24},{1,5},{5... | collective-permute-start | bytes 104 | tf_op jit(solution)/shard_map/ppermute | solution.py:362
  37.2 2.7 %collective-permute-start.8 = (s32[8]{0:T(128)S(1)}, s32[8]{0:T(128)S(1)}, u32[]{:S(2)}, u32[]{:S(2)}) collective-permute-start(s32[8]{0:T(128)S(1)} %pad_add_fusion.table), channel_id=1, source_target_pairs={{8,0},{12,4},{16,8},{20,12},{24,16},{28,20},{9,1},{13,5},{17,9},{2... | collective-permute-start | bytes 104 | tf_op jit(solution)/shard_map/ppermute | solution.py:362
  40.0 0.9 shard_map.70
  40.9 0.9 shard_map.71
  41.9 1.3 %collective-permute-start = (s32[8]{0:T(128)S(1)}, s32[8]{0:T(128)S(1)}, u32[]{:S(2)}, u32[]{:S(2)}) collective-permute-start(s32[8]{0:T(128)S(1)} %pad_add_fusion.table), channel_id=1, source_target_pairs={{0,8},{4,12},{8,16},{12,20},{16,24},{20,28},{1,9},{5,13},{9,17},{1... | collective-permute-start | bytes 104 | tf_op jit(solution)/shard_map/ppermute | solution.py:362
  43.2 18.8 %collective-permute-start.1 = (s32[8]{0:T(128)S(1)}, s32[8]{0:T(128)S(1)}, u32[]{:S(2)}, u32[]{:S(2)}) collective-permute-start(s32[8]{0:T(128)S(1)} %pad_add_fusion.table), channel_id=1, source_target_pairs={{4,8},{8,4},{12,16},{16,12},{20,24},{24,20},{5,9},{9,5},{13,17},{1... | collective-permute-start | bytes 104 | tf_op jit(solution)/shard_map/ppermute | solution.py:362
  61.9 0.1 collective-permute-start.12
  62.0 1.4 %collective-permute-done.1.refs_1_ = s32[8]{0:T(128)S(1)} collective-permute-done((s32[8]{0:T(128)S(1)}, s32[8]{0:T(128)S(1)}, u32[]{:S(2)}, u32[]{:S(2)}) %collective-permute-start.1) | collective-permute-done | bytes 64 | tf_op jit(solution)/shard_map/ppermute | solution.py:362
  63.5 2.1 %collective-permute-start.13 = (f32[4,256,256]{2,1,0:T(8,128)S(1)}, f32[4,256,256]{2,1,0:T(8,128)S(1)}, u32[]{:S(2)}, u32[]{:S(2)}) collective-permute-start(f32[4,256,256]{2,1,0:T(8,128)S(1)} %get-tuple-element.22), channel_id=1, source_target_pairs={{8,0},{12,4},{16,8},{20,12},{24,16},{28,20},{9,1},{13,5},{17,9},{2... | collective-permute-start | bytes 3145736 | tf_op jit(solution)/shard_map/ppermute | solution.py:362
  65.6 1.3 %collective-permute-start.14 = (f32[4,256,256]{2,1,0:T(8,128)S(1)}, f32[4,256,256]{2,1,0:T(8,128)S(1)}, u32[]{:S(2)}, u32[]{:S(2)}) collective-permute-start(f32[4,256,256]{2,1,0:T(8,128)S(1)} %get-tuple-element.23), channel_id=1, source_target_pairs={{0,8},{4,12},{8,16},{12,20},{16,24},{20,28},{1,9},{5,13},{9,17},{1... | collective-permute-start | bytes 3145736 | tf_op jit(solution)/shard_map/ppermute | solution.py:362
  66.9 7.3 %collective-permute-start.15 = (f32[4,256,256]{2,1,0:T(8,128)S(1)}, f32[4,256,256]{2,1,0:T(8,128)S(1)}, u32[]{:S(2)}, u32[]{:S(2)}) collective-permute-start(f32[4,256,256]{2,1,0:T(8,128)S(1)} %get-tuple-element.24), channel_id=1, source_target_pairs={{4,8},{8,4},{12,16},{16,12},{20,24},{24,20},{5,9},{9,5},{13,17},{1... | collective-permute-start | bytes 3145736 | tf_op jit(solution)/shard_map/ppermute | solution.py:362
  74.3 1.3 %collective-permute-start.10 = (f32[1,256,256]{2,1,0:T(8,128)S(1)}, f32[1,256,256]{2,1,0:T(8,128)S(1)}, u32[]{:S(2)}, u32[]{:S(2)}) collective-permute-start(f32[1,256,256]{2,1,0:T(8,128)S(1)} %get-tuple-element.35), channel_id=1, source_target_pairs={{0,1},{1,2},{2,3},{4,5},{5,6},{6,7},{8,9},{9,10},{10,11},{12,13},{... | collective-permute-start | bytes 786440 | tf_op jit(solution)/shard_map/ppermute | solution.py:362
  75.6 1.1 collective-permute-done.10.refs_10_
  76.7 1.3 %collective-permute-start.11 = (f32[1,256,256]{2,1,0:T(8,128)S(1)}, f32[1,256,256]{2,1,0:T(8,128)S(1)}, u32[]{:S(2)}, u32[]{:S(2)}) collective-permute-start(f32[1,256,256]{2,1,0:T(8,128)S(1)} %get-tuple-element.34), channel_id=1, source_target_pairs={{1,0},{2,1},{3,2},{5,4},{6,5},{7,6},{9,8},{10,9},{11,10},{13,12},{... | collective-permute-start | bytes 786440 | tf_op jit(solution)/shard_map/ppermute | solution.py:362
  78.0 6.5 %shard_map.68 = (f32[4,4,256,256]{3,2,1,0:T(8,128)}, f32[4,256,256]{2,1,0:T(8,128)S(1)}, f32[4,256,256]{2,1,0:T(8,128)S(1)}, f32[4,256,256]{2,1,0:T(8,128)S(1)},...) custom-call(s32[8]{0:T(128)S(1)} %pad_add_fusion.table, s32[8]{0:T(128)S(1)} %collective-permute-done.7.refs_0_, ...), custom_call_target="tpu_custom_call" | custom-call | flops 31457280 | bytes 17825792 | tf_op jit(solution)/shard_map/pallas_call | solution.py:289
  84.5 6.5 %shard_map.69 = (f32[4,4,256,256]{3,2,1,0:T(8,128)}, f32[4,256,256]{2,1,0:T(8,128)S(1)}, f32[4,256,256]{2,1,0:T(8,128)S(1)}, f32[4,256,256]{2,1,0:T(8,128)S(1)},...) custom-call(s32[8]{0:T(128)S(1)} %pad_add_fusion.table, ...), custom_call_target="tpu_custom_call", output_to_operand_aliasing={{0}: (14, {})} | custom-call | flops 31457280 | bytes 17825792 | tf_op jit(solution)/shard_map/pallas_call | solution.py:289
  91.1 1.5 %collective-permute-done.14.refs_2_ = f32[4,256,256]{2,1,0:T(8,128)S(1)} collective-permute-done((f32[4,256,256]{2,1,0:T(8,128)S(1)}, f32[4,256,256]{2,1,0:T(8,128)S(1)}, u32[]{:S(2)}, u32[]{:S(2)}) %collective-permute-start.14) | collective-permute-done | bytes 1048608 | tf_op jit(solution)/shard_map/ppermute | solution.py:362
  92.6 24.8 %collective-permute-done.15.refs_3_ = f32[4,256,256]{2,1,0:T(8,128)S(1)} collective-permute-done((f32[4,256,256]{2,1,0:T(8,128)S(1)}, f32[4,256,256]{2,1,0:T(8,128)S(1)}, u32[]{:S(2)}, u32[]{:S(2)}) %collective-permute-start.15) | collective-permute-done | bytes 1048608 | tf_op jit(solution)/shard_map/ppermute | solution.py:362
  117.4 1.7 %shard_map.72 = f32[4,256,256]{2,1,0:T(8,128)} custom-call(f32[4,256,256]{2,1,0:T(8,128)S(1)} %get-tuple-element.20.total, f32[4,256,256]{2,1,0:T(8,128)S(1)} %collective-permute-done.12.refs_0_, f32[4,256,256]{2,1,0:T(8,128)S(1)} %collective-permute-done.13.refs_1_, f32[4,256,256]{2,1,0:T(8,128)S(1)} %collective-permute-done.14.refs_2_, ...), custom_call_target="tpu_custom_call" | custom-call | flops 5242880 | bytes 14680064 | tf_op jit(solution)/shard_map/pallas_call | solution.py:331
  (23 shorter events, 0.2 us)
Async XLA Ops:
  0.6 34.7 %copy-start.3 = (s32[1,4]{1,0:T(1,128)S(1)}, s32[1,4]{1,0:T(1,128)}, u32[]{:S(2)}) copy-start(s32[1,4]{1,0:T(1,128)} %param.9) | copy-start | bytes 52
  0.6 34.7 %copy-start.4 = (s32[1,4]{1,0:T(1,128)S(1)}, s32[1,4]{1,0:T(1,128)}, u32[]{:S(2)}) copy-start(s32[1,4]{1,0:T(1,128)} %param.8) | copy-start | bytes 52
  0.7 39.3 %copy-start = (f32[1,4,4,256,256]{4,3,2,1,0:T(8,128)S(1)}, f32[1,4,4,256,256]{4,3,2,1,0:T(8,128)}, u32[]{:S(2)}) copy-start(f32[1,4,4,256,256]{4,3,2,1,0:T(8,128)} %param.7) | copy-start | bytes 12582916
  0.7 25.2 %collective-permute-start.2 = (f32[4,256,256]{2,1,0:T(8,128)}, f32[4,256,256]{2,1,0:T(8,128)S(1)}, u32[]{:S(2)}, u32[]{:S(2)}) collective-permute-start(f32[4,256,256]{2,1,0:T(8,128)} %bitcast.15), channel_id=1, source_target_pairs={{0,4},{4,0},{8,12},{12,8},{16,20},{20,16},{24,28},{28,24},{1,5},{5... | collective-permute-start | bytes 3145736 | tf_op jit(solution)/shard_map/ppermute | solution.py:362
  2.2 24.8 %collective-permute-start.3 = (f32[4,256,256]{2,1,0:T(8,128)}, f32[4,256,256]{2,1,0:T(8,128)S(1)}, u32[]{:S(2)}, u32[]{:S(2)}) collective-permute-start(f32[4,256,256]{2,1,0:T(8,128)} %bitcast.16), channel_id=1, source_target_pairs={{8,0},{12,4},{16,8},{20,12},{24,16},{28,20},{9,1},{13,5},{17,9},{2... | collective-permute-start | bytes 3145736 | tf_op jit(solution)/shard_map/ppermute | solution.py:362
  4.7 26.4 %collective-permute-start.4 = (f32[4,256,256]{2,1,0:T(8,128)}, f32[4,256,256]{2,1,0:T(8,128)S(1)}, u32[]{:S(2)}, u32[]{:S(2)}) collective-permute-start(f32[4,256,256]{2,1,0:T(8,128)} %bitcast.17), channel_id=1, source_target_pairs={{0,8},{4,12},{8,16},{12,20},{16,24},{20,28},{1,9},{5,13},{9,17},{1... | collective-permute-start | bytes 3145736 | tf_op jit(solution)/shard_map/ppermute | solution.py:362
  31.2 34.3 %collective-permute-start.5 = (f32[4,256,256]{2,1,0:T(8,128)S(1)}, f32[4,256,256]{2,1,0:T(8,128)S(1)}, u32[]{:S(2)}, u32[]{:S(2)}) collective-permute-start(f32[4,256,256]{2,1,0:T(8,128)S(1)} %pad_maximum_fusion), channel_id=1, source_target_pairs={{0,1},{1,2},{2,3},{4,5},{5,6},{6,7},{8,9},{9,10},{10,11},{12,13},{... | collective-permute-start | bytes 3145736 | tf_op jit(solution)/shard_map/ppermute | solution.py:362
  32.6 34.3 %collective-permute-start.9 = (f32[4,256,256]{2,1,0:T(8,128)S(1)}, f32[4,256,256]{2,1,0:T(8,128)S(1)}, u32[]{:S(2)}, u32[]{:S(2)}) collective-permute-start(f32[4,256,256]{2,1,0:T(8,128)S(1)} %collective-permute-done.2.refs_7_), channel_id=1, source_target_pairs={{0,8},{8,16},{12,4},{16,24},{20,12},{28,20},{1,9},{9,17},{13,5},{1... | collective-permute-start | bytes 3145736 | tf_op jit(solution)/shard_map/ppermute | solution.py:362
  34.0 40.3 %collective-permute-start.6 = (f32[4,256,256]{2,1,0:T(8,128)S(1)}, f32[4,256,256]{2,1,0:T(8,128)S(1)}, u32[]{:S(2)}, u32[]{:S(2)}) collective-permute-start(f32[4,256,256]{2,1,0:T(8,128)S(1)} %pad_maximum_fusion.1), channel_id=1, source_target_pairs={{1,0},{2,1},{3,2},{5,4},{6,5},{7,6},{9,8},{10,9},{11,10},{13,12},{... | collective-permute-start | bytes 3145736 | tf_op jit(solution)/shard_map/ppermute | solution.py:362
  35.4 6.5 %collective-permute-start.7 = (s32[8]{0:T(128)S(1)}, s32[8]{0:T(128)S(1)}, u32[]{:S(2)}, u32[]{:S(2)}) collective-permute-start(s32[8]{0:T(128)S(1)} %pad_add_fusion.table), channel_id=1, source_target_pairs={{0,4},{4,0},{8,12},{12,8},{16,20},{20,16},{24,28},{28,24},{1,5},{5... | collective-permute-start | bytes 104 | tf_op jit(solution)/shard_map/ppermute | solution.py:362
  37.2 5.9 %collective-permute-start.8 = (s32[8]{0:T(128)S(1)}, s32[8]{0:T(128)S(1)}, u32[]{:S(2)}, u32[]{:S(2)}) collective-permute-start(s32[8]{0:T(128)S(1)} %pad_add_fusion.table), channel_id=1, source_target_pairs={{8,0},{12,4},{16,8},{20,12},{24,16},{28,20},{9,1},{13,5},{17,9},{2... | collective-permute-start | bytes 104 | tf_op jit(solution)/shard_map/ppermute | solution.py:362
  40.0 38.0 %copy-start.1 = (f32[1,4,256,256]{3,2,1,0:T(8,128)S(1)}, f32[1,4,256,256]{3,2,1,0:T(8,128)}, u32[]{:S(2)}) copy-start(f32[1,4,256,256]{3,2,1,0:T(8,128)} %param.5) | copy-start | bytes 3145732
  40.0 38.0 %copy-start.2 = (f32[1,4,256,256]{3,2,1,0:T(8,128)S(1)}, f32[1,4,256,256]{3,2,1,0:T(8,128)}, u32[]{:S(2)}) copy-start(f32[1,4,256,256]{3,2,1,0:T(8,128)} %param.6) | copy-start | bytes 3145732
  41.9 20.1 %collective-permute-start = (s32[8]{0:T(128)S(1)}, s32[8]{0:T(128)S(1)}, u32[]{:S(2)}, u32[]{:S(2)}) collective-permute-start(s32[8]{0:T(128)S(1)} %pad_add_fusion.table), channel_id=1, source_target_pairs={{0,8},{4,12},{8,16},{12,20},{16,24},{20,28},{1,9},{5,13},{9,17},{1... | collective-permute-start | bytes 104 | tf_op jit(solution)/shard_map/ppermute | solution.py:362
  43.2 20.3 %collective-permute-start.1 = (s32[8]{0:T(128)S(1)}, s32[8]{0:T(128)S(1)}, u32[]{:S(2)}, u32[]{:S(2)}) collective-permute-start(s32[8]{0:T(128)S(1)} %pad_add_fusion.table), channel_id=1, source_target_pairs={{4,8},{8,4},{12,16},{16,12},{20,24},{24,20},{5,9},{9,5},{13,17},{1... | collective-permute-start | bytes 104 | tf_op jit(solution)/shard_map/ppermute | solution.py:362
  61.9 29.1 %collective-permute-start.12 = (f32[4,256,256]{2,1,0:T(8,128)S(1)}, f32[4,256,256]{2,1,0:T(8,128)S(1)}, u32[]{:S(2)}, u32[]{:S(2)}) collective-permute-start(f32[4,256,256]{2,1,0:T(8,128)S(1)} %get-tuple-element.21), channel_id=1, source_target_pairs={{0,4},{4,0},{8,12},{12,8},{16,20},{20,16},{24,28},{28,24},{1,5},{5... | collective-permute-start | bytes 3145736 | tf_op jit(solution)/shard_map/ppermute | solution.py:362
  63.5 27.6 %collective-permute-start.13 = (f32[4,256,256]{2,1,0:T(8,128)S(1)}, f32[4,256,256]{2,1,0:T(8,128)S(1)}, u32[]{:S(2)}, u32[]{:S(2)}) collective-permute-start(f32[4,256,256]{2,1,0:T(8,128)S(1)} %get-tuple-element.22), channel_id=1, source_target_pairs={{8,0},{12,4},{16,8},{20,12},{24,16},{28,20},{9,1},{13,5},{17,9},{2... | collective-permute-start | bytes 3145736 | tf_op jit(solution)/shard_map/ppermute | solution.py:362
  65.6 27.0 %collective-permute-start.14 = (f32[4,256,256]{2,1,0:T(8,128)S(1)}, f32[4,256,256]{2,1,0:T(8,128)S(1)}, u32[]{:S(2)}, u32[]{:S(2)}) collective-permute-start(f32[4,256,256]{2,1,0:T(8,128)S(1)} %get-tuple-element.23), channel_id=1, source_target_pairs={{0,8},{4,12},{8,16},{12,20},{16,24},{20,28},{1,9},{5,13},{9,17},{1... | collective-permute-start | bytes 3145736 | tf_op jit(solution)/shard_map/ppermute | solution.py:362
  66.9 50.5 %collective-permute-start.15 = (f32[4,256,256]{2,1,0:T(8,128)S(1)}, f32[4,256,256]{2,1,0:T(8,128)S(1)}, u32[]{:S(2)}, u32[]{:S(2)}) collective-permute-start(f32[4,256,256]{2,1,0:T(8,128)S(1)} %get-tuple-element.24), channel_id=1, source_target_pairs={{4,8},{8,4},{12,16},{16,12},{20,24},{24,20},{5,9},{9,5},{13,17},{1... | collective-permute-start | bytes 3145736 | tf_op jit(solution)/shard_map/ppermute | solution.py:362
  74.3 2.4 %collective-permute-start.10 = (f32[1,256,256]{2,1,0:T(8,128)S(1)}, f32[1,256,256]{2,1,0:T(8,128)S(1)}, u32[]{:S(2)}, u32[]{:S(2)}) collective-permute-start(f32[1,256,256]{2,1,0:T(8,128)S(1)} %get-tuple-element.35), channel_id=1, source_target_pairs={{0,1},{1,2},{2,3},{4,5},{5,6},{6,7},{8,9},{9,10},{10,11},{12,13},{... | collective-permute-start | bytes 786440 | tf_op jit(solution)/shard_map/ppermute | solution.py:362
  76.7 7.8 %collective-permute-start.11 = (f32[1,256,256]{2,1,0:T(8,128)S(1)}, f32[1,256,256]{2,1,0:T(8,128)S(1)}, u32[]{:S(2)}, u32[]{:S(2)}) collective-permute-start(f32[1,256,256]{2,1,0:T(8,128)S(1)} %get-tuple-element.34), channel_id=1, source_target_pairs={{1,0},{2,1},{3,2},{5,4},{6,5},{7,6},{9,8},{10,9},{11,10},{13,12},{... | collective-permute-start | bytes 786440 | tf_op jit(solution)/shard_map/ppermute | solution.py:362

commit v2 on v1

--- a/solution.py
+++ b/solution.py
@@ -56,11 +56,10 @@
 
 
 def hop_of(place, stride):
-    if place > 1:
-        return jnp.int32(2 if place == 2 else -2)
-    parity = (lax.axis_index("tm") // stride) % 2
-    near = (1 - 2 * parity).astype(jnp.int32)
-    return near if place == 0 else -near
+    width = 1 if place < 2 else 2
+    parity = (lax.axis_index("tm") // (stride * width)) % 2
+    near = (width * (1 - 2 * parity)).astype(jnp.int32)
+    return near if place % 2 == 0 else -near
 
 
 def pack_kernel(places, stride, table, dual, *refs):
@@ -115,7 +114,7 @@
         cost_estimate=pl.CostEstimate(
             flops=0, bytes_accessed=2 * count * 4 * depth * rows * columns, transcendentals=0
         ),
-    )(table, dual)
+    )(table, pltpu.with_memory_space_constraint(dual, pltpu.HBM))
 
 
 def box_rows(sums, z, half, start):
@@ -142,30 +141,44 @@
     refs = list(refs)
     take = lambda k: [refs.pop(0) for _ in range(k)]
     tables = take(count)
-    image, above, below, dual, start = take(5)
-    partners, tails, heads = take(count), take(count), take(count)
+    image, dual, start = take(3)
+    partners, inner, outer, own_halos = take(count), take(count), take(count), take(2)
     if not first:
         take(1)
     fresh_out, total = take(2)
     weights, gains = take(count), take(count)
-    held, own_sums, in_sums, fresh, sems, out_sems = refs
+    held, rim, own_sums, in_sums, fresh, sems, out_sems = refs
     depth, rows, _ = image.shape
     f32 = jnp.float32
 
-    def copies(i):
+    even = lax.axis_index("space") % 2 == 0
+
+    def copies(i, upper, lower):
         stacked = places[i][1]
         moves = []
         for half in range(2):
             lanes = pl.ds(half * LANES, LANES)
             moves.append((partners[i].at[:, :, lanes], held.at[i, pl.ds(1, depth), half, pl.ds(EDGE, rows), :]))
-            moves.append((tails[i].at[stacked, :, lanes], held.at[i, 0, half, pl.ds(EDGE, rows), :]))
-            moves.append((heads[i].at[stacked, :, lanes], held.at[i, depth + 1, half, pl.ds(EDGE, rows), :]))
+            moves.append((upper.at[stacked, :, lanes], held.at[i, 0, half, pl.ds(EDGE, rows), :]))
+            moves.append((lower.at[stacked, :, lanes], held.at[i, depth + 1, half, pl.ds(EDGE, rows), :]))
         return [pltpu.make_async_copy(a, b, sems.at[6 * i + j]) for j, (a, b) in enumerate(moves)]
 
-    in_copies = [copies(i) for i in range(count)]
-    for group in in_copies:
-        for c in group:
+    def start_all(uppers, lowers, own_upper, own_lower):
+        for c in rim_copies(own_upper, own_lower):
             c.start()
+        for i in range(count):
+            for c in copies(i, uppers[i], lowers[i]):
+                c.start()
+
+    def rim_copies(upper, lower):
+        return [
+            pltpu.make_async_copy(upper.at[0], rim.at[0], sems.at[6 * count]),
+            pltpu.make_async_copy(lower.at[0], rim.at[1], sems.at[6 * count + 1]),
+        ]
+
+    pl.when(even)(lambda: start_all(outer, inner, own_halos[1], own_halos[0]))
+    pl.when(jnp.logical_not(even))(lambda: start_all(inner, outer, own_halos[0], own_halos[1]))
+    in_copies = [copies(i, inner[i], outer[i]) for i in range(count)]
     for i in range(count):
         for z in range(depth + 2):
             for half in range(2):
@@ -182,15 +195,17 @@
     def mine(z, half, y):
         here, lanes = pl.ds(pl.multiple_of(y, 8), STEP), pl.ds(half * LANES, LANES)
         if z == 0:
-            return above[0, here, lanes]
+            return rim[0, here, lanes]
         if z == depth + 1:
-            return below[0, here, lanes]
+            return rim[1, here, lanes]
         return image[z - 1, here, lanes]
 
     def store_sums(sums, half, y, size, squares):
         for z in range(depth):
             sums[z, half, pl.ds(pl.multiple_of(RIM + y, 8), size), :] = squares[z] + squares[z + 1] + squares[z + 2]
 
+    for c in rim_copies(*own_halos):
+        c.wait()
     out_copies = []
     for i in range(count):
         hop = hop_of(places[i][0], stride)
@@ -269,7 +284,7 @@
         c.wait()
 
 
-def pairs(places, stride, table, tables, image, above, below, dual, start, partners, tails, heads, fresh=None):
+def pairs(places, stride, table, tables, image, dual, start, partners, inner, outer, own_halos, fresh=None):
     count = len(places)
     depth, rows, columns = image.shape
     first = fresh is None
@@ -278,8 +293,8 @@
     any_spec = pl.BlockSpec(memory_space=pl.ANY)
     vmem_spec = pl.BlockSpec(memory_space=pltpu.VMEM)
     smem = pl.BlockSpec(memory_space=pltpu.SMEM)
-    operands = [table, *tables, image, above, below, dual, start, *partners, *tails, *heads]
-    specs = [smem] * (1 + count) + [vmem_spec] * 5 + [any_spec] * (3 * count)
+    operands = [table, *tables, image, dual, start, *partners, *inner, *outer, *own_halos]
+    specs = [smem] * (1 + count) + [vmem_spec] * 3 + [any_spec] * (3 * count + 2)
     aliases = {}
     if not first:
         aliases = {len(operands): 0}
@@ -294,17 +309,51 @@
         input_output_aliases=aliases,
         scratch_shapes=[
             pltpu.VMEM((count, depth + 2, 2, rows + 2 * EDGE, LANES), f32),
+            pltpu.VMEM((2, rows, columns), f32),
             pltpu.VMEM((depth, 2, rows + 2 * RIM, LANES), f32),
             pltpu.VMEM((depth, 2, rows + 2 * RIM, LANES), f32),
             pltpu.VMEM((count, depth, rows, columns), f32),
-            pltpu.SemaphoreType.DMA((6 * count,)),
+            pltpu.SemaphoreType.DMA((6 * count + 2,)),
             pltpu.SemaphoreType.DMA((PARTS * count,)),
         ],
-        compiler_params=pltpu.CompilerParams(vmem_limit_bytes=24 << 20),
+        compiler_params=pltpu.CompilerParams(vmem_limit_bytes=16 << 20),
         cost_estimate=pl.CostEstimate(
             flops=count * 60 * cells, bytes_accessed=4 * (3 + 7 * count) * cells, transcendentals=2 * count * cells
         ),
     )(*operands)
+
+
+def cut_kernel(*refs):
+    count = len(refs) - 3
+    images, (within, across, sems) = refs[:count], refs[count:]
+    last = images[0].shape[0] - 1
+    even = lax.axis_index("space") % 2 == 0
+
+    def copies(inner, outer):
+        moves = []
+        for k, image in enumerate(images):
+            moves.append(pltpu.make_async_copy(image.at[inner], within.at[k], sems.at[2 * k]))
+            moves.append(pltpu.make_async_copy(image.at[outer], across.at[k], sems.at[2 * k + 1]))
+        return moves
+
+    pl.when(even)(lambda: [c.start() for c in copies(last, 0)] and None)
+    pl.when(jnp.logical_not(even))(lambda: [c.start() for c in copies(0, last)] and None)
+    for c in copies(last, 0):
+        c.wait()
+
+
+def cut(images):
+    count = len(images)
+    block = (count,) + images[0].shape[1:]
+    return pl.pallas_call(
+        cut_kernel,
+        in_specs=[pl.BlockSpec(memory_space=pl.ANY)] * count,
+        out_specs=[pl.BlockSpec(memory_space=pltpu.VMEM)] * 2,
+        out_shape=[jax.ShapeDtypeStruct(block, jnp.float32)] * 2,
+        scratch_shapes=[pltpu.SemaphoreType.DMA((2 * count,))],
+        compiler_params=pltpu.CompilerParams(vmem_limit_bytes=6 << 20),
+        cost_estimate=pl.CostEstimate(flops=0, bytes_accessed=16 * count * block[1] * block[2], transcendentals=0),
+    )(*images)
 
 
 def settle_kernel(count, total, *refs):
@@ -333,7 +382,7 @@
         in_specs=[vmem_spec] * (1 + 3 * count),
         out_specs=vmem_spec,
         out_shape=jax.ShapeDtypeStruct(total.shape, jnp.float32),
-        compiler_params=pltpu.CompilerParams(vmem_limit_bytes=20 << 20),
+        compiler_params=pltpu.CompilerParams(vmem_limit_bytes=10 << 20),
         cost_estimate=pl.CostEstimate(
             flops=5 * count * total.size, bytes_accessed=4 * (2 + 3 * count) * total.size, transcendentals=0
         ),
@@ -351,50 +400,51 @@
     swap = [(t, t + stride if cycle_of(t) % 2 == 0 else t - stride) for t in every]
     cross = [(t, t - stride if cycle_of(t) % 2 == 0 else t + stride) for t in every]
     cross = [(a, b) for a, b in cross if 0 <= b < frames]
-    later = [(t, t + 2 * stride) for t in every if t + 2 * stride < frames]
-    sooner = [(t, t - 2 * stride) for t in every if t - 2 * stride >= 0]
+    wide_swap = [(t, t + 2 * stride if cycle_of(t) // 2 % 2 == 0 else t - 2 * stride) for t in every]
+    wide_cross = [(t, t - 2 * stride if cycle_of(t) // 2 % 2 == 0 else t + 2 * stride) for t in every]
+    wide_cross = [(a, b) for a, b in wide_cross if 0 <= b < frames]
     relay = [(t, t + 2 * stride if cycle_of(t) % 2 == 0 else t - 2 * stride) for t in every]
     relay = [(a, b) for a, b in relay if 0 <= b < frames]
-    onward = [(s, s + 1) for s in range(spaces - 1)]
-    backward = [(s + 1, s) for s in range(spaces - 1)]
+    inner = [(s, s ^ 1) for s in range(spaces)]
+    outer = [(s, s - 1 if s % 2 == 0 else s + 1) for s in range(spaces)]
+    outer = [(a, b) for a, b in outer if 0 <= b < spaces]
 
     def send(x, pairs_, axis="tm"):
         return lax.ppermute(x, axis, pairs_)
 
     table = jnp.concatenate([pair_cycle[0], pair_offset[0]])
 
+    def halos(images):
+        within, across = cut(images)
+        return send(within, inner, "space"), send(across, outer, "space")
+
     near_image = send(image, swap)
-    before_image = send(image, later)
-    after_image = send(image, sooner)
+    wide_near_image = send(image, wide_swap)
+    wide_far_image = send(image, wide_cross)
+    near_table = send(table, swap)
+    far_table = send(table, cross)
+    wide_near_table = send(table, wide_swap)
+    wide_far_table = send(table, wide_cross)
     near_dual, far_dual = pack((0, 1), stride, table, dual)
     near_dual = send(near_dual, swap)
     far_dual = send(far_dual, cross)
     far_image = send(near_image, relay)
-    near_table = send(table, swap)
-    far_table = send(table, cross)
-    before_table = send(table, later)
-    after_table = send(table, sooner)
-
-    stack = (image, near_image, after_image, before_image)
-    bottoms = jnp.stack([x[-1] for x in stack])
-    tops = jnp.stack([x[0] for x in stack])
-    tails = send(bottoms, onward, "space")
-    heads = send(tops, backward, "space")
-    later_dual, sooner_dual = pack((2, 3), stride, table, dual)
-    before_dual = send(later_dual, later)
-    after_dual = send(sooner_dual, sooner)
-    fresh, total, wn, wa, gn, ga = pairs(
-        ((0, 1), (2, 2)), stride, table, (near_table, after_table), image, tails, heads, dual, prior_image[0],
-        (near_image, after_image), (tails,) * 2, (heads,) * 2,
-    )
-    far_tail = send(far_image[-1:], onward, "space")
-    far_head = send(far_image[:1], backward, "space")
-    fresh, total, wb, wf, gb, gf = pairs(
-        ((3, 3), (1, 0)), stride, table, (before_table, far_table), image, tails, heads, dual, total,
-        (before_image, far_image), (tails, far_tail), (heads, far_head), fresh,
+
+    within, across = halos((image, near_image, wide_near_image, wide_far_image))
+    wide_near_dual, wide_far_dual = pack((2, 3), stride, table, dual)
+    wide_near_dual = send(wide_near_dual, wide_swap)
+    wide_far_dual = send(wide_far_dual, wide_cross)
+    fresh, total, w0, w2, g0, g2 = pairs(
+        ((0, 1), (2, 2)), stride, table, (near_table, wide_near_table), image, dual, prior_image[0],
+        (near_image, wide_near_image), (within,) * 2, (across,) * 2, (within, across),
+    )
+    far_within, far_across = halos((far_image,))
+    fresh, total, w3, w1, g3, g1 = pairs(
+        ((3, 3), (1, 0)), stride, table, (wide_far_table, far_table), image, dual, total,
+        (wide_far_image, far_image), (within, far_within), (across, far_across), (within, across), fresh,
     )
     volume_next = settle(
-        total, (near_dual, after_dual, before_dual, far_dual), (wn, wa, wb, wf), (gn, ga, gb, gf)
+        total, (near_dual, wide_near_dual, wide_far_dual, far_dual), (w0, w2, w3, w1), (g0, g2, g3, g1)
     )
     return (volume_next[None], fresh[None])
 

time: 120 us -> 116 us (0.967)
  the two profiles are of different devices: /device:TPU:24 before, /device:TPU:12 now
where the time goes in v2:
time: 116 us
  waiting for transfers between devices  63.4 us (55%)
  starting transfers between devices  29.9 us (26%)
  Pallas kernels  20.1 us (17%)
  local copies, waits for them, and re-layouts  1.24 us (1%)
    ppermute x16, waiting for transfers between devices, send(): return lax.ppermute(x, axis, pairs_)  63.4 us
    ppermute x16, starting transfers between devices, send(): return lax.ppermute(x, axis, pairs_)  29.9 us
    pallas_call x2, Pallas kernels, pairs(): pl.pallas_call(functools.partial(pair_kernel, places, first, stride), in_...  13.1 us
    pallas_call x2, Pallas kernels, pack(): pl.pallas_call(functools.partial(pack_kernel, places, stride), in_specs=[...  4.75 us
  transfers between devices with their start and end apart: 16, of which 9 were waited for; matrix products, arithmetic and copies ran while one was open for 0% of the time, Pallas kernels for 16%

profile of v2, /device:TPU:12, one launch (start us, length us, event | category | flops | bytes accessed | tf_op | source)
XLA Modules:
  0.0 115.5 jit_solution(6371343051133492675)
XLA Ops:
  0.6 0.6 collective-permute-start.4
  1.2 5.0 %collective-permute-start.6 = (f32[4,256,256]{2,1,0:T(8,128)}, f32[4,256,256]{2,1,0:T(8,128)S(1)}, u32[]{:S(2)}, u32[]{:S(2)}) collective-permute-start(f32[4,256,256]{2,1,0:T(8,128)} %bitcast.13), channel_id=1, source_target_pairs={{8,16},{12,20},{16,8},{20,12},{9,17},{13,21},{17,9},{21,13},{10,18... | collective-permute-start | bytes 3145736 | tf_op jit(solution)/shard_map/ppermute | solution.py:413
  6.3 19.5 %collective-permute-done.4.refs_1_.refs_5_ = f32[4,256,256]{2,1,0:T(8,128)S(1)} collective-permute-done((f32[4,256,256]{2,1,0:T(8,128)}, f32[4,256,256]{2,1,0:T(8,128)S(1)}, u32[]{:S(2)}, u32[]{:S(2)}) %collective-permute-start.4) | collective-permute-done | bytes 1048608 | tf_op jit(solution)/shard_map/ppermute | solution.py:413
  25.8 0.2 collective-permute-done.5.refs_2_.refs_6_
  26.1 3.0 %collective-permute-done.6.refs_3_.refs_5_ = f32[4,256,256]{2,1,0:T(8,128)S(1)} collective-permute-done((f32[4,256,256]{2,1,0:T(8,128)}, f32[4,256,256]{2,1,0:T(8,128)S(1)}, u32[]{:S(2)}, u32[]{:S(2)}) %collective-permute-start.6) | collective-permute-done | bytes 1048608 | tf_op jit(solution)/shard_map/ppermute | solution.py:413
  29.1 1.2 %copy-done.1 = f32[1,4,256,256]{3,2,1,0:T(8,128)S(1)} copy-done((f32[1,4,256,256]{3,2,1,0:T(8,128)S(1)}, f32[1,4,256,256]{3,2,1,0:T(8,128)}, u32[]{:S(2)}) %copy-start.1) | copy-done | bytes 1048600
  30.3 0.2 shard_map.68
  30.6 1.9 %collective-permute-start.9 = (f32[4,256,256]{2,1,0:T(8,128)S(1)}, f32[4,256,256]{2,1,0:T(8,128)S(1)}, u32[]{:S(2)}, u32[]{:S(2)}) collective-permute-start(f32[4,256,256]{2,1,0:T(8,128)S(1)} %collective-permute-done.4.refs_1_.refs_5_), channel_id=1, source_target_pairs={{0,8},{8,16},{12,4},{16,24},{20,12},{28,20},{1,9},{9,17},{13,5},{1... | collective-permute-start | bytes 3145736 | tf_op jit(solution)/shard_map/ppermute | solution.py:413
  32.5 0.7 collective-permute-start.8
  33.3 0.1 pad_add_fusion.table
  33.4 3.2 %collective-permute-start.2 = (s32[8]{0:T(128)S(1)}, s32[8]{0:T(128)S(1)}, u32[]{:S(2)}, u32[]{:S(2)}) collective-permute-start(s32[8]{0:T(128)S(1)} %pad_add_fusion.table), channel_id=1, source_target_pairs={{0,4},{4,0},{8,12},{12,8},{16,20},{20,16},{24,28},{28,24},{1,5},{5... | collective-permute-start | bytes 104 | tf_op jit(solution)/shard_map/ppermute | solution.py:413
  36.6 0.4 collective-permute-start.3
  37.0 2.5 %shard_map.72 = (f32[4,256,256]{2,1,0:T(8,128)S(1)}, f32[4,256,256]{2,1,0:T(8,128)S(1)}) custom-call(s32[8]{0:T(128)S(1)} %pad_add_fusion.table, f32[4,4,256,256]{3,2,1,0:T(8,128)} %bitcast.7), custom_call_target="tpu_custom_call" | custom-call | bytes 4194304 | tf_op jit(solution)/shard_map/pallas_call | solution.py:104
  39.5 2.3 %shard_map.73 = (f32[4,256,256]{2,1,0:T(8,128)S(1)}, f32[4,256,256]{2,1,0:T(8,128)S(1)}) custom-call(s32[8]{0:T(128)S(1)} %pad_add_fusion.table, f32[4,4,256,256]{3,2,1,0:T(8,128)} %bitcast.8), custom_call_target="tpu_custom_call" | custom-call | bytes 4194304 | tf_op jit(solution)/shard_map/pallas_call | solution.py:104
  41.8 2.2 %collective-permute-start = (s32[8]{0:T(128)S(1)}, s32[8]{0:T(128)S(1)}, u32[]{:S(2)}, u32[]{:S(2)}) collective-permute-start(s32[8]{0:T(128)S(1)} %pad_add_fusion.table), channel_id=1, source_target_pairs={{8,16},{12,20},{16,8},{20,12},{9,17},{13,21},{17,9},{21,13},{10,18... | collective-permute-start | bytes 104 | tf_op jit(solution)/shard_map/ppermute | solution.py:413
  44.0 12.0 %collective-permute-done.3.refs_1_ = s32[8]{0:T(128)S(1)} collective-permute-done((s32[8]{0:T(128)S(1)}, s32[8]{0:T(128)S(1)}, u32[]{:S(2)}, u32[]{:S(2)}) %collective-permute-start.3) | collective-permute-done | bytes 64 | tf_op jit(solution)/shard_map/ppermute | solution.py:413
  55.9 4.6 %collective-permute-start.1 = (s32[8]{0:T(128)S(1)}, s32[8]{0:T(128)S(1)}, u32[]{:S(2)}, u32[]{:S(2)}) collective-permute-start(s32[8]{0:T(128)S(1)} %pad_add_fusion.table), channel_id=1, source_target_pairs={{4,8},{8,4},{12,16},{16,12},{20,24},{24,20},{5,9},{9,5},{13,17},{1... | collective-permute-start | bytes 104 | tf_op jit(solution)/shard_map/ppermute | solution.py:413
  60.5 1.4 %collective-permute-start.12 = (f32[4,256,256]{2,1,0:T(8,128)S(1)}, f32[4,256,256]{2,1,0:T(8,128)S(1)}, u32[]{:S(2)}, u32[]{:S(2)}) collective-permute-start(f32[4,256,256]{2,1,0:T(8,128)S(1)} %get-tuple-element.29), channel_id=1, source_target_pairs={{0,4},{4,0},{8,12},{12,8},{16,20},{20,16},{24,28},{28,24},{1,5},{5... | collective-permute-start | bytes 3145736 | tf_op jit(solution)/shard_map/ppermute | solution.py:413
  61.9 0.4 collective-permute-done.1.refs_1_
  62.3 2.5 %collective-permute-start.13 = (f32[4,256,256]{2,1,0:T(8,128)S(1)}, f32[4,256,256]{2,1,0:T(8,128)S(1)}, u32[]{:S(2)}, u32[]{:S(2)}) collective-permute-start(f32[4,256,256]{2,1,0:T(8,128)S(1)} %get-tuple-element.30), channel_id=1, source_target_pairs={{0,8},{4,12},{8,0},{12,4},{16,24},{20,28},{24,16},{28,20},{1,9},{5... | collective-permute-start | bytes 3145736 | tf_op jit(solution)/shard_map/ppermute | solution.py:413
  64.8 3.3 %collective-permute-start.14 = (f32[4,256,256]{2,1,0:T(8,128)S(1)}, f32[4,256,256]{2,1,0:T(8,128)S(1)}, u32[]{:S(2)}, u32[]{:S(2)}) collective-permute-start(f32[4,256,256]{2,1,0:T(8,128)S(1)} %get-tuple-element.31), channel_id=1, source_target_pairs={{8,16},{12,20},{16,8},{20,12},{9,17},{13,21},{17,9},{21,13},{10,18... | collective-permute-start | bytes 3145736 | tf_op jit(solution)/shard_map/ppermute | solution.py:413
  68.2 3.2 %collective-permute-start.15 = (f32[4,256,256]{2,1,0:T(8,128)S(1)}, f32[4,256,256]{2,1,0:T(8,128)S(1)}, u32[]{:S(2)}, u32[]{:S(2)}) collective-permute-start(f32[4,256,256]{2,1,0:T(8,128)S(1)} %get-tuple-element.32), channel_id=1, source_target_pairs={{4,8},{8,4},{12,16},{16,12},{20,24},{24,20},{5,9},{9,5},{13,17},{1... | collective-permute-start | bytes 3145736 | tf_op jit(solution)/shard_map/ppermute | solution.py:413
  71.3 0.1 shard_map.70
  71.4 0.1 collective-permute-start.10
  71.5 1.5 %collective-permute-done.10.refs_8_ = f32[1,256,256]{2,1,0:T(8,128)S(1)} collective-permute-done((f32[1,256,256]{2,1,0:T(8,128)S(1)}, f32[1,256,256]{2,1,0:T(8,128)S(1)}, u32[]{:S(2)}, u32[]{:S(2)}) %collective-permute-start.10) | collective-permute-done | bytes 262176 | tf_op jit(solution)/shard_map/ppermute | solution.py:413
  73.0 0.7 collective-permute-start.11
  73.7 6.6 %shard_map.69 = (f32[4,4,256,256]{3,2,1,0:T(8,128)}, f32[4,256,256]{2,1,0:T(8,128)S(1)}, f32[4,256,256]{2,1,0:T(8,128)S(1)}, f32[4,256,256]{2,1,0:T(8,128)S(1)},...) custom-call(s32[8]{0:T(128)S(1)} %pad_add_fusion.table, s32[8]{0:T(128)S(1)} %collective-permute-done.2.refs_0_, ...), custom_call_target="tpu_custom_call" | custom-call | flops 31457280 | bytes 17825792 | tf_op jit(solution)/shard_map/pallas_call | solution.py:304
  80.3 6.5 %shard_map.71 = (f32[4,4,256,256]{3,2,1,0:T(8,128)}, f32[4,256,256]{2,1,0:T(8,128)S(1)}, f32[4,256,256]{2,1,0:T(8,128)S(1)}, f32[4,256,256]{2,1,0:T(8,128)S(1)},...) custom-call(s32[8]{0:T(128)S(1)} %pad_add_fusion.table, ...), custom_call_target="tpu_custom_call", output_to_operand_aliasing={{0}: (14, {})} | custom-call | flops 31457280 | bytes 17825792 | tf_op jit(solution)/shard_map/pallas_call | solution.py:304
  86.9 2.0 %collective-permute-done.13.refs_1_ = f32[4,256,256]{2,1,0:T(8,128)S(1)} collective-permute-done((f32[4,256,256]{2,1,0:T(8,128)S(1)}, f32[4,256,256]{2,1,0:T(8,128)S(1)}, u32[]{:S(2)}, u32[]{:S(2)}) %collective-permute-start.13) | collective-permute-done | bytes 1048608 | tf_op jit(solution)/shard_map/ppermute | solution.py:413
  88.8 2.9 %collective-permute-done.14.refs_2_ = f32[4,256,256]{2,1,0:T(8,128)S(1)} collective-permute-done((f32[4,256,256]{2,1,0:T(8,128)S(1)}, f32[4,256,256]{2,1,0:T(8,128)S(1)}, u32[]{:S(2)}, u32[]{:S(2)}) %collective-permute-start.14) | collective-permute-done | bytes 1048608 | tf_op jit(solution)/shard_map/ppermute | solution.py:413
  91.7 21.9 %collective-permute-done.15.refs_3_ = f32[4,256,256]{2,1,0:T(8,128)S(1)} collective-permute-done((f32[4,256,256]{2,1,0:T(8,128)S(1)}, f32[4,256,256]{2,1,0:T(8,128)S(1)}, u32[]{:S(2)}, u32[]{:S(2)}) %collective-permute-start.15) | collective-permute-done | bytes 1048608 | tf_op jit(solution)/shard_map/ppermute | solution.py:413
  113.6 1.9 %shard_map.74 = f32[4,256,256]{2,1,0:T(8,128)} custom-call(f32[4,256,256]{2,1,0:T(8,128)S(1)} %get-tuple-element.28.total, f32[4,256,256]{2,1,0:T(8,128)S(1)} %collective-permute-done.12.refs_0_, f32[4,256,256]{2,1,0:T(8,128)S(1)} %collective-permute-done.13.refs_1_, f32[4,256,256]{2,1,0:T(8,128)S(1)} %collective-permute-done.14.refs_2_, ...), custom_call_target="tpu_custom_call" | custom-call | flops 5242880 | bytes 14680064 | tf_op jit(solution)/shard_map/pallas_call | solution.py:380
  (20 shorter events, 0.1 us)
Async XLA Ops:
  0.6 32.7 %copy-start.5 = (s32[1,4]{1,0:T(1,128)S(1)}, s32[1,4]{1,0:T(1,128)}, u32[]{:S(2)}) copy-start(s32[1,4]{1,0:T(1,128)} %param.8) | copy-start | bytes 52
  0.6 32.7 %copy-start.4 = (s32[1,4]{1,0:T(1,128)S(1)}, s32[1,4]{1,0:T(1,128)}, u32[]{:S(2)}) copy-start(s32[1,4]{1,0:T(1,128)} %param.9) | copy-start | bytes 52
  0.6 25.2 %collective-permute-start.4 = (f32[4,256,256]{2,1,0:T(8,128)}, f32[4,256,256]{2,1,0:T(8,128)S(1)}, u32[]{:S(2)}, u32[]{:S(2)}) collective-permute-start(f32[4,256,256]{2,1,0:T(8,128)} %bitcast.11), channel_id=1, source_target_pairs={{0,4},{4,0},{8,12},{12,8},{16,20},{20,16},{24,28},{28,24},{1,5},{5... | collective-permute-start | bytes 3145736 | tf_op jit(solution)/shard_map/ppermute | solution.py:413
  1.2 24.8 %collective-permute-start.5 = (f32[4,256,256]{2,1,0:T(8,128)}, f32[4,256,256]{2,1,0:T(8,128)S(1)}, u32[]{:S(2)}, u32[]{:S(2)}) collective-permute-start(f32[4,256,256]{2,1,0:T(8,128)} %bitcast.12), channel_id=1, source_target_pairs={{0,8},{4,12},{8,0},{12,4},{16,24},{20,28},{24,16},{28,20},{1,9},{5... | collective-permute-start | bytes 3145736 | tf_op jit(solution)/shard_map/ppermute | solution.py:413
  1.2 27.8 %collective-permute-start.6 = (f32[4,256,256]{2,1,0:T(8,128)}, f32[4,256,256]{2,1,0:T(8,128)S(1)}, u32[]{:S(2)}, u32[]{:S(2)}) collective-permute-start(f32[4,256,256]{2,1,0:T(8,128)} %bitcast.13), channel_id=1, source_target_pairs={{8,16},{12,20},{16,8},{20,12},{9,17},{13,21},{17,9},{21,13},{10,18... | collective-permute-start | bytes 3145736 | tf_op jit(solution)/shard_map/ppermute | solution.py:413
  29.1 1.2 %copy-start.1 = (f32[1,4,256,256]{3,2,1,0:T(8,128)S(1)}, f32[1,4,256,256]{3,2,1,0:T(8,128)}, u32[]{:S(2)}) copy-start(f32[1,4,256,256]{3,2,1,0:T(8,128)} %param.5) | copy-start | bytes 3145732
  30.5 34.3 %collective-permute-start.7 = (f32[4,256,256]{2,1,0:T(8,128)S(1)}, f32[4,256,256]{2,1,0:T(8,128)S(1)}, u32[]{:S(2)}, u32[]{:S(2)}) collective-permute-start(f32[4,256,256]{2,1,0:T(8,128)S(1)} %get-tuple-element.22), channel_id=1, source_target_pairs={{0,1},{1,0},{2,3},{3,2},{4,5},{5,4},{6,7},{7,6},{8,9},{9,8},{10,11... | collective-permute-start | bytes 3145736 | tf_op jit(solution)/shard_map/ppermute | solution.py:413
  30.6 37.5 %collective-permute-start.9 = (f32[4,256,256]{2,1,0:T(8,128)S(1)}, f32[4,256,256]{2,1,0:T(8,128)S(1)}, u32[]{:S(2)}, u32[]{:S(2)}) collective-permute-start(f32[4,256,256]{2,1,0:T(8,128)S(1)} %collective-permute-done.4.refs_1_.refs_5_), channel_id=1, source_target_pairs={{0,8},{8,16},{12,4},{16,24},{20,12},{28,20},{1,9},{9,17},{13,5},{1... | collective-permute-start | bytes 3145736 | tf_op jit(solution)/shard_map/ppermute | solution.py:413
  32.5 38.9 %collective-permute-start.8 = (f32[4,256,256]{2,1,0:T(8,128)S(1)}, f32[4,256,256]{2,1,0:T(8,128)S(1)}, u32[]{:S(2)}, u32[]{:S(2)}) collective-permute-start(f32[4,256,256]{2,1,0:T(8,128)S(1)} %get-tuple-element.23), channel_id=1, source_target_pairs={{1,2},{2,1},{5,6},{6,5},{9,10},{10,9},{13,14},{14,13},{17,18},{18,... | collective-permute-start | bytes 3145736 | tf_op jit(solution)/shard_map/ppermute | solution.py:413
  33.4 8.4 %collective-permute-start.2 = (s32[8]{0:T(128)S(1)}, s32[8]{0:T(128)S(1)}, u32[]{:S(2)}, u32[]{:S(2)}) collective-permute-start(s32[8]{0:T(128)S(1)} %pad_add_fusion.table), channel_id=1, source_target_pairs={{0,4},{4,0},{8,12},{12,8},{16,20},{20,16},{24,28},{28,24},{1,5},{5... | collective-permute-start | bytes 104 | tf_op jit(solution)/shard_map/ppermute | solution.py:413
  36.6 19.3 %collective-permute-start.3 = (s32[8]{0:T(128)S(1)}, s32[8]{0:T(128)S(1)}, u32[]{:S(2)}, u32[]{:S(2)}) collective-permute-start(s32[8]{0:T(128)S(1)} %pad_add_fusion.table), channel_id=1, source_target_pairs={{0,8},{4,12},{8,0},{12,4},{16,24},{20,28},{24,16},{28,20},{1,9},{5... | collective-permute-start | bytes 104 | tf_op jit(solution)/shard_map/ppermute | solution.py:413
  37.0 36.7 %copy-start = (f32[1,4,4,256,256]{4,3,2,1,0:T(8,128)S(1)}, f32[1,4,4,256,256]{4,3,2,1,0:T(8,128)}, u32[]{:S(2)}) copy-start(f32[1,4,4,256,256]{4,3,2,1,0:T(8,128)} %param.7) | copy-start | bytes 12582916
  37.0 36.7 %copy-start.2 = (f32[1,4,256,256]{3,2,1,0:T(8,128)S(1)}, f32[1,4,256,256]{3,2,1,0:T(8,128)}, u32[]{:S(2)}) copy-start(f32[1,4,256,256]{3,2,1,0:T(8,128)} %param.5) | copy-start | bytes 3145732
  37.0 36.7 %copy-start.3 = (f32[1,4,256,256]{3,2,1,0:T(8,128)S(1)}, f32[1,4,256,256]{3,2,1,0:T(8,128)}, u32[]{:S(2)}) copy-start(f32[1,4,256,256]{3,2,1,0:T(8,128)} %param.6) | copy-start | bytes 3145732
  41.8 18.7 %collective-permute-start = (s32[8]{0:T(128)S(1)}, s32[8]{0:T(128)S(1)}, u32[]{:S(2)}, u32[]{:S(2)}) collective-permute-start(s32[8]{0:T(128)S(1)} %pad_add_fusion.table), channel_id=1, source_target_pairs={{8,16},{12,20},{16,8},{20,12},{9,17},{13,21},{17,9},{21,13},{10,18... | collective-permute-start | bytes 104 | tf_op jit(solution)/shard_map/ppermute | solution.py:413
  55.9 6.3 %collective-permute-start.1 = (s32[8]{0:T(128)S(1)}, s32[8]{0:T(128)S(1)}, u32[]{:S(2)}, u32[]{:S(2)}) collective-permute-start(s32[8]{0:T(128)S(1)} %pad_add_fusion.table), channel_id=1, source_target_pairs={{4,8},{8,4},{12,16},{16,12},{20,24},{24,20},{5,9},{9,5},{13,17},{1... | collective-permute-start | bytes 104 | tf_op jit(solution)/shard_map/ppermute | solution.py:413
  60.5 26.3 %collective-permute-start.12 = (f32[4,256,256]{2,1,0:T(8,128)S(1)}, f32[4,256,256]{2,1,0:T(8,128)S(1)}, u32[]{:S(2)}, u32[]{:S(2)}) collective-permute-start(f32[4,256,256]{2,1,0:T(8,128)S(1)} %get-tuple-element.29), channel_id=1, source_target_pairs={{0,4},{4,0},{8,12},{12,8},{16,20},{20,16},{24,28},{28,24},{1,5},{5... | collective-permute-start | bytes 3145736 | tf_op jit(solution)/shard_map/ppermute | solution.py:413
  62.3 26.5 %collective-permute-start.13 = (f32[4,256,256]{2,1,0:T(8,128)S(1)}, f32[4,256,256]{2,1,0:T(8,128)S(1)}, u32[]{:S(2)}, u32[]{:S(2)}) collective-permute-start(f32[4,256,256]{2,1,0:T(8,128)S(1)} %get-tuple-element.30), channel_id=1, source_target_pairs={{0,8},{4,12},{8,0},{12,4},{16,24},{20,28},{24,16},{28,20},{1,9},{5... | collective-permute-start | bytes 3145736 | tf_op jit(solution)/shard_map/ppermute | solution.py:413
  64.8 26.9 %collective-permute-start.14 = (f32[4,256,256]{2,1,0:T(8,128)S(1)}, f32[4,256,256]{2,1,0:T(8,128)S(1)}, u32[]{:S(2)}, u32[]{:S(2)}) collective-permute-start(f32[4,256,256]{2,1,0:T(8,128)S(1)} %get-tuple-element.31), channel_id=1, source_target_pairs={{8,16},{12,20},{16,8},{20,12},{9,17},{13,21},{17,9},{21,13},{10,18... | collective-permute-start | bytes 3145736 | tf_op jit(solution)/shard_map/ppermute | solution.py:413
  68.2 45.4 %collective-permute-start.15 = (f32[4,256,256]{2,1,0:T(8,128)S(1)}, f32[4,256,256]{2,1,0:T(8,128)S(1)}, u32[]{:S(2)}, u32[]{:S(2)}) collective-permute-start(f32[4,256,256]{2,1,0:T(8,128)S(1)} %get-tuple-element.32), channel_id=1, source_target_pairs={{4,8},{8,4},{12,16},{16,12},{20,24},{24,20},{5,9},{9,5},{13,17},{1... | collective-permute-start | bytes 3145736 | tf_op jit(solution)/shard_map/ppermute | solution.py:413
  71.4 1.6 %collective-permute-start.10 = (f32[1,256,256]{2,1,0:T(8,128)S(1)}, f32[1,256,256]{2,1,0:T(8,128)S(1)}, u32[]{:S(2)}, u32[]{:S(2)}) collective-permute-start(f32[1,256,256]{2,1,0:T(8,128)S(1)} %get-tuple-element.25), channel_id=1, source_target_pairs={{0,1},{1,0},{2,3},{3,2},{4,5},{5,4},{6,7},{7,6},{8,9},{9,8},{10,11... | collective-permute-start | bytes 786440 | tf_op jit(solution)/shard_map/ppermute | solution.py:413
  73.0 7.3 %collective-permute-start.11 = (f32[1,256,256]{2,1,0:T(8,128)S(1)}, f32[1,256,256]{2,1,0:T(8,128)S(1)}, u32[]{:S(2)}, u32[]{:S(2)}) collective-permute-start(f32[1,256,256]{2,1,0:T(8,128)S(1)} %get-tuple-element.26), channel_id=1, source_target_pairs={{1,2},{2,1},{5,6},{6,5},{9,10},{10,9},{13,14},{14,13},{17,18},{18,... | collective-permute-start | bytes 786440 | tf_op jit(solution)/shard_map/ppermute | solution.py:413

commit v3 on v2

--- a/solution.py
+++ b/solution.py
@@ -62,9 +62,16 @@
     return near if place % 2 == 0 else -near
 
 
-def pack_kernel(places, stride, table, dual, *refs):
+def piece_of(pieces, z):
+    for piece, size in enumerate(pieces):
+        if z < size:
+            return piece, z
+        z -= size
+
+
+def pack_kernel(places, pieces, stride, table, dual, *refs):
     count = len(places)
-    outs, (held, sems) = refs[:count], refs[count:]
+    outs, (held, sems) = refs[: count * len(pieces)], refs[count * len(pieces) :]
     depth, rows = dual.shape[1:3]
     moves = []
     for j, place in enumerate(places):
@@ -90,7 +97,8 @@
             y = pl.multiple_of(step * STEP, STEP)
             for z in range(depth):
                 for half in range(2):
-                    outs[j][z, pl.ds(y, STEP), pl.ds(half * LANES, LANES)] = held[
+                    piece, within = piece_of(pieces, z)
+                    outs[j * len(pieces) + piece][within, pl.ds(y, STEP), pl.ds(half * LANES, LANES)] = held[
                         j, z, half, pl.ds(RIM + y + offset, STEP), :
                     ]
             return carry
@@ -98,14 +106,14 @@
         lax.fori_loop(0, rows // STEP, body, 0)
 
 
-def pack(places, stride, table, dual):
+def pack(places, pieces, stride, table, dual):
     _, depth, rows, columns = dual.shape
     count = len(places)
     return pl.pallas_call(
-        functools.partial(pack_kernel, places, stride),
+        functools.partial(pack_kernel, places, pieces, stride),
         in_specs=[pl.BlockSpec(memory_space=pltpu.SMEM), pl.BlockSpec(memory_space=pltpu.HBM)],
-        out_specs=[pl.BlockSpec(memory_space=pltpu.VMEM)] * count,
-        out_shape=[jax.ShapeDtypeStruct((depth, rows, columns), jnp.float32)] * count,
+        out_specs=[pl.BlockSpec(memory_space=pltpu.VMEM)] * (count * len(pieces)),
+        out_shape=[jax.ShapeDtypeStruct((size, rows, columns), jnp.float32) for size in pieces] * count,
         scratch_shapes=[
             pltpu.VMEM((count, depth, 2, rows + 2 * RIM, LANES), jnp.float32),
             pltpu.SemaphoreType.DMA((2 * count,)),
@@ -316,7 +324,7 @@
             pltpu.SemaphoreType.DMA((6 * count + 2,)),
             pltpu.SemaphoreType.DMA((PARTS * count,)),
         ],
-        compiler_params=pltpu.CompilerParams(vmem_limit_bytes=16 << 20),
+        compiler_params=pltpu.CompilerParams(vmem_limit_bytes=20 << 20),
         cost_estimate=pl.CostEstimate(
             flops=count * 60 * cells, bytes_accessed=4 * (3 + 7 * count) * cells, transcendentals=2 * count * cells
         ),
@@ -356,32 +364,47 @@
     )(*images)
 
 
-def settle_kernel(count, total, *refs):
-    duals, weights, gains, out = refs[:count], refs[count : 2 * count], refs[2 * count : 3 * count], refs[-1]
+def settle_kernel(count, pieces, last, total, *refs):
+    refs = list(refs)
+    take = lambda k: [refs.pop(0) for _ in range(k)]
+    duals, weights, gains = take(count * len(pieces)), take(count), take(count)
+    if last:
+        result, out, sems = refs
+    else:
+        (out,) = refs
     depth, rows, _ = total.shape
-
-    def body(step, carry):
-        here = pl.ds(pl.multiple_of(step * STEP, STEP), STEP)
-        for z in range(depth):
+    moves = []
+    for z in range(depth):
+        piece, within = piece_of(pieces, z)
+
+        def body(step, carry):
+            here = pl.ds(pl.multiple_of(step * STEP, STEP), STEP)
             arriving = None
             for i in range(count):
-                value = duals[i][z, here, :] + gains[i][z, here, :]
+                value = duals[i * len(pieces) + piece][within, here, :] + gains[i][z, here, :]
                 value = weights[i][z, here, :] * jnp.minimum(jnp.maximum(value, -dual_bound), dual_bound)
                 arriving = value if arriving is None else arriving + value
             out[z, here, :] = total[z, here, :] - flow * arriving
-        return carry
-
-    lax.fori_loop(0, rows // STEP, body, 0)
-
-
-def settle(total, duals, weights, gains):
-    count = len(duals)
+            return carry
+
+        lax.fori_loop(0, rows // STEP, body, 0)
+        if last:
+            moves.append(pltpu.make_async_copy(out.at[z], result.at[z], sems.at[z]))
+            moves[-1].start()
+    for m in moves:
+        m.wait()
+
+
+def settle(total, duals, pieces, weights, gains, last):
+    count = len(weights)
+    depth = total.shape[0]
     vmem_spec = pl.BlockSpec(memory_space=pltpu.VMEM)
     return pl.pallas_call(
-        functools.partial(settle_kernel, count),
-        in_specs=[vmem_spec] * (1 + 3 * count),
-        out_specs=vmem_spec,
+        functools.partial(settle_kernel, count, pieces, last),
+        in_specs=[vmem_spec] * (1 + len(duals) + 2 * count),
+        out_specs=pl.BlockSpec(memory_space=pl.ANY) if last else vmem_spec,
         out_shape=jax.ShapeDtypeStruct(total.shape, jnp.float32),
+        scratch_shapes=[pltpu.VMEM(total.shape, jnp.float32), pltpu.SemaphoreType.DMA((depth,))] if last else [],
         compiler_params=pltpu.CompilerParams(vmem_limit_bytes=10 << 20),
         cost_estimate=pl.CostEstimate(
             flops=5 * count * total.size, bytes_accessed=4 * (2 + 3 * count) * total.size, transcendentals=0
@@ -425,27 +448,32 @@
     far_table = send(table, cross)
     wide_near_table = send(table, wide_swap)
     wide_far_table = send(table, wide_cross)
-    near_dual, far_dual = pack((0, 1), stride, table, dual)
+    depth = image.shape[0]
+    lead = max(depth // 4, 1)
+    pieces = (lead, depth - lead)
+    near_dual, far_dual = pack((0, 1), (depth,), stride, table, dual)
     near_dual = send(near_dual, swap)
     far_dual = send(far_dual, cross)
+    wide = list(pack((2, 3), pieces, stride, table, dual))
+    wide[0] = send(wide[0], wide_swap)
+    wide[2] = send(wide[2], wide_cross)
     far_image = send(near_image, relay)
 
     within, across = halos((image, near_image, wide_near_image, wide_far_image))
-    wide_near_dual, wide_far_dual = pack((2, 3), stride, table, dual)
-    wide_near_dual = send(wide_near_dual, wide_swap)
-    wide_far_dual = send(wide_far_dual, wide_cross)
-    fresh, total, w0, w2, g0, g2 = pairs(
-        ((0, 1), (2, 2)), stride, table, (near_table, wide_near_table), image, dual, prior_image[0],
-        (near_image, wide_near_image), (within,) * 2, (across,) * 2, (within, across),
+    wide[1] = send(wide[1], wide_swap)
+    wide[3] = send(wide[3], wide_cross)
+    fresh, total, w0, w2, w3, g0, g2, g3 = pairs(
+        ((0, 1), (2, 2), (3, 3)), stride, table, (near_table, wide_near_table, wide_far_table),
+        image, dual, prior_image[0],
+        (near_image, wide_near_image, wide_far_image), (within,) * 3, (across,) * 3, (within, across),
     )
     far_within, far_across = halos((far_image,))
-    fresh, total, w3, w1, g3, g1 = pairs(
-        ((3, 3), (1, 0)), stride, table, (wide_far_table, far_table), image, dual, total,
-        (wide_far_image, far_image), (within, far_within), (across, far_across), (within, across), fresh,
+    fresh, total, w1, g1 = pairs(
+        ((1, 0),), stride, table, (far_table,), image, dual, total,
+        (far_image,), (far_within,), (far_across,), (within, across), fresh,
     )
-    volume_next = settle(
-        total, (near_dual, wide_near_dual, wide_far_dual, far_dual), (w0, w2, w3, w1), (g0, g2, g3, g1)
-    )
+    total = settle(total, (near_dual, far_dual), (depth,), (w0, w1), (g0, g1), False)
+    volume_next = settle(total, wide, pieces, (w2, w3), (g2, g3), True)
     return (volume_next[None], fresh[None])
 
 

time: 116 us -> 112 us (0.966)
  the two profiles are of different devices: /device:TPU:12 before, /device:TPU:10 now
where the time goes in v3:
time: 112 us; the launch traced here: 111 us
  waiting for transfers between devices  57.3 us (51%)
  starting transfers between devices  32.5 us (29%)
  Pallas kernels  19.7 us (18%)
    ppermute x18, waiting for transfers between devices, send(): return lax.ppermute(x, axis, pairs_)  57.3 us
    ppermute x18, starting transfers between devices, send(): return lax.ppermute(x, axis, pairs_)  32.5 us
    pallas_call x2, Pallas kernels, pairs(): pl.pallas_call(functools.partial(pair_kernel, places, first, stride), in_...  12.8 us
    pallas_call x2, Pallas kernels, pack(): pl.pallas_call(functools.partial(pack_kernel, places, pieces, stride), in...  4.5 us
  transfers between devices with their start and end apart: 18, of which 8 were waited for; matrix products, arithmetic and copies ran while one was open for 1% of the time, Pallas kernels for 16%

profile of v3, /device:TPU:10, one launch (start us, length us, event | category | flops | bytes accessed | tf_op | source)
XLA Modules:
  0.0 111.2 jit_solution(7347280672975673440)
XLA Ops:
  0.6 1.6 %collective-permute-start.4 = (f32[4,256,256]{2,1,0:T(8,128)}, f32[4,256,256]{2,1,0:T(8,128)S(1)}, u32[]{:S(2)}, u32[]{:S(2)}) collective-permute-start(f32[4,256,256]{2,1,0:T(8,128)} %bitcast.11), channel_id=1, source_target_pairs={{0,4},{4,0},{8,12},{12,8},{16,20},{20,16},{24,28},{28,24},{1,5},{5... | collective-permute-start | bytes 3145736 | tf_op jit(solution)/shard_map/ppermute | solution.py:436
  2.2 0.4 collective-permute-start.5
  2.7 4.6 %collective-permute-start.6 = (f32[4,256,256]{2,1,0:T(8,128)}, f32[4,256,256]{2,1,0:T(8,128)S(1)}, u32[]{:S(2)}, u32[]{:S(2)}) collective-permute-start(f32[4,256,256]{2,1,0:T(8,128)} %bitcast.13), channel_id=1, source_target_pairs={{8,16},{12,20},{16,8},{20,12},{9,17},{13,21},{17,9},{21,13},{10,18... | collective-permute-start | bytes 3145736 | tf_op jit(solution)/shard_map/ppermute | solution.py:436
  7.3 0.7 pad_add_fusion.table
  8.0 2.2 %shard_map.72 = (f32[4,256,256]{2,1,0:T(8,128)S(1)}, f32[4,256,256]{2,1,0:T(8,128)S(1)}) custom-call(s32[8]{0:T(128)S(1)} %pad_add_fusion.table, f32[4,4,256,256]{3,2,1,0:T(8,128)} %bitcast.7), custom_call_target="tpu_custom_call" | custom-call | bytes 4194304 | tf_op jit(solution)/shard_map/pallas_call | solution.py:112
  10.3 0.6 collective-permute-start.12
  10.9 16.1 %collective-permute-done.4.refs_1_.refs_6_ = f32[4,256,256]{2,1,0:T(8,128)S(1)} collective-permute-done((f32[4,256,256]{2,1,0:T(8,128)}, f32[4,256,256]{2,1,0:T(8,128)S(1)}, u32[]{:S(2)}, u32[]{:S(2)}) %collective-permute-start.4) | collective-permute-done | bytes 1048608 | tf_op jit(solution)/shard_map/ppermute | solution.py:436
  26.9 3.5 %collective-permute-start.9 = (f32[4,256,256]{2,1,0:T(8,128)S(1)}, f32[4,256,256]{2,1,0:T(8,128)S(1)}, u32[]{:S(2)}, u32[]{:S(2)}) collective-permute-start(f32[4,256,256]{2,1,0:T(8,128)S(1)} %collective-permute-done.4.refs_1_.refs_6_), channel_id=1, source_target_pairs={{0,8},{8,16},{12,4},{16,24},{20,12},{28,20},{1,9},{9,17},{13,5},{1... | collective-permute-start | bytes 3145736 | tf_op jit(solution)/shard_map/ppermute | solution.py:436
  30.5 0.3 shard_map.68
  30.8 2.5 %collective-permute-start.8 = (f32[4,256,256]{2,1,0:T(8,128)S(1)}, f32[4,256,256]{2,1,0:T(8,128)S(1)}, u32[]{:S(2)}, u32[]{:S(2)}) collective-permute-start(f32[4,256,256]{2,1,0:T(8,128)S(1)} %get-tuple-element.25), channel_id=1, source_target_pairs={{1,2},{2,1},{5,6},{6,5},{9,10},{10,9},{13,14},{14,13},{17,18},{18,... | collective-permute-start | bytes 3145736 | tf_op jit(solution)/shard_map/ppermute | solution.py:436
  33.3 0.5 collective-permute-start.1
  33.8 14.6 %collective-permute-done.1.refs_0_ = s32[8]{0:T(128)S(1)} collective-permute-done((s32[8]{0:T(128)S(1)}, s32[8]{0:T(128)S(1)}, u32[]{:S(2)}, u32[]{:S(2)}) %collective-permute-start.1) | collective-permute-done | bytes 64 | tf_op jit(solution)/shard_map/ppermute | solution.py:436
  48.4 0.4 collective-permute-start.2
  48.8 3.1 %collective-permute-done.2.refs_1_ = s32[8]{0:T(128)S(1)} collective-permute-done((s32[8]{0:T(128)S(1)}, s32[8]{0:T(128)S(1)}, u32[]{:S(2)}, u32[]{:S(2)}) %collective-permute-start.2) | collective-permute-done | bytes 64 | tf_op jit(solution)/shard_map/ppermute | solution.py:436
  52.0 3.5 %collective-permute-start.3 = (s32[8]{0:T(128)S(1)}, s32[8]{0:T(128)S(1)}, u32[]{:S(2)}, u32[]{:S(2)}) collective-permute-start(s32[8]{0:T(128)S(1)} %pad_add_fusion.table), channel_id=1, source_target_pairs={{8,16},{12,20},{16,8},{20,12},{9,17},{13,21},{17,9},{21,13},{10,18... | collective-permute-start | bytes 104 | tf_op jit(solution)/shard_map/ppermute | solution.py:436
  55.4 2.0 %collective-permute-done.3.refs_2_ = s32[8]{0:T(128)S(1)} collective-permute-done((s32[8]{0:T(128)S(1)}, s32[8]{0:T(128)S(1)}, u32[]{:S(2)}, u32[]{:S(2)}) %collective-permute-start.3) | collective-permute-done | bytes 64 | tf_op jit(solution)/shard_map/ppermute | solution.py:436
  57.4 1.9 %collective-permute-start = (s32[8]{0:T(128)S(1)}, s32[8]{0:T(128)S(1)}, u32[]{:S(2)}, u32[]{:S(2)}) collective-permute-start(s32[8]{0:T(128)S(1)} %pad_add_fusion.table), channel_id=1, source_target_pairs={{4,8},{8,4},{12,16},{16,12},{20,24},{24,20},{5,9},{9,5},{13,17},{1... | collective-permute-start | bytes 104 | tf_op jit(solution)/shard_map/ppermute | solution.py:436
  59.3 4.4 %collective-permute-done.refs_0_ = s32[8]{0:T(128)S(1)} collective-permute-done((s32[8]{0:T(128)S(1)}, s32[8]{0:T(128)S(1)}, u32[]{:S(2)}, u32[]{:S(2)}) %collective-permute-start) | collective-permute-done | bytes 64 | tf_op jit(solution)/shard_map/ppermute | solution.py:436
  63.8 1.9 %collective-permute-start.13 = (f32[4,256,256]{2,1,0:T(8,128)S(1)}, f32[4,256,256]{2,1,0:T(8,128)S(1)}, u32[]{:S(2)}, u32[]{:S(2)}) collective-permute-start(f32[4,256,256]{2,1,0:T(8,128)S(1)} %get-tuple-element.32), channel_id=1, source_target_pairs={{4,8},{8,4},{12,16},{16,12},{20,24},{24,20},{5,9},{9,5},{13,17},{1... | collective-permute-start | bytes 3145736 | tf_op jit(solution)/shard_map/ppermute | solution.py:436
  65.7 2.3 %shard_map.74 = (f32[1,256,256]{2,1,0:T(8,128)S(1)}, f32[3,256,256]{2,1,0:T(8,128)S(1)}, f32[1,256,256]{2,1,0:T(8,128)S(1)}, f32[3,256,256]{2,1,0:T(8,128)S(1)}) custom-call(s32[8]{0:T(128)S(1)} %pad_add_fusion.table, f32[4,4,256,256]{3,2,1,0:T(8,128)} %bitcast.8), custom_call_target="tpu_custom_call" | custom-call | bytes 4194304 | tf_op jit(solution)/shard_map/pallas_call | solution.py:112
  67.9 0.1 collective-permute-start.15
  68.0 6.4 %collective-permute-start.17 = (f32[3,256,256]{2,1,0:T(8,128)S(1)}, f32[3,256,256]{2,1,0:T(8,128)S(1)}, u32[]{:S(2)}, u32[]{:S(2)}) collective-permute-start(f32[3,256,256]{2,1,0:T(8,128)S(1)} %get-tuple-element.40), channel_id=1, source_target_pairs={{8,16},{12,20},{16,8},{20,12},{9,17},{13,21},{17,9},{21,13},{10,18... | collective-permute-start | bytes 2359304 | tf_op jit(solution)/shard_map/ppermute | solution.py:436
  74.4 0.1 shard_map.70
  74.6 2.5 %collective-permute-start.11 = (f32[1,256,256]{2,1,0:T(8,128)S(1)}, f32[1,256,256]{2,1,0:T(8,128)S(1)}, u32[]{:S(2)}, u32[]{:S(2)}) collective-permute-start(f32[1,256,256]{2,1,0:T(8,128)S(1)} %get-tuple-element.28), channel_id=1, source_target_pairs={{1,2},{2,1},{5,6},{6,5},{9,10},{10,9},{13,14},{14,13},{17,18},{18,... | collective-permute-start | bytes 786440 | tf_op jit(solution)/shard_map/ppermute | solution.py:436
  77.3 5.1 %collective-permute-done.11.refs_6_ = f32[1,256,256]{2,1,0:T(8,128)S(1)} collective-permute-done((f32[1,256,256]{2,1,0:T(8,128)S(1)}, f32[1,256,256]{2,1,0:T(8,128)S(1)}, u32[]{:S(2)}, u32[]{:S(2)}) %collective-permute-start.11) | collective-permute-done | bytes 262176 | tf_op jit(solution)/shard_map/ppermute | solution.py:436
  82.3 1.9 %collective-permute-start.16 = (f32[1,256,256]{2,1,0:T(8,128)S(1)}, f32[1,256,256]{2,1,0:T(8,128)S(1)}, u32[]{:S(2)}, u32[]{:S(2)}) collective-permute-start(f32[1,256,256]{2,1,0:T(8,128)S(1)} %get-tuple-element.39), channel_id=1, source_target_pairs={{8,16},{12,20},{16,8},{20,12},{9,17},{13,21},{17,9},{21,13},{10,18... | collective-permute-start | bytes 786440 | tf_op jit(solution)/shard_map/ppermute | solution.py:436
  84.3 8.9 %shard_map.69 = (f32[4,4,256,256]{3,2,1,0:T(8,128)}, f32[4,256,256]{2,1,0:T(8,128)S(1)}, f32[4,256,256]{2,1,0:T(8,128)S(1)}, f32[4,256,256]{2,1,0:T(8,128)S(1)},...) custom-call(s32[8]{0:T(128)S(1)} %pad_add_fusion.table, ...), custom_call_target="tpu_custom_call" | custom-call | flops 47185920 | bytes 25165824 | tf_op jit(solution)/shard_map/pallas_call | solution.py:312
  93.2 3.9 %shard_map.71 = (f32[4,4,256,256]{3,2,1,0:T(8,128)}, f32[4,256,256]{2,1,0:T(8,128)S(1)}, f32[4,256,256]{2,1,0:T(8,128)S(1)}, f32[4,256,256]{2,1,0:T(8,128)S(1)}) custom-call(s32[8]{0:T(128)S(1)} %pad_add_fusion.table, s32[8]{0:T(128)S(1)} %collective-permute-done.refs_0_, f32[4,256,256]{2,1,0:T(8,128)S(1)} %bitcast.16, ...), custom_call_target="tpu_custom_call", output_to_operand_aliasing={{0}: (10, {})} | custom-call | flops 15728640 | bytes 10485760 | tf_op jit(solution)/shard_map/pallas_call | solution.py:312
  97.1 0.7 shard_map.73.total
  97.8 8.9 %collective-permute-done.14.refs_0_ = f32[1,256,256]{2,1,0:T(8,128)S(1)} collective-permute-done((f32[1,256,256]{2,1,0:T(8,128)S(1)}, f32[1,256,256]{2,1,0:T(8,128)S(1)}, u32[]{:S(2)}, u32[]{:S(2)}) %collective-permute-start.14) | collective-permute-done | bytes 262176 | tf_op jit(solution)/shard_map/ppermute | solution.py:436
  106.7 3.1 %collective-permute-done.16.refs_2_ = f32[1,256,256]{2,1,0:T(8,128)S(1)} collective-permute-done((f32[1,256,256]{2,1,0:T(8,128)S(1)}, f32[1,256,256]{2,1,0:T(8,128)S(1)}, u32[]{:S(2)}, u32[]{:S(2)}) %collective-permute-start.16) | collective-permute-done | bytes 262176 | tf_op jit(solution)/shard_map/ppermute | solution.py:436
  109.9 1.4 %shard_map.75 = f32[4,256,256]{2,1,0:T(8,128)} custom-call(f32[4,256,256]{2,1,0:T(8,128)S(1)} %shard_map.73.total, f32[1,256,256]{2,1,0:T(8,128)S(1)} %collective-permute-done.14.refs_0_, f32[3,256,256]{2,1,0:T(8,128)S(1)} %collective-permute-done.15.refs_1_, f32[1,256,256]{2,1,0:T(8,128)S(1)} %collective-permute-done.16.refs_2_, ...), custom_call_target="tpu_custom_call" | custom-call | flops 2621440 | bytes 8388608 | tf_op jit(solution)/shard_map/pallas_call | solution.py:402
  (19 shorter events, 0.3 us)
Async XLA Ops:
  0.6 29.8 %copy-start.1 = (f32[1,4,256,256]{3,2,1,0:T(8,128)S(1)}, f32[1,4,256,256]{3,2,1,0:T(8,128)}, u32[]{:S(2)}) copy-start(f32[1,4,256,256]{3,2,1,0:T(8,128)} %param.5) | copy-start | bytes 3145732
  0.6 26.3 %collective-permute-start.4 = (f32[4,256,256]{2,1,0:T(8,128)}, f32[4,256,256]{2,1,0:T(8,128)S(1)}, u32[]{:S(2)}, u32[]{:S(2)}) collective-permute-start(f32[4,256,256]{2,1,0:T(8,128)} %bitcast.11), channel_id=1, source_target_pairs={{0,4},{4,0},{8,12},{12,8},{16,20},{20,16},{24,28},{28,24},{1,5},{5... | collective-permute-start | bytes 3145736 | tf_op jit(solution)/shard_map/ppermute | solution.py:436
  2.2 28.2 %collective-permute-start.5 = (f32[4,256,256]{2,1,0:T(8,128)}, f32[4,256,256]{2,1,0:T(8,128)S(1)}, u32[]{:S(2)}, u32[]{:S(2)}) collective-permute-start(f32[4,256,256]{2,1,0:T(8,128)} %bitcast.12), channel_id=1, source_target_pairs={{0,8},{4,12},{8,0},{12,4},{16,24},{20,28},{24,16},{28,20},{1,9},{5... | collective-permute-start | bytes 3145736 | tf_op jit(solution)/shard_map/ppermute | solution.py:436
  2.7 27.8 %collective-permute-start.6 = (f32[4,256,256]{2,1,0:T(8,128)}, f32[4,256,256]{2,1,0:T(8,128)S(1)}, u32[]{:S(2)}, u32[]{:S(2)}) collective-permute-start(f32[4,256,256]{2,1,0:T(8,128)} %bitcast.13), channel_id=1, source_target_pairs={{8,16},{12,20},{16,8},{20,12},{9,17},{13,21},{17,9},{21,13},{10,18... | collective-permute-start | bytes 3145736 | tf_op jit(solution)/shard_map/ppermute | solution.py:436
  10.3 74.0 %copy-start = (f32[1,4,4,256,256]{4,3,2,1,0:T(8,128)S(1)}, f32[1,4,4,256,256]{4,3,2,1,0:T(8,128)}, u32[]{:S(2)}) copy-start(f32[1,4,4,256,256]{4,3,2,1,0:T(8,128)} %param.7) | copy-start | bytes 12582916
  10.3 74.0 %copy-start.2 = (f32[1,4,256,256]{3,2,1,0:T(8,128)S(1)}, f32[1,4,256,256]{3,2,1,0:T(8,128)}, u32[]{:S(2)}) copy-start(f32[1,4,256,256]{3,2,1,0:T(8,128)} %param.6) | copy-start | bytes 3145732
  10.3 57.6 %collective-permute-start.12 = (f32[4,256,256]{2,1,0:T(8,128)S(1)}, f32[4,256,256]{2,1,0:T(8,128)S(1)}, u32[]{:S(2)}, u32[]{:S(2)}) collective-permute-start(f32[4,256,256]{2,1,0:T(8,128)S(1)} %get-tuple-element.31), channel_id=1, source_target_pairs={{0,4},{4,0},{8,12},{12,8},{16,20},{20,16},{24,28},{28,24},{1,5},{5... | collective-permute-start | bytes 3145736 | tf_op jit(solution)/shard_map/ppermute | solution.py:436
  26.9 41.1 %collective-permute-start.9 = (f32[4,256,256]{2,1,0:T(8,128)S(1)}, f32[4,256,256]{2,1,0:T(8,128)S(1)}, u32[]{:S(2)}, u32[]{:S(2)}) collective-permute-start(f32[4,256,256]{2,1,0:T(8,128)S(1)} %collective-permute-done.4.refs_1_.refs_6_), channel_id=1, source_target_pairs={{0,8},{8,16},{12,4},{16,24},{20,12},{28,20},{1,9},{9,17},{13,5},{1... | collective-permute-start | bytes 3145736 | tf_op jit(solution)/shard_map/ppermute | solution.py:436
  30.7 43.8 %collective-permute-start.7 = (f32[4,256,256]{2,1,0:T(8,128)S(1)}, f32[4,256,256]{2,1,0:T(8,128)S(1)}, u32[]{:S(2)}, u32[]{:S(2)}) collective-permute-start(f32[4,256,256]{2,1,0:T(8,128)S(1)} %get-tuple-element.24), channel_id=1, source_target_pairs={{0,1},{1,0},{2,3},{3,2},{4,5},{5,4},{6,7},{7,6},{8,9},{9,8},{10,11... | collective-permute-start | bytes 3145736 | tf_op jit(solution)/shard_map/ppermute | solution.py:436
  30.8 43.8 %collective-permute-start.8 = (f32[4,256,256]{2,1,0:T(8,128)S(1)}, f32[4,256,256]{2,1,0:T(8,128)S(1)}, u32[]{:S(2)}, u32[]{:S(2)}) collective-permute-start(f32[4,256,256]{2,1,0:T(8,128)S(1)} %get-tuple-element.25), channel_id=1, source_target_pairs={{1,2},{2,1},{5,6},{6,5},{9,10},{10,9},{13,14},{14,13},{17,18},{18,... | collective-permute-start | bytes 3145736 | tf_op jit(solution)/shard_map/ppermute | solution.py:436
  33.3 15.0 %collective-permute-start.1 = (s32[8]{0:T(128)S(1)}, s32[8]{0:T(128)S(1)}, u32[]{:S(2)}, u32[]{:S(2)}) collective-permute-start(s32[8]{0:T(128)S(1)} %pad_add_fusion.table), channel_id=1, source_target_pairs={{0,4},{4,0},{8,12},{12,8},{16,20},{20,16},{24,28},{28,24},{1,5},{5... | collective-permute-start | bytes 104 | tf_op jit(solution)/shard_map/ppermute | solution.py:436
  48.4 3.6 %collective-permute-start.2 = (s32[8]{0:T(128)S(1)}, s32[8]{0:T(128)S(1)}, u32[]{:S(2)}, u32[]{:S(2)}) collective-permute-start(s32[8]{0:T(128)S(1)} %pad_add_fusion.table), channel_id=1, source_target_pairs={{0,8},{4,12},{8,0},{12,4},{16,24},{20,28},{24,16},{28,20},{1,9},{5... | collective-permute-start | bytes 104 | tf_op jit(solution)/shard_map/ppermute | solution.py:436
  52.0 5.5 %collective-permute-start.3 = (s32[8]{0:T(128)S(1)}, s32[8]{0:T(128)S(1)}, u32[]{:S(2)}, u32[]{:S(2)}) collective-permute-start(s32[8]{0:T(128)S(1)} %pad_add_fusion.table), channel_id=1, source_target_pairs={{8,16},{12,20},{16,8},{20,12},{9,17},{13,21},{17,9},{21,13},{10,18... | collective-permute-start | bytes 104 | tf_op jit(solution)/shard_map/ppermute | solution.py:436
  57.4 6.3 %collective-permute-start = (s32[8]{0:T(128)S(1)}, s32[8]{0:T(128)S(1)}, u32[]{:S(2)}, u32[]{:S(2)}) collective-permute-start(s32[8]{0:T(128)S(1)} %pad_add_fusion.table), channel_id=1, source_target_pairs={{4,8},{8,4},{12,16},{16,12},{20,24},{24,20},{5,9},{9,5},{13,17},{1... | collective-permute-start | bytes 104 | tf_op jit(solution)/shard_map/ppermute | solution.py:436
  63.8 33.3 %collective-permute-start.13 = (f32[4,256,256]{2,1,0:T(8,128)S(1)}, f32[4,256,256]{2,1,0:T(8,128)S(1)}, u32[]{:S(2)}, u32[]{:S(2)}) collective-permute-start(f32[4,256,256]{2,1,0:T(8,128)S(1)} %get-tuple-element.32), channel_id=1, source_target_pairs={{4,8},{8,4},{12,16},{16,12},{20,24},{24,20},{5,9},{9,5},{13,17},{1... | collective-permute-start | bytes 3145736 | tf_op jit(solution)/shard_map/ppermute | solution.py:436
  67.9 41.9 %collective-permute-start.15 = (f32[3,256,256]{2,1,0:T(8,128)S(1)}, f32[3,256,256]{2,1,0:T(8,128)S(1)}, u32[]{:S(2)}, u32[]{:S(2)}) collective-permute-start(f32[3,256,256]{2,1,0:T(8,128)S(1)} %get-tuple-element.38), channel_id=1, source_target_pairs={{0,8},{4,12},{8,0},{12,4},{16,24},{20,28},{24,16},{28,20},{1,9},{5... | collective-permute-start | bytes 2359304 | tf_op jit(solution)/shard_map/ppermute | solution.py:436
  68.0 41.8 %collective-permute-start.17 = (f32[3,256,256]{2,1,0:T(8,128)S(1)}, f32[3,256,256]{2,1,0:T(8,128)S(1)}, u32[]{:S(2)}, u32[]{:S(2)}) collective-permute-start(f32[3,256,256]{2,1,0:T(8,128)S(1)} %get-tuple-element.40), channel_id=1, source_target_pairs={{8,16},{12,20},{16,8},{20,12},{9,17},{13,21},{17,9},{21,13},{10,18... | collective-permute-start | bytes 2359304 | tf_op jit(solution)/shard_map/ppermute | solution.py:436
  74.5 2.6 %collective-permute-start.10 = (f32[1,256,256]{2,1,0:T(8,128)S(1)}, f32[1,256,256]{2,1,0:T(8,128)S(1)}, u32[]{:S(2)}, u32[]{:S(2)}) collective-permute-start(f32[1,256,256]{2,1,0:T(8,128)S(1)} %get-tuple-element.27), channel_id=1, source_target_pairs={{0,1},{1,0},{2,3},{3,2},{4,5},{5,4},{6,7},{7,6},{8,9},{9,8},{10,11... | collective-permute-start | bytes 786440 | tf_op jit(solution)/shard_map/ppermute | solution.py:436
  74.6 7.7 %collective-permute-start.11 = (f32[1,256,256]{2,1,0:T(8,128)S(1)}, f32[1,256,256]{2,1,0:T(8,128)S(1)}, u32[]{:S(2)}, u32[]{:S(2)}) collective-permute-start(f32[1,256,256]{2,1,0:T(8,128)S(1)} %get-tuple-element.28), channel_id=1, source_target_pairs={{1,2},{2,1},{5,6},{6,5},{9,10},{10,9},{13,14},{14,13},{17,18},{18,... | collective-permute-start | bytes 786440 | tf_op jit(solution)/shard_map/ppermute | solution.py:436
  77.2 29.5 %collective-permute-start.14 = (f32[1,256,256]{2,1,0:T(8,128)S(1)}, f32[1,256,256]{2,1,0:T(8,128)S(1)}, u32[]{:S(2)}, u32[]{:S(2)}) collective-permute-start(f32[1,256,256]{2,1,0:T(8,128)S(1)} %get-tuple-element.37), channel_id=1, source_target_pairs={{0,8},{4,12},{8,0},{12,4},{16,24},{20,28},{24,16},{28,20},{1,9},{5... | collective-permute-start | bytes 786440 | tf_op jit(solution)/shard_map/ppermute | solution.py:436
  82.3 27.5 %collective-permute-start.16 = (f32[1,256,256]{2,1,0:T(8,128)S(1)}, f32[1,256,256]{2,1,0:T(8,128)S(1)}, u32[]{:S(2)}, u32[]{:S(2)}) collective-permute-start(f32[1,256,256]{2,1,0:T(8,128)S(1)} %get-tuple-element.39), channel_id=1, source_target_pairs={{8,16},{12,20},{16,8},{20,12},{9,17},{13,21},{17,9},{21,13},{10,18... | collective-permute-start | bytes 786440 | tf_op jit(solution)/shard_map/ppermute | solution.py:436

commit v4 on v3

--- a/solution.py
+++ b/solution.py
@@ -71,7 +71,9 @@
 
 def pack_kernel(places, pieces, stride, table, dual, *refs):
     count = len(places)
-    outs, (held, sems) = refs[: count * len(pieces)], refs[count * len(pieces) :]
+    held, sems = refs[-2:]
+    refs = list(refs[:-2])
+    outs = [[refs.pop(0) for _ in some] for some in pieces]
     depth, rows = dual.shape[1:3]
     moves = []
     for j, place in enumerate(places):
@@ -97,8 +99,8 @@
             y = pl.multiple_of(step * STEP, STEP)
             for z in range(depth):
                 for half in range(2):
-                    piece, within = piece_of(pieces, z)
-                    outs[j * len(pieces) + piece][within, pl.ds(y, STEP), pl.ds(half * LANES, LANES)] = held[
+                    piece, within = piece_of(pieces[j], z)
+                    outs[j][piece][within, pl.ds(y, STEP), pl.ds(half * LANES, LANES)] = held[
                         j, z, half, pl.ds(RIM + y + offset, STEP), :
                     ]
             return carry
@@ -112,8 +114,8 @@
     return pl.pallas_call(
         functools.partial(pack_kernel, places, pieces, stride),
         in_specs=[pl.BlockSpec(memory_space=pltpu.SMEM), pl.BlockSpec(memory_space=pltpu.HBM)],
-        out_specs=[pl.BlockSpec(memory_space=pltpu.VMEM)] * (count * len(pieces)),
-        out_shape=[jax.ShapeDtypeStruct((size, rows, columns), jnp.float32) for size in pieces] * count,
+        out_specs=[pl.BlockSpec(memory_space=pltpu.VMEM)] * sum(map(len, pieces)),
+        out_shape=[jax.ShapeDtypeStruct((size, rows, columns), jnp.float32) for some in pieces for size in some],
         scratch_shapes=[
             pltpu.VMEM((count, depth, 2, rows + 2 * RIM, LANES), jnp.float32),
             pltpu.SemaphoreType.DMA((2 * count,)),
@@ -364,52 +366,78 @@
     )(*images)
 
 
-def settle_kernel(count, pieces, last, total, *refs):
+def settle_kernel(terms, slices, kept, total, *refs):
     refs = list(refs)
     take = lambda k: [refs.pop(0) for _ in range(k)]
-    duals, weights, gains = take(count * len(pieces)), take(count), take(count)
-    if last:
-        result, out, sems = refs
-    else:
-        (out,) = refs
-    depth, rows, _ = total.shape
+    duals = [take(len(starts)) for starts in terms]
+    weights, gains = take(len(terms)), take(len(terms))
+    finished = [z for z in slices if z not in kept]
+    if finished:
+        out, sems = refs[-2:]
+        del refs[-2:]
+        result = refs.pop()
+    rest = refs[-1] if kept else None
+    rows = total.shape[1]
     moves = []
-    for z in range(depth):
-        piece, within = piece_of(pieces, z)
+    for z in finished + list(kept):
+        here_terms = []
+        for k, starts in enumerate(terms):
+            for piece, start in enumerate(starts):
+                if start <= z < start + duals[k][piece].shape[0]:
+                    here_terms.append((duals[k][piece], z - start, weights[k], gains[k]))
+        place = kept.index(z) if z in kept else finished.index(z)
+        target = rest if z in kept else out
 
         def body(step, carry):
             here = pl.ds(pl.multiple_of(step * STEP, STEP), STEP)
             arriving = None
-            for i in range(count):
-                value = duals[i * len(pieces) + piece][within, here, :] + gains[i][z, here, :]
-                value = weights[i][z, here, :] * jnp.minimum(jnp.maximum(value, -dual_bound), dual_bound)
+            for dual, within, weight, gain in here_terms:
+                value = dual[within, here, :] + gain[z, here, :]
+                value = weight[z, here, :] * jnp.minimum(jnp.maximum(value, -dual_bound), dual_bound)
                 arriving = value if arriving is None else arriving + value
-            out[z, here, :] = total[z, here, :] - flow * arriving
+            target[place, here, :] = total[z - slices[0], here, :] - flow * arriving
             return carry
 
         lax.fori_loop(0, rows // STEP, body, 0)
-        if last:
-            moves.append(pltpu.make_async_copy(out.at[z], result.at[z], sems.at[z]))
+        if z not in kept:
+            moves.append(pltpu.make_async_copy(out.at[place], result.at[z], sems.at[place]))
             moves[-1].start()
     for m in moves:
         m.wait()
 
 
-def settle(total, duals, pieces, weights, gains, last):
-    count = len(weights)
-    depth = total.shape[0]
-    vmem_spec = pl.BlockSpec(memory_space=pltpu.VMEM)
+def settle(total, terms, slices, kept, depth, result=None):
+    vmem_spec, any_spec = pl.BlockSpec(memory_space=pltpu.VMEM), pl.BlockSpec(memory_space=pl.ANY)
+    rows, columns = total.shape[1:]
+    f32 = jnp.float32
+    operands = [total, *(d for t in terms for d in t[0]), *(t[2] for t in terms), *(t[3] for t in terms)]
+    specs = [vmem_spec] * len(operands)
+    finished = len(slices) - len(kept)
+    aliases = {}
+    if result is not None:
+        aliases = {len(operands): 0}
+        operands.append(result)
+        specs.append(any_spec)
+    shapes, out_specs, scratch = [], [], []
+    if kept:
+        shapes.append(jax.ShapeDtypeStruct((len(kept), rows, columns), f32))
+        out_specs.append(vmem_spec)
+    if finished:
+        shapes.append(jax.ShapeDtypeStruct((depth, rows, columns), f32))
+        out_specs.append(any_spec)
+        scratch = [pltpu.VMEM((finished, rows, columns), f32), pltpu.SemaphoreType.DMA((finished,))]
     return pl.pallas_call(
-        functools.partial(settle_kernel, count, pieces, last),
-        in_specs=[vmem_spec] * (1 + len(duals) + 2 * count),
-        out_specs=pl.BlockSpec(memory_space=pl.ANY) if last else vmem_spec,
-        out_shape=jax.ShapeDtypeStruct(total.shape, jnp.float32),
-        scratch_shapes=[pltpu.VMEM(total.shape, jnp.float32), pltpu.SemaphoreType.DMA((depth,))] if last else [],
+        functools.partial(settle_kernel, tuple(t[1] for t in terms), slices, kept),
+        in_specs=specs,
+        out_specs=out_specs,
+        out_shape=shapes,
+        input_output_aliases=aliases,
+        scratch_shapes=scratch,
         compiler_params=pltpu.CompilerParams(vmem_limit_bytes=10 << 20),
         cost_estimate=pl.CostEstimate(
-            flops=5 * count * total.size, bytes_accessed=4 * (2 + 3 * count) * total.size, transcendentals=0
+            flops=5 * len(terms) * total.size, bytes_accessed=4 * (2 + 3 * len(terms)) * total.size, transcendentals=0
         ),
-    )(total, *duals, *weights, *gains)
+    )(*operands)
 
 
 def shards(volume, prior_image, dual_pairs, pair_cycle, pair_offset):
@@ -449,19 +477,18 @@
     wide_near_table = send(table, wide_swap)
     wide_far_table = send(table, wide_cross)
     depth = image.shape[0]
-    lead = max(depth // 4, 1)
-    pieces = (lead, depth - lead)
-    near_dual, far_dual = pack((0, 1), (depth,), stride, table, dual)
+    part = max(depth // 4, 1)
+    near_dual, far_dual = pack((0, 1), ((depth,),) * 2, stride, table, dual)
     near_dual = send(near_dual, swap)
     far_dual = send(far_dual, cross)
-    wide = list(pack((2, 3), pieces, stride, table, dual))
-    wide[0] = send(wide[0], wide_swap)
-    wide[2] = send(wide[2], wide_cross)
+    lead, rest, main, last = pack((2, 3), ((part, depth - part), (depth - part, part)), stride, table, dual)
+    lead = send(lead, wide_swap)
     far_image = send(near_image, relay)
 
     within, across = halos((image, near_image, wide_near_image, wide_far_image))
-    wide[1] = send(wide[1], wide_swap)
-    wide[3] = send(wide[3], wide_cross)
+    main = send(main, wide_cross)
+    rest = send(rest, wide_swap)
+    last = send(last, wide_cross)
     fresh, total, w0, w2, w3, g0, g2, g3 = pairs(
         ((0, 1), (2, 2), (3, 3)), stride, table, (near_table, wide_near_table, wide_far_table),
         image, dual, prior_image[0],
@@ -472,8 +499,14 @@
         ((1, 0),), stride, table, (far_table,), image, dual, total,
         (far_image,), (far_within,), (far_across,), (within, across), fresh,
     )
-    total = settle(total, (near_dual, far_dual), (depth,), (w0, w1), (g0, g1), False)
-    volume_next = settle(total, wide, pieces, (w2, w3), (g2, g3), True)
+    every_slice, late = tuple(range(depth)), tuple(range(depth - part, depth))
+    (total,) = settle(
+        total, (((near_dual,), (0,), w0, g0), ((far_dual,), (0,), w1, g1)), every_slice, every_slice, depth
+    )
+    total, volume_next = settle(
+        total, (((lead, rest), (0, part), w2, g2), ((main,), (0,), w3, g3)), every_slice, late, depth
+    )
+    (volume_next,) = settle(total, (((last,), (depth - part,), w3, g3),), late, (), depth, volume_next)
     return (volume_next[None], fresh[None])
 
 

time: 112 us -> 113 us (level); the launches traced: 111 us -> 111 us
    ppermute x18, waiting for transfers between devices: 57.3 us -> 56.2 us  [send(): return lax.ppermute(x, axis, pairs_)]
    pallas_call x2 -> x3, Pallas kernels: 2.07 us -> 2.66 us  [settle(): pl.pallas_call(functools.partial(settle_kernel, tuple((t[1] for t in term...]
  transfers between devices with their start and end apart: 18 -> 18, of which waited for: 8 -> 9; matrix products, arithmetic and copies ran while one was open for 1% -> 1% of each run, Pallas kernels for 16% -> 18%
where the time goes in v4:
time: 113 us; the launch traced here: 111 us
  waiting for transfers between devices  56.2 us (50%)
  starting transfers between devices  32.5 us (29%)
  Pallas kernels  20.3 us (18%)
    ppermute x18, waiting for transfers between devices, send(): return lax.ppermute(x, axis, pairs_)  56.2 us
    ppermute x18, starting transfers between devices, send(): return lax.ppermute(x, axis, pairs_)  32.5 us
    pallas_call x2, Pallas kernels, pairs(): pl.pallas_call(functools.partial(pair_kernel, places, first, stride), in_...  12.8 us
    pallas_call x2, Pallas kernels, pack(): pl.pallas_call(functools.partial(pack_kernel, places, pieces, stride), in...  4.5 us
    pallas_call x3, Pallas kernels, settle(): pl.pallas_call(functools.partial(settle_kernel, tuple((t[1] for t in term...  2.66 us
  transfers between devices with their start and end apart: 18, of which 9 were waited for; matrix products, arithmetic and copies ran while one was open for 1% of the time, Pallas kernels for 18%

profile of v4, /device:TPU:10, one launch (start us, length us, event | category | flops | bytes accessed | tf_op | source)
XLA Modules:
  0.0 110.7 jit_solution(6749320768575871740)
XLA Ops:
  0.6 1.6 %collective-permute-start.4 = (f32[4,256,256]{2,1,0:T(8,128)}, f32[4,256,256]{2,1,0:T(8,128)S(1)}, u32[]{:S(2)}, u32[]{:S(2)}) collective-permute-start(f32[4,256,256]{2,1,0:T(8,128)} %bitcast.11), channel_id=1, source_target_pairs={{0,4},{4,0},{8,12},{12,8},{16,20},{20,16},{24,28},{28,24},{1,5},{5... | collective-permute-start | bytes 3145736 | tf_op jit(solution)/shard_map/ppermute | solution.py:464
  2.2 0.4 collective-permute-start.5
  2.7 4.6 %collective-permute-start.6 = (f32[4,256,256]{2,1,0:T(8,128)}, f32[4,256,256]{2,1,0:T(8,128)S(1)}, u32[]{:S(2)}, u32[]{:S(2)}) collective-permute-start(f32[4,256,256]{2,1,0:T(8,128)} %bitcast.13), channel_id=1, source_target_pairs={{8,16},{12,20},{16,8},{20,12},{9,17},{13,21},{17,9},{21,13},{10,18... | collective-permute-start | bytes 3145736 | tf_op jit(solution)/shard_map/ppermute | solution.py:464
  7.3 0.7 pad_add_fusion.table
  8.0 2.2 %shard_map.72 = (f32[4,256,256]{2,1,0:T(8,128)S(1)}, f32[4,256,256]{2,1,0:T(8,128)S(1)}) custom-call(s32[8]{0:T(128)S(1)} %pad_add_fusion.table, f32[4,4,256,256]{3,2,1,0:T(8,128)} %bitcast.7), custom_call_target="tpu_custom_call" | custom-call | bytes 4194304 | tf_op jit(solution)/shard_map/pallas_call | solution.py:114
  10.3 0.6 collective-permute-start.12
  10.9 16.1 %collective-permute-done.4.refs_1_.refs_6_ = f32[4,256,256]{2,1,0:T(8,128)S(1)} collective-permute-done((f32[4,256,256]{2,1,0:T(8,128)}, f32[4,256,256]{2,1,0:T(8,128)S(1)}, u32[]{:S(2)}, u32[]{:S(2)}) %collective-permute-start.4) | collective-permute-done | bytes 1048608 | tf_op jit(solution)/shard_map/ppermute | solution.py:464
  26.9 3.5 %collective-permute-start.9 = (f32[4,256,256]{2,1,0:T(8,128)S(1)}, f32[4,256,256]{2,1,0:T(8,128)S(1)}, u32[]{:S(2)}, u32[]{:S(2)}) collective-permute-start(f32[4,256,256]{2,1,0:T(8,128)S(1)} %collective-permute-done.4.refs_1_.refs_6_), channel_id=1, source_target_pairs={{0,8},{8,16},{12,4},{16,24},{20,12},{28,20},{1,9},{9,17},{13,5},{1... | collective-permute-start | bytes 3145736 | tf_op jit(solution)/shard_map/ppermute | solution.py:464
  30.5 0.3 shard_map.68
  30.8 2.5 %collective-permute-start.8 = (f32[4,256,256]{2,1,0:T(8,128)S(1)}, f32[4,256,256]{2,1,0:T(8,128)S(1)}, u32[]{:S(2)}, u32[]{:S(2)}) collective-permute-start(f32[4,256,256]{2,1,0:T(8,128)S(1)} %get-tuple-element.27), channel_id=1, source_target_pairs={{1,2},{2,1},{5,6},{6,5},{9,10},{10,9},{13,14},{14,13},{17,18},{18,... | collective-permute-start | bytes 3145736 | tf_op jit(solution)/shard_map/ppermute | solution.py:464
  33.3 0.5 collective-permute-start.1
  33.8 14.6 %collective-permute-done.1.refs_0_ = s32[8]{0:T(128)S(1)} collective-permute-done((s32[8]{0:T(128)S(1)}, s32[8]{0:T(128)S(1)}, u32[]{:S(2)}, u32[]{:S(2)}) %collective-permute-start.1) | collective-permute-done | bytes 64 | tf_op jit(solution)/shard_map/ppermute | solution.py:464
  48.4 0.4 collective-permute-start.2
  48.8 3.1 %collective-permute-done.2.refs_1_ = s32[8]{0:T(128)S(1)} collective-permute-done((s32[8]{0:T(128)S(1)}, s32[8]{0:T(128)S(1)}, u32[]{:S(2)}, u32[]{:S(2)}) %collective-permute-start.2) | collective-permute-done | bytes 64 | tf_op jit(solution)/shard_map/ppermute | solution.py:464
  52.0 3.5 %collective-permute-start.3 = (s32[8]{0:T(128)S(1)}, s32[8]{0:T(128)S(1)}, u32[]{:S(2)}, u32[]{:S(2)}) collective-permute-start(s32[8]{0:T(128)S(1)} %pad_add_fusion.table), channel_id=1, source_target_pairs={{8,16},{12,20},{16,8},{20,12},{9,17},{13,21},{17,9},{21,13},{10,18... | collective-permute-start | bytes 104 | tf_op jit(solution)/shard_map/ppermute | solution.py:464
  55.4 2.0 %collective-permute-done.3.refs_2_ = s32[8]{0:T(128)S(1)} collective-permute-done((s32[8]{0:T(128)S(1)}, s32[8]{0:T(128)S(1)}, u32[]{:S(2)}, u32[]{:S(2)}) %collective-permute-start.3) | collective-permute-done | bytes 64 | tf_op jit(solution)/shard_map/ppermute | solution.py:464
  57.4 1.9 %collective-permute-start = (s32[8]{0:T(128)S(1)}, s32[8]{0:T(128)S(1)}, u32[]{:S(2)}, u32[]{:S(2)}) collective-permute-start(s32[8]{0:T(128)S(1)} %pad_add_fusion.table), channel_id=1, source_target_pairs={{4,8},{8,4},{12,16},{16,12},{20,24},{24,20},{5,9},{9,5},{13,17},{1... | collective-permute-start | bytes 104 | tf_op jit(solution)/shard_map/ppermute | solution.py:464
  59.3 4.4 %collective-permute-done.refs_0_ = s32[8]{0:T(128)S(1)} collective-permute-done((s32[8]{0:T(128)S(1)}, s32[8]{0:T(128)S(1)}, u32[]{:S(2)}, u32[]{:S(2)}) %collective-permute-start) | collective-permute-done | bytes 64 | tf_op jit(solution)/shard_map/ppermute | solution.py:464
  63.8 1.9 %collective-permute-start.13 = (f32[4,256,256]{2,1,0:T(8,128)S(1)}, f32[4,256,256]{2,1,0:T(8,128)S(1)}, u32[]{:S(2)}, u32[]{:S(2)}) collective-permute-start(f32[4,256,256]{2,1,0:T(8,128)S(1)} %get-tuple-element.34), channel_id=1, source_target_pairs={{4,8},{8,4},{12,16},{16,12},{20,24},{24,20},{5,9},{9,5},{13,17},{1... | collective-permute-start | bytes 3145736 | tf_op jit(solution)/shard_map/ppermute | solution.py:464
  65.7 2.3 %shard_map.74 = (f32[1,256,256]{2,1,0:T(8,128)S(1)}, f32[3,256,256]{2,1,0:T(8,128)S(1)}, f32[3,256,256]{2,1,0:T(8,128)S(1)}, f32[1,256,256]{2,1,0:T(8,128)S(1)}) custom-call(s32[8]{0:T(128)S(1)} %pad_add_fusion.table, f32[4,4,256,256]{3,2,1,0:T(8,128)} %bitcast.8), custom_call_target="tpu_custom_call" | custom-call | bytes 4194304 | tf_op jit(solution)/shard_map/pallas_call | solution.py:114
  68.0 6.4 %collective-permute-start.16 = (f32[3,256,256]{2,1,0:T(8,128)S(1)}, f32[3,256,256]{2,1,0:T(8,128)S(1)}, u32[]{:S(2)}, u32[]{:S(2)}) collective-permute-start(f32[3,256,256]{2,1,0:T(8,128)S(1)} %get-tuple-element.41), channel_id=1, source_target_pairs={{8,16},{12,20},{16,8},{20,12},{9,17},{13,21},{17,9},{21,13},{10,18... | collective-permute-start | bytes 2359304 | tf_op jit(solution)/shard_map/ppermute | solution.py:464
  74.6 2.5 %collective-permute-start.11 = (f32[1,256,256]{2,1,0:T(8,128)S(1)}, f32[1,256,256]{2,1,0:T(8,128)S(1)}, u32[]{:S(2)}, u32[]{:S(2)}) collective-permute-start(f32[1,256,256]{2,1,0:T(8,128)S(1)} %get-tuple-element.30), channel_id=1, source_target_pairs={{1,2},{2,1},{5,6},{6,5},{9,10},{10,9},{13,14},{14,13},{17,18},{18,... | collective-permute-start | bytes 786440 | tf_op jit(solution)/shard_map/ppermute | solution.py:464
  77.3 5.1 %collective-permute-done.11.refs_6_ = f32[1,256,256]{2,1,0:T(8,128)S(1)} collective-permute-done((f32[1,256,256]{2,1,0:T(8,128)S(1)}, f32[1,256,256]{2,1,0:T(8,128)S(1)}, u32[]{:S(2)}, u32[]{:S(2)}) %collective-permute-start.11) | collective-permute-done | bytes 262176 | tf_op jit(solution)/shard_map/ppermute | solution.py:464
  82.3 1.9 %collective-permute-start.17 = (f32[1,256,256]{2,1,0:T(8,128)S(1)}, f32[1,256,256]{2,1,0:T(8,128)S(1)}, u32[]{:S(2)}, u32[]{:S(2)}) collective-permute-start(f32[1,256,256]{2,1,0:T(8,128)S(1)} %get-tuple-element.47), channel_id=1, source_target_pairs={{8,16},{12,20},{16,8},{20,12},{9,17},{13,21},{17,9},{21,13},{10,18... | collective-permute-start | bytes 786440 | tf_op jit(solution)/shard_map/ppermute | solution.py:464
  84.3 8.9 %shard_map.69 = (f32[4,4,256,256]{3,2,1,0:T(8,128)}, f32[4,256,256]{2,1,0:T(8,128)S(1)}, f32[4,256,256]{2,1,0:T(8,128)S(1)}, f32[4,256,256]{2,1,0:T(8,128)S(1)},...) custom-call(s32[8]{0:T(128)S(1)} %pad_add_fusion.table, ...), custom_call_target="tpu_custom_call" | custom-call | flops 47185920 | bytes 25165824 | tf_op jit(solution)/shard_map/pallas_call | solution.py:314
  93.2 3.9 %shard_map.71 = (f32[4,4,256,256]{3,2,1,0:T(8,128)}, f32[4,256,256]{2,1,0:T(8,128)S(1)}, f32[4,256,256]{2,1,0:T(8,128)S(1)}, f32[4,256,256]{2,1,0:T(8,128)S(1)}) custom-call(s32[8]{0:T(128)S(1)} %pad_add_fusion.table, s32[8]{0:T(128)S(1)} %collective-permute-done.refs_0_, f32[4,256,256]{2,1,0:T(8,128)S(1)} %bitcast.16, ...), custom_call_target="tpu_custom_call", output_to_operand_aliasing={{0}: (10, {})} | custom-call | flops 15728640 | bytes 10485760 | tf_op jit(solution)/shard_map/pallas_call | solution.py:314
  97.1 0.6 shard_map.73.total
  97.7 9.0 %collective-permute-done.14.refs_0_ = f32[1,256,256]{2,1,0:T(8,128)S(1)} collective-permute-done((f32[1,256,256]{2,1,0:T(8,128)S(1)}, f32[1,256,256]{2,1,0:T(8,128)S(1)}, u32[]{:S(2)}, u32[]{:S(2)}) %collective-permute-start.14) | collective-permute-done | bytes 262176 | tf_op jit(solution)/shard_map/ppermute | solution.py:464
  106.7 0.3 collective-permute-done.16.refs_2_
  107.1 1.2 %shard_map.75 = (f32[1,256,256]{2,1,0:T(8,128)S(1)}, f32[4,256,256]{2,1,0:T(8,128)}) custom-call(f32[4,256,256]{2,1,0:T(8,128)S(1)} %shard_map.73.total, f32[1,256,256]{2,1,0:T(8,128)S(1)} %collective-permute-done.14.refs_0_, f32[3,256,256]{2,1,0:T(8,128)S(1)} %collective-permute-done.15.refs_1_, f32[3,256,256]{2,1,0:T(8,128)S(1)} %collective-permute-done.16.refs_2_, ...), custom_call_target="tpu_custom_call" | custom-call | flops 2621440 | bytes 8388608 | tf_op jit(solution)/shard_map/pallas_call | solution.py:429
  108.3 1.6 %collective-permute-done.17.refs_0_ = f32[1,256,256]{2,1,0:T(8,128)S(1)} collective-permute-done((f32[1,256,256]{2,1,0:T(8,128)S(1)}, f32[1,256,256]{2,1,0:T(8,128)S(1)}, u32[]{:S(2)}, u32[]{:S(2)}) %collective-permute-start.17) | collective-permute-done | bytes 262176 | tf_op jit(solution)/shard_map/ppermute | solution.py:464
  109.9 0.8 shard_map.76
  (20 shorter events, 0.4 us)
Async XLA Ops:
  0.6 29.8 %copy-start.1 = (f32[1,4,256,256]{3,2,1,0:T(8,128)S(1)}, f32[1,4,256,256]{3,2,1,0:T(8,128)}, u32[]{:S(2)}) copy-start(f32[1,4,256,256]{3,2,1,0:T(8,128)} %param.5) | copy-start | bytes 3145732
  0.6 26.3 %collective-permute-start.4 = (f32[4,256,256]{2,1,0:T(8,128)}, f32[4,256,256]{2,1,0:T(8,128)S(1)}, u32[]{:S(2)}, u32[]{:S(2)}) collective-permute-start(f32[4,256,256]{2,1,0:T(8,128)} %bitcast.11), channel_id=1, source_target_pairs={{0,4},{4,0},{8,12},{12,8},{16,20},{20,16},{24,28},{28,24},{1,5},{5... | collective-permute-start | bytes 3145736 | tf_op jit(solution)/shard_map/ppermute | solution.py:464
  2.2 28.2 %collective-permute-start.5 = (f32[4,256,256]{2,1,0:T(8,128)}, f32[4,256,256]{2,1,0:T(8,128)S(1)}, u32[]{:S(2)}, u32[]{:S(2)}) collective-permute-start(f32[4,256,256]{2,1,0:T(8,128)} %bitcast.12), channel_id=1, source_target_pairs={{0,8},{4,12},{8,0},{12,4},{16,24},{20,28},{24,16},{28,20},{1,9},{5... | collective-permute-start | bytes 3145736 | tf_op jit(solution)/shard_map/ppermute | solution.py:464
  2.7 27.8 %collective-permute-start.6 = (f32[4,256,256]{2,1,0:T(8,128)}, f32[4,256,256]{2,1,0:T(8,128)S(1)}, u32[]{:S(2)}, u32[]{:S(2)}) collective-permute-start(f32[4,256,256]{2,1,0:T(8,128)} %bitcast.13), channel_id=1, source_target_pairs={{8,16},{12,20},{16,8},{20,12},{9,17},{13,21},{17,9},{21,13},{10,18... | collective-permute-start | bytes 3145736 | tf_op jit(solution)/shard_map/ppermute | solution.py:464
  10.3 74.0 %copy-start = (f32[1,4,4,256,256]{4,3,2,1,0:T(8,128)S(1)}, f32[1,4,4,256,256]{4,3,2,1,0:T(8,128)}, u32[]{:S(2)}) copy-start(f32[1,4,4,256,256]{4,3,2,1,0:T(8,128)} %param.7) | copy-start | bytes 12582916
  10.3 74.0 %copy-start.2 = (f32[1,4,256,256]{3,2,1,0:T(8,128)S(1)}, f32[1,4,256,256]{3,2,1,0:T(8,128)}, u32[]{:S(2)}) copy-start(f32[1,4,256,256]{3,2,1,0:T(8,128)} %param.6) | copy-start | bytes 3145732
  10.3 57.6 %collective-permute-start.12 = (f32[4,256,256]{2,1,0:T(8,128)S(1)}, f32[4,256,256]{2,1,0:T(8,128)S(1)}, u32[]{:S(2)}, u32[]{:S(2)}) collective-permute-start(f32[4,256,256]{2,1,0:T(8,128)S(1)} %get-tuple-element.33), channel_id=1, source_target_pairs={{0,4},{4,0},{8,12},{12,8},{16,20},{20,16},{24,28},{28,24},{1,5},{5... | collective-permute-start | bytes 3145736 | tf_op jit(solution)/shard_map/ppermute | solution.py:464
  26.9 41.1 %collective-permute-start.9 = (f32[4,256,256]{2,1,0:T(8,128)S(1)}, f32[4,256,256]{2,1,0:T(8,128)S(1)}, u32[]{:S(2)}, u32[]{:S(2)}) collective-permute-start(f32[4,256,256]{2,1,0:T(8,128)S(1)} %collective-permute-done.4.refs_1_.refs_6_), channel_id=1, source_target_pairs={{0,8},{8,16},{12,4},{16,24},{20,12},{28,20},{1,9},{9,17},{13,5},{1... | collective-permute-start | bytes 3145736 | tf_op jit(solution)/shard_map/ppermute | solution.py:464
  30.7 43.8 %collective-permute-start.7 = (f32[4,256,256]{2,1,0:T(8,128)S(1)}, f32[4,256,256]{2,1,0:T(8,128)S(1)}, u32[]{:S(2)}, u32[]{:S(2)}) collective-permute-start(f32[4,256,256]{2,1,0:T(8,128)S(1)} %get-tuple-element.26), channel_id=1, source_target_pairs={{0,1},{1,0},{2,3},{3,2},{4,5},{5,4},{6,7},{7,6},{8,9},{9,8},{10,11... | collective-permute-start | bytes 3145736 | tf_op jit(solution)/shard_map/ppermute | solution.py:464
  30.8 43.8 %collective-permute-start.8 = (f32[4,256,256]{2,1,0:T(8,128)S(1)}, f32[4,256,256]{2,1,0:T(8,128)S(1)}, u32[]{:S(2)}, u32[]{:S(2)}) collective-permute-start(f32[4,256,256]{2,1,0:T(8,128)S(1)} %get-tuple-element.27), channel_id=1, source_target_pairs={{1,2},{2,1},{5,6},{6,5},{9,10},{10,9},{13,14},{14,13},{17,18},{18,... | collective-permute-start | bytes 3145736 | tf_op jit(solution)/shard_map/ppermute | solution.py:464
  33.3 15.0 %collective-permute-start.1 = (s32[8]{0:T(128)S(1)}, s32[8]{0:T(128)S(1)}, u32[]{:S(2)}, u32[]{:S(2)}) collective-permute-start(s32[8]{0:T(128)S(1)} %pad_add_fusion.table), channel_id=1, source_target_pairs={{0,4},{4,0},{8,12},{12,8},{16,20},{20,16},{24,28},{28,24},{1,5},{5... | collective-permute-start | bytes 104 | tf_op jit(solution)/shard_map/ppermute | solution.py:464
  48.4 3.6 %collective-permute-start.2 = (s32[8]{0:T(128)S(1)}, s32[8]{0:T(128)S(1)}, u32[]{:S(2)}, u32[]{:S(2)}) collective-permute-start(s32[8]{0:T(128)S(1)} %pad_add_fusion.table), channel_id=1, source_target_pairs={{0,8},{4,12},{8,0},{12,4},{16,24},{20,28},{24,16},{28,20},{1,9},{5... | collective-permute-start | bytes 104 | tf_op jit(solution)/shard_map/ppermute | solution.py:464
  52.0 5.5 %collective-permute-start.3 = (s32[8]{0:T(128)S(1)}, s32[8]{0:T(128)S(1)}, u32[]{:S(2)}, u32[]{:S(2)}) collective-permute-start(s32[8]{0:T(128)S(1)} %pad_add_fusion.table), channel_id=1, source_target_pairs={{8,16},{12,20},{16,8},{20,12},{9,17},{13,21},{17,9},{21,13},{10,18... | collective-permute-start | bytes 104 | tf_op jit(solution)/shard_map/ppermute | solution.py:464
  57.4 6.3 %collective-permute-start = (s32[8]{0:T(128)S(1)}, s32[8]{0:T(128)S(1)}, u32[]{:S(2)}, u32[]{:S(2)}) collective-permute-start(s32[8]{0:T(128)S(1)} %pad_add_fusion.table), channel_id=1, source_target_pairs={{4,8},{8,4},{12,16},{16,12},{20,24},{24,20},{5,9},{9,5},{13,17},{1... | collective-permute-start | bytes 104 | tf_op jit(solution)/shard_map/ppermute | solution.py:464
  63.8 33.3 %collective-permute-start.13 = (f32[4,256,256]{2,1,0:T(8,128)S(1)}, f32[4,256,256]{2,1,0:T(8,128)S(1)}, u32[]{:S(2)}, u32[]{:S(2)}) collective-permute-start(f32[4,256,256]{2,1,0:T(8,128)S(1)} %get-tuple-element.34), channel_id=1, source_target_pairs={{4,8},{8,4},{12,16},{16,12},{20,24},{24,20},{5,9},{9,5},{13,17},{1... | collective-permute-start | bytes 3145736 | tf_op jit(solution)/shard_map/ppermute | solution.py:464
  67.9 38.8 %collective-permute-start.15 = (f32[3,256,256]{2,1,0:T(8,128)S(1)}, f32[3,256,256]{2,1,0:T(8,128)S(1)}, u32[]{:S(2)}, u32[]{:S(2)}) collective-permute-start(f32[3,256,256]{2,1,0:T(8,128)S(1)} %get-tuple-element.40), channel_id=1, source_target_pairs={{0,8},{4,12},{8,0},{12,4},{16,24},{20,28},{24,16},{28,20},{1,9},{5... | collective-permute-start | bytes 2359304 | tf_op jit(solution)/shard_map/ppermute | solution.py:464
  68.0 39.0 %collective-permute-start.16 = (f32[3,256,256]{2,1,0:T(8,128)S(1)}, f32[3,256,256]{2,1,0:T(8,128)S(1)}, u32[]{:S(2)}, u32[]{:S(2)}) collective-permute-start(f32[3,256,256]{2,1,0:T(8,128)S(1)} %get-tuple-element.41), channel_id=1, source_target_pairs={{8,16},{12,20},{16,8},{20,12},{9,17},{13,21},{17,9},{21,13},{10,18... | collective-permute-start | bytes 2359304 | tf_op jit(solution)/shard_map/ppermute | solution.py:464
  74.5 2.6 %collective-permute-start.10 = (f32[1,256,256]{2,1,0:T(8,128)S(1)}, f32[1,256,256]{2,1,0:T(8,128)S(1)}, u32[]{:S(2)}, u32[]{:S(2)}) collective-permute-start(f32[1,256,256]{2,1,0:T(8,128)S(1)} %get-tuple-element.29), channel_id=1, source_target_pairs={{0,1},{1,0},{2,3},{3,2},{4,5},{5,4},{6,7},{7,6},{8,9},{9,8},{10,11... | collective-permute-start | bytes 786440 | tf_op jit(solution)/shard_map/ppermute | solution.py:464
  74.6 7.7 %collective-permute-start.11 = (f32[1,256,256]{2,1,0:T(8,128)S(1)}, f32[1,256,256]{2,1,0:T(8,128)S(1)}, u32[]{:S(2)}, u32[]{:S(2)}) collective-permute-start(f32[1,256,256]{2,1,0:T(8,128)S(1)} %get-tuple-element.30), channel_id=1, source_target_pairs={{1,2},{2,1},{5,6},{6,5},{9,10},{10,9},{13,14},{14,13},{17,18},{18,... | collective-permute-start | bytes 786440 | tf_op jit(solution)/shard_map/ppermute | solution.py:464
  77.2 29.5 %collective-permute-start.14 = (f32[1,256,256]{2,1,0:T(8,128)S(1)}, f32[1,256,256]{2,1,0:T(8,128)S(1)}, u32[]{:S(2)}, u32[]{:S(2)}) collective-permute-start(f32[1,256,256]{2,1,0:T(8,128)S(1)} %get-tuple-element.39), channel_id=1, source_target_pairs={{0,8},{4,12},{8,0},{12,4},{16,24},{20,28},{24,16},{28,20},{1,9},{5... | collective-permute-start | bytes 786440 | tf_op jit(solution)/shard_map/ppermute | solution.py:464
  82.3 27.5 %collective-permute-start.17 = (f32[1,256,256]{2,1,0:T(8,128)S(1)}, f32[1,256,256]{2,1,0:T(8,128)S(1)}, u32[]{:S(2)}, u32[]{:S(2)}) collective-permute-start(f32[1,256,256]{2,1,0:T(8,128)S(1)} %get-tuple-element.47), channel_id=1, source_target_pairs={{8,16},{12,20},{16,8},{20,12},{9,17},{13,21},{17,9},{21,13},{10,18... | collective-permute-start | bytes 786440 | tf_op jit(solution)/shard_map/ppermute | solution.py:464

commit v5 on v4

--- a/solution.py
+++ b/solution.py
@@ -22,6 +22,7 @@
 
 LANES = 128
 STEP = 32
+SHARE = 16
 PARTS = 2
 EDGE = 16
 RIM = 8
@@ -146,13 +147,14 @@
     )
 
 
-def pair_kernel(places, first, stride, table, *refs):
+def pair_kernel(places, parts, first, stride, table, *refs):
     count = len(places)
     refs = list(refs)
     take = lambda k: [refs.pop(0) for _ in range(k)]
     tables = take(count)
     image, dual, start = take(3)
-    partners, inner, outer, own_halos = take(count), take(count), take(count), take(2)
+    partners = [take(k) for k in parts]
+    inner, outer, own_halos = take(count), take(count), take(2)
     if not first:
         take(1)
     fresh_out, total = take(2)
@@ -168,10 +170,13 @@
         moves = []
         for half in range(2):
             lanes = pl.ds(half * LANES, LANES)
-            moves.append((partners[i].at[:, :, lanes], held.at[i, pl.ds(1, depth), half, pl.ds(EDGE, rows), :]))
+            top = EDGE
+            for part in partners[i]:
+                moves.append((part.at[:, :, lanes], held.at[i, pl.ds(1, depth), half, pl.ds(top, part.shape[1]), :]))
+                top += part.shape[1]
             moves.append((upper.at[stacked, :, lanes], held.at[i, 0, half, pl.ds(EDGE, rows), :]))
             moves.append((lower.at[stacked, :, lanes], held.at[i, depth + 1, half, pl.ds(EDGE, rows), :]))
-        return [pltpu.make_async_copy(a, b, sems.at[6 * i + j]) for j, (a, b) in enumerate(moves)]
+        return [pltpu.make_async_copy(a, b, sems.at[8 * i + j]) for j, (a, b) in enumerate(moves)]
 
     def start_all(uppers, lowers, own_upper, own_lower):
         for c in rim_copies(own_upper, own_lower):
@@ -182,8 +187,8 @@
 
     def rim_copies(upper, lower):
         return [
-            pltpu.make_async_copy(upper.at[0], rim.at[0], sems.at[6 * count]),
-            pltpu.make_async_copy(lower.at[0], rim.at[1], sems.at[6 * count + 1]),
+            pltpu.make_async_copy(upper.at[0], rim.at[0], sems.at[8 * count]),
+            pltpu.make_async_copy(lower.at[0], rim.at[1], sems.at[8 * count + 1]),
         ]
 
     pl.when(even)(lambda: start_all(outer, inner, own_halos[1], own_halos[0]))
@@ -303,8 +308,10 @@
     any_spec = pl.BlockSpec(memory_space=pl.ANY)
     vmem_spec = pl.BlockSpec(memory_space=pltpu.VMEM)
     smem = pl.BlockSpec(memory_space=pltpu.SMEM)
+    parts = tuple(map(len, partners))
+    partners = [part for partner in partners for part in partner]
     operands = [table, *tables, image, dual, start, *partners, *inner, *outer, *own_halos]
-    specs = [smem] * (1 + count) + [vmem_spec] * 3 + [any_spec] * (3 * count + 2)
+    specs = [smem] * (1 + count) + [vmem_spec] * 3 + [any_spec] * (len(partners) + 2 * count + 2)
     aliases = {}
     if not first:
         aliases = {len(operands): 0}
@@ -312,7 +319,7 @@
         specs.append(any_spec)
     cells = depth * rows * columns
     return pl.pallas_call(
-        functools.partial(pair_kernel, places, first, stride),
+        functools.partial(pair_kernel, places, parts, first, stride),
         in_specs=specs,
         out_specs=[any_spec] + [vmem_spec] * (1 + 2 * count),
         out_shape=[jax.ShapeDtypeStruct(dual.shape, f32)] + [block] * (1 + 2 * count),
@@ -323,7 +330,7 @@
             pltpu.VMEM((depth, 2, rows + 2 * RIM, LANES), f32),
             pltpu.VMEM((depth, 2, rows + 2 * RIM, LANES), f32),
             pltpu.VMEM((count, depth, rows, columns), f32),
-            pltpu.SemaphoreType.DMA((6 * count + 2,)),
+            pltpu.SemaphoreType.DMA((8 * count + 2,)),
             pltpu.SemaphoreType.DMA((PARTS * count,)),
         ],
         compiler_params=pltpu.CompilerParams(vmem_limit_bytes=20 << 20),
@@ -333,17 +340,22 @@
     )(*operands)
 
 
-def cut_kernel(*refs):
-    count = len(refs) - 3
-    images, (within, across, sems) = refs[:count], refs[count:]
-    last = images[0].shape[0] - 1
+def cut_kernel(parts, *refs):
+    refs = list(refs)
+    images = [[refs.pop(0) for _ in range(k)] for k in parts]
+    within, across, sems = refs
+    last = images[0][0].shape[0] - 1
     even = lax.axis_index("space") % 2 == 0
 
     def copies(inner, outer):
         moves = []
         for k, image in enumerate(images):
-            moves.append(pltpu.make_async_copy(image.at[inner], within.at[k], sems.at[2 * k]))
-            moves.append(pltpu.make_async_copy(image.at[outer], across.at[k], sems.at[2 * k + 1]))
+            top = 0
+            for part in image:
+                some = pl.ds(top, part.shape[1])
+                for source, target in ((part.at[inner], within), (part.at[outer], across)):
+                    moves.append(pltpu.make_async_copy(source, target.at[k, some, :], sems.at[len(moves)]))
+                top += part.shape[1]
         return moves
 
     pl.when(even)(lambda: [c.start() for c in copies(last, 0)] and None)
@@ -353,16 +365,47 @@
 
 
 def cut(images):
-    count = len(images)
-    block = (count,) + images[0].shape[1:]
+    parts = tuple(map(len, images))
+    rows = sum(part.shape[1] for part in images[0])
+    block = (len(images), rows, images[0][0].shape[2])
     return pl.pallas_call(
-        cut_kernel,
-        in_specs=[pl.BlockSpec(memory_space=pl.ANY)] * count,
+        functools.partial(cut_kernel, parts),
+        in_specs=[pl.BlockSpec(memory_space=pl.ANY)] * sum(parts),
         out_specs=[pl.BlockSpec(memory_space=pltpu.VMEM)] * 2,
         out_shape=[jax.ShapeDtypeStruct(block, jnp.float32)] * 2,
-        scratch_shapes=[pltpu.SemaphoreType.DMA((2 * count,))],
+        scratch_shapes=[pltpu.SemaphoreType.DMA((2 * sum(parts),))],
         compiler_params=pltpu.CompilerParams(vmem_limit_bytes=6 << 20),
-        cost_estimate=pl.CostEstimate(flops=0, bytes_accessed=16 * count * block[1] * block[2], transcendentals=0),
+        cost_estimate=pl.CostEstimate(flops=0, bytes_accessed=16 * len(images) * block[1] * block[2], transcendentals=0),
+    )(*(part for image in images for part in image))
+
+
+def rows_kernel(top, image, out, sem):
+    copy = pltpu.make_async_copy(image.at[:, pl.ds(top, out.shape[1]), :], out, sem)
+    copy.start()
+    copy.wait()
+
+
+def shift_kernel(stride, wide_near, wide_far, out, sem):
+    cycle = lax.axis_index("tm") // stride
+    same = cycle % 2 == cycle // 2 % 2
+    some = pl.ds(0, out.shape[1])
+    near_copy = pltpu.make_async_copy(wide_near.at[:, some, :], out, sem)
+    far_copy = pltpu.make_async_copy(wide_far.at[:, some, :], out, sem)
+    pl.when(same)(near_copy.start)
+    pl.when(jnp.logical_not(same))(far_copy.start)
+    near_copy.wait()
+
+
+def rows_of(kernel, images, size):
+    depth, _, columns = images[0].shape
+    return pl.pallas_call(
+        kernel,
+        in_specs=[pl.BlockSpec(memory_space=pl.ANY)] * len(images),
+        out_specs=pl.BlockSpec(memory_space=pltpu.VMEM),
+        out_shape=jax.ShapeDtypeStruct((depth, size, columns), jnp.float32),
+        scratch_shapes=[pltpu.SemaphoreType.DMA],
+        compiler_params=pltpu.CompilerParams(vmem_limit_bytes=4 << 20),
+        cost_estimate=pl.CostEstimate(flops=0, bytes_accessed=8 * depth * size * columns, transcendentals=0),
     )(*images)
 
 
@@ -478,21 +521,27 @@
     wide_far_table = send(table, wide_cross)
     depth = image.shape[0]
     part = max(depth // 4, 1)
-    near_dual, far_dual = pack((0, 1), ((depth,),) * 2, stride, table, dual)
-    near_dual = send(near_dual, swap)
+    near_lead, near_rest, far_dual = pack((0, 1), ((part, depth - part), (depth,)), stride, table, dual)
+    near_lead = send(near_lead, swap)
     far_dual = send(far_dual, cross)
     lead, rest, main, last = pack((2, 3), ((part, depth - part), (depth - part, part)), stride, table, dual)
     lead = send(lead, wide_swap)
-    far_image = send(near_image, relay)
-
-    within, across = halos((image, near_image, wide_near_image, wide_far_image))
+    rows = image.shape[1]
+    ahead = rows // SHARE // 8 * 8
+    relayed = rows_of(functools.partial(rows_kernel, ahead), (near_image,), rows - ahead)
+    relayed = send(relayed, relay)
+    within, across = halos(((image,), (near_image,), (wide_near_image,), (wide_far_image,)))
+    shifted = rows_of(functools.partial(shift_kernel, stride), (wide_near_image, wide_far_image), ahead)
+    shifted = send(shifted, swap)
+    far_image = (shifted, relayed)
     main = send(main, wide_cross)
+    near_rest = send(near_rest, swap)
     rest = send(rest, wide_swap)
     last = send(last, wide_cross)
     fresh, total, w0, w2, w3, g0, g2, g3 = pairs(
         ((0, 1), (2, 2), (3, 3)), stride, table, (near_table, wide_near_table, wide_far_table),
         image, dual, prior_image[0],
-        (near_image, wide_near_image, wide_far_image), (within,) * 3, (across,) * 3, (within, across),
+        ((near_image,), (wide_near_image,), (wide_far_image,)), (within,) * 3, (across,) * 3, (within, across),
     )
     far_within, far_across = halos((far_image,))
     fresh, total, w1, g1 = pairs(
@@ -501,7 +550,7 @@
     )
     every_slice, late = tuple(range(depth)), tuple(range(depth - part, depth))
     (total,) = settle(
-        total, (((near_dual,), (0,), w0, g0), ((far_dual,), (0,), w1, g1)), every_slice, every_slice, depth
+        total, (((near_lead, near_rest), (0, part), w0, g0), ((far_dual,), (0,), w1, g1)), every_slice, every_slice, depth
     )
     total, volume_next = settle(
         total, (((lead, rest), (0, part), w2, g2), ((main,), (0,), w3, g3)), every_slice, late, depth

time: 113 us -> 125 us (1.11)
  waiting for transfers between devices: 56.2 us -> 65.4 us
  starting transfers between devices: 32.5 us -> 35 us
    ppermute x18 -> x20, waiting for transfers between devices: 56.2 us -> 65.4 us  [send(): return lax.ppermute(x, axis, pairs_)]
    ppermute x18 -> x20, starting transfers between devices: 32.5 us -> 35 us  [send(): return lax.ppermute(x, axis, pairs_)]
    pallas_call x4 -> x6, Pallas kernels: 13.1 us -> 14.1 us  [the longest x2 12.9 us: pairs(): pl.pallas_call(functools.partial(pair_kernel, places, parts, first, strid...]
  transfers between devices with their start and end apart: 18 -> 20, of which waited for: 9 -> 9; matrix products, arithmetic and copies ran while one was open for 1% -> 1% of each run, Pallas kernels for 18% -> 17%
where the time goes in v5:
time: 125 us; the launch traced here: 123 us
  waiting for transfers between devices  65.4 us (52%)
  starting transfers between devices  35 us (28%)
  Pallas kernels  21.2 us (17%)
    ppermute x20, waiting for transfers between devices, send(): return lax.ppermute(x, axis, pairs_)  65.4 us
    ppermute x20, starting transfers between devices, send(): return lax.ppermute(x, axis, pairs_)  35 us
    pallas_call x2, Pallas kernels, pairs(): pl.pallas_call(functools.partial(pair_kernel, places, parts, first, strid...  12.9 us
    pallas_call x2, Pallas kernels, pack(): pl.pallas_call(functools.partial(pack_kernel, places, pieces, stride), in...  4.5 us
    pallas_call x3, Pallas kernels, settle(): pl.pallas_call(functools.partial(settle_kernel, tuple((t[1] for t in term...  2.68 us
  transfers between devices with their start and end apart: 20, of which 9 were waited for; matrix products, arithmetic and copies ran while one was open for 1% of the time, Pallas kernels for 17%

profile of v5, /device:TPU:10, one launch (start us, length us, event | category | flops | bytes accessed | tf_op | source)
XLA Modules:
  0.0 123.3 jit_solution(11069397319080099699)
XLA Ops:
  0.6 1.6 %collective-permute-start.4 = (f32[4,256,256]{2,1,0:T(8,128)}, f32[4,256,256]{2,1,0:T(8,128)S(1)}, u32[]{:S(2)}, u32[]{:S(2)}) collective-permute-start(f32[4,256,256]{2,1,0:T(8,128)} %bitcast.11), channel_id=1, source_target_pairs={{0,4},{4,0},{8,12},{12,8},{16,20},{20,16},{24,28},{28,24},{1,5},{5... | collective-permute-start | bytes 3145736 | tf_op jit(solution)/shard_map/ppermute | solution.py:507
  2.2 0.4 collective-permute-start.5
  2.7 4.6 %collective-permute-start.6 = (f32[4,256,256]{2,1,0:T(8,128)}, f32[4,256,256]{2,1,0:T(8,128)S(1)}, u32[]{:S(2)}, u32[]{:S(2)}) collective-permute-start(f32[4,256,256]{2,1,0:T(8,128)} %bitcast.13), channel_id=1, source_target_pairs={{8,16},{12,20},{16,8},{20,12},{9,17},{13,21},{17,9},{21,13},{10,18... | collective-permute-start | bytes 3145736 | tf_op jit(solution)/shard_map/ppermute | solution.py:507
  7.3 18.5 %collective-permute-done.4.refs_1_.refs_6_.image = f32[4,256,256]{2,1,0:T(8,128)S(1)} collective-permute-done((f32[4,256,256]{2,1,0:T(8,128)}, f32[4,256,256]{2,1,0:T(8,128)S(1)}, u32[]{:S(2)}, u32[]{:S(2)}) %collective-permute-start.4) | collective-permute-done | bytes 1048608 | tf_op jit(solution)/shard_map/ppermute | solution.py:507
  25.9 3.5 %collective-permute-start.10 = (f32[4,240,256]{2,1,0:T(8,128)S(1)}, f32[4,240,256]{2,1,0:T(8,128)S(1)}, u32[]{:S(2)}, u32[]{:S(2)}) collective-permute-start(f32[4,240,256]{2,1,0:T(8,128)S(1)} %shard_map.71), channel_id=1, source_target_pairs={{0,8},{8,16},{12,4},{16,24},{20,12},{28,20},{1,9},{9,17},{13,5},{1... | collective-permute-start | bytes 2949128 | tf_op jit(solution)/shard_map/ppermute | solution.py:507
  29.4 0.7 pad_add_fusion.table
  30.2 2.2 %shard_map.74 = (f32[1,256,256]{2,1,0:T(8,128)S(1)}, f32[3,256,256]{2,1,0:T(8,128)S(1)}, f32[4,256,256]{2,1,0:T(8,128)S(1)}) custom-call(s32[8]{0:T(128)S(1)} %pad_add_fusion.table, f32[4,4,256,256]{3,2,1,0:T(8,128)} %bitcast.7), custom_call_target="tpu_custom_call" | custom-call | bytes 4194304 | tf_op jit(solution)/shard_map/pallas_call | solution.py:115
  32.4 0.5 collective-permute-start.14
  33.3 2.5 %collective-permute-start.8 = (f32[4,256,256]{2,1,0:T(8,128)S(1)}, f32[4,256,256]{2,1,0:T(8,128)S(1)}, u32[]{:S(2)}, u32[]{:S(2)}) collective-permute-start(f32[4,256,256]{2,1,0:T(8,128)S(1)} %get-tuple-element.28), channel_id=1, source_target_pairs={{1,2},{2,1},{5,6},{6,5},{9,10},{10,9},{13,14},{14,13},{17,18},{18,... | collective-permute-start | bytes 3145736 | tf_op jit(solution)/shard_map/ppermute | solution.py:507
  35.8 1.7 %collective-permute-start.1 = (s32[8]{0:T(128)S(1)}, s32[8]{0:T(128)S(1)}, u32[]{:S(2)}, u32[]{:S(2)}) collective-permute-start(s32[8]{0:T(128)S(1)} %pad_add_fusion.table), channel_id=1, source_target_pairs={{0,4},{4,0},{8,12},{12,8},{16,20},{20,16},{24,28},{28,24},{1,5},{5... | collective-permute-start | bytes 104 | tf_op jit(solution)/shard_map/ppermute | solution.py:507
  37.5 13.2 %collective-permute-done.1.refs_0_ = s32[8]{0:T(128)S(1)} collective-permute-done((s32[8]{0:T(128)S(1)}, s32[8]{0:T(128)S(1)}, u32[]{:S(2)}, u32[]{:S(2)}) %collective-permute-start.1) | collective-permute-done | bytes 64 | tf_op jit(solution)/shard_map/ppermute | solution.py:507
  50.7 0.5 collective-permute-start.2
  51.2 3.1 %collective-permute-done.2.refs_1_ = s32[8]{0:T(128)S(1)} collective-permute-done((s32[8]{0:T(128)S(1)}, s32[8]{0:T(128)S(1)}, u32[]{:S(2)}, u32[]{:S(2)}) %collective-permute-start.2) | collective-permute-done | bytes 64 | tf_op jit(solution)/shard_map/ppermute | solution.py:507
  54.3 3.5 %collective-permute-start.3 = (s32[8]{0:T(128)S(1)}, s32[8]{0:T(128)S(1)}, u32[]{:S(2)}, u32[]{:S(2)}) collective-permute-start(s32[8]{0:T(128)S(1)} %pad_add_fusion.table), channel_id=1, source_target_pairs={{8,16},{12,20},{16,8},{20,12},{9,17},{13,21},{17,9},{21,13},{10,18... | collective-permute-start | bytes 104 | tf_op jit(solution)/shard_map/ppermute | solution.py:507
  57.8 2.0 %collective-permute-done.3.refs_2_ = s32[8]{0:T(128)S(1)} collective-permute-done((s32[8]{0:T(128)S(1)}, s32[8]{0:T(128)S(1)}, u32[]{:S(2)}, u32[]{:S(2)}) %collective-permute-start.3) | collective-permute-done | bytes 64 | tf_op jit(solution)/shard_map/ppermute | solution.py:507
  59.8 1.9 %collective-permute-start = (s32[8]{0:T(128)S(1)}, s32[8]{0:T(128)S(1)}, u32[]{:S(2)}, u32[]{:S(2)}) collective-permute-start(s32[8]{0:T(128)S(1)} %pad_add_fusion.table), channel_id=1, source_target_pairs={{4,8},{8,4},{12,16},{16,12},{20,24},{24,20},{5,9},{9,5},{13,17},{1... | collective-permute-start | bytes 104 | tf_op jit(solution)/shard_map/ppermute | solution.py:507
  61.7 4.4 %collective-permute-done.refs_0_ = s32[8]{0:T(128)S(1)} collective-permute-done((s32[8]{0:T(128)S(1)}, s32[8]{0:T(128)S(1)}, u32[]{:S(2)}, u32[]{:S(2)}) %collective-permute-start) | collective-permute-done | bytes 64 | tf_op jit(solution)/shard_map/ppermute | solution.py:507
  66.5 17.9 %collective-permute-done.13.refs_0_ = f32[1,256,256]{2,1,0:T(8,128)S(1)} collective-permute-done((f32[1,256,256]{2,1,0:T(8,128)S(1)}, f32[1,256,256]{2,1,0:T(8,128)S(1)}, u32[]{:S(2)}, u32[]{:S(2)}) %collective-permute-start.13) | collective-permute-done | bytes 262176 | tf_op jit(solution)/shard_map/ppermute | solution.py:507
  84.4 1.9 %collective-permute-start.15 = (f32[4,256,256]{2,1,0:T(8,128)S(1)}, f32[4,256,256]{2,1,0:T(8,128)S(1)}, u32[]{:S(2)}, u32[]{:S(2)}) collective-permute-start(f32[4,256,256]{2,1,0:T(8,128)S(1)} %get-tuple-element.36), channel_id=1, source_target_pairs={{4,8},{8,4},{12,16},{16,12},{20,24},{24,20},{5,9},{9,5},{13,17},{1... | collective-permute-start | bytes 3145736 | tf_op jit(solution)/shard_map/ppermute | solution.py:507
  86.4 3.1 %collective-permute-start.9 = (f32[4,16,256]{2,1,0:T(8,128)S(1)}, f32[4,16,256]{2,1,0:T(8,128)S(1)}, u32[]{:S(2)}, u32[]{:S(2)}) collective-permute-start(f32[4,16,256]{2,1,0:T(8,128)S(1)} %shard_map.70), channel_id=1, source_target_pairs={{0,4},{4,0},{8,12},{12,8},{16,20},{20,16},{24,28},{28,24},{1,5},{5... | collective-permute-start | bytes 196616 | tf_op jit(solution)/shard_map/ppermute | solution.py:507
  89.5 2.3 %shard_map.76 = (f32[1,256,256]{2,1,0:T(8,128)S(1)}, f32[3,256,256]{2,1,0:T(8,128)S(1)}, f32[3,256,256]{2,1,0:T(8,128)S(1)}, f32[1,256,256]{2,1,0:T(8,128)S(1)}) custom-call(s32[8]{0:T(128)S(1)} %pad_add_fusion.table, f32[4,4,256,256]{3,2,1,0:T(8,128)} %bitcast.8), custom_call_target="tpu_custom_call" | custom-call | bytes 4194304 | tf_op jit(solution)/shard_map/pallas_call | solution.py:115
  91.8 0.7 collective-permute-done.9.refs_0_.refs_4_
  92.5 4.3 %collective-permute-start.18 = (f32[3,256,256]{2,1,0:T(8,128)S(1)}, f32[3,256,256]{2,1,0:T(8,128)S(1)}, u32[]{:S(2)}, u32[]{:S(2)}) collective-permute-start(f32[3,256,256]{2,1,0:T(8,128)S(1)} %get-tuple-element.43), channel_id=1, source_target_pairs={{8,16},{12,20},{16,8},{20,12},{9,17},{13,21},{17,9},{21,13},{10,18... | collective-permute-start | bytes 2359304 | tf_op jit(solution)/shard_map/ppermute | solution.py:507
  96.8 0.7 shard_map.72
  97.6 2.5 %collective-permute-start.12 = (f32[1,256,256]{2,1,0:T(8,128)S(1)}, f32[1,256,256]{2,1,0:T(8,128)S(1)}, u32[]{:S(2)}, u32[]{:S(2)}) collective-permute-start(f32[1,256,256]{2,1,0:T(8,128)S(1)} %get-tuple-element.31), channel_id=1, source_target_pairs={{1,2},{2,1},{5,6},{6,5},{9,10},{10,9},{13,14},{14,13},{17,18},{18,... | collective-permute-start | bytes 786440 | tf_op jit(solution)/shard_map/ppermute | solution.py:507
  100.3 5.1 %collective-permute-done.12.refs_7_ = f32[1,256,256]{2,1,0:T(8,128)S(1)} collective-permute-done((f32[1,256,256]{2,1,0:T(8,128)S(1)}, f32[1,256,256]{2,1,0:T(8,128)S(1)}, u32[]{:S(2)}, u32[]{:S(2)}) %collective-permute-start.12) | collective-permute-done | bytes 262176 | tf_op jit(solution)/shard_map/ppermute | solution.py:507
  105.3 1.9 %collective-permute-start.19 = (f32[1,256,256]{2,1,0:T(8,128)S(1)}, f32[1,256,256]{2,1,0:T(8,128)S(1)}, u32[]{:S(2)}, u32[]{:S(2)}) collective-permute-start(f32[1,256,256]{2,1,0:T(8,128)S(1)} %get-tuple-element.49), channel_id=1, source_target_pairs={{8,16},{12,20},{16,8},{20,12},{9,17},{13,21},{17,9},{21,13},{10,18... | collective-permute-start | bytes 786440 | tf_op jit(solution)/shard_map/ppermute | solution.py:507
  107.3 9.0 %shard_map.69 = (f32[4,4,256,256]{3,2,1,0:T(8,128)}, f32[4,256,256]{2,1,0:T(8,128)S(1)}, f32[4,256,256]{2,1,0:T(8,128)S(1)}, f32[4,256,256]{2,1,0:T(8,128)S(1)},...) custom-call(s32[8]{0:T(128)S(1)} %pad_add_fusion.table, ...), custom_call_target="tpu_custom_call" | custom-call | flops 47185920 | bytes 25165824 | tf_op jit(solution)/shard_map/pallas_call | solution.py:321
  116.3 3.9 %shard_map.73 = (f32[4,4,256,256]{3,2,1,0:T(8,128)}, f32[4,256,256]{2,1,0:T(8,128)S(1)}, f32[4,256,256]{2,1,0:T(8,128)S(1)}, f32[4,256,256]{2,1,0:T(8,128)S(1)}) custom-call(s32[8]{0:T(128)S(1)} %pad_add_fusion.table, s32[8]{0:T(128)S(1)} %collective-permute-done.refs_0_, f32[4,256,256]{2,1,0:T(8,128)S(1)} %bitcast.16, ...), custom_call_target="tpu_custom_call", output_to_operand_aliasing={{0}: (11, {})} | custom-call | flops 15728640 | bytes 10485760 | tf_op jit(solution)/shard_map/pallas_call | solution.py:321
  120.2 0.6 shard_map.75.total
  120.8 1.2 shard_map.77
  122.5 0.8 shard_map.78
  (26 shorter events, 1.5 us)
Async XLA Ops:
  0.6 32.3 %copy-start.1 = (f32[1,4,256,256]{3,2,1,0:T(8,128)S(1)}, f32[1,4,256,256]{3,2,1,0:T(8,128)}, u32[]{:S(2)}) copy-start(f32[1,4,256,256]{3,2,1,0:T(8,128)} %param.5) | copy-start | bytes 3145732
  0.6 25.2 %collective-permute-start.4 = (f32[4,256,256]{2,1,0:T(8,128)}, f32[4,256,256]{2,1,0:T(8,128)S(1)}, u32[]{:S(2)}, u32[]{:S(2)}) collective-permute-start(f32[4,256,256]{2,1,0:T(8,128)} %bitcast.11), channel_id=1, source_target_pairs={{0,4},{4,0},{8,12},{12,8},{16,20},{20,16},{24,28},{28,24},{1,5},{5... | collective-permute-start | bytes 3145736 | tf_op jit(solution)/shard_map/ppermute | solution.py:507
  2.2 30.7 %collective-permute-start.5 = (f32[4,256,256]{2,1,0:T(8,128)}, f32[4,256,256]{2,1,0:T(8,128)S(1)}, u32[]{:S(2)}, u32[]{:S(2)}) collective-permute-start(f32[4,256,256]{2,1,0:T(8,128)} %bitcast.12), channel_id=1, source_target_pairs={{0,8},{4,12},{8,0},{12,4},{16,24},{20,28},{24,16},{28,20},{1,9},{5... | collective-permute-start | bytes 3145736 | tf_op jit(solution)/shard_map/ppermute | solution.py:507
  2.7 30.2 %collective-permute-start.6 = (f32[4,256,256]{2,1,0:T(8,128)}, f32[4,256,256]{2,1,0:T(8,128)S(1)}, u32[]{:S(2)}, u32[]{:S(2)}) collective-permute-start(f32[4,256,256]{2,1,0:T(8,128)} %bitcast.13), channel_id=1, source_target_pairs={{8,16},{12,20},{16,8},{20,12},{9,17},{13,21},{17,9},{21,13},{10,18... | collective-permute-start | bytes 3145736 | tf_op jit(solution)/shard_map/ppermute | solution.py:507
  25.9 66.5 %collective-permute-start.10 = (f32[4,240,256]{2,1,0:T(8,128)S(1)}, f32[4,240,256]{2,1,0:T(8,128)S(1)}, u32[]{:S(2)}, u32[]{:S(2)}) collective-permute-start(f32[4,240,256]{2,1,0:T(8,128)S(1)} %shard_map.71), channel_id=1, source_target_pairs={{0,8},{8,16},{12,4},{16,24},{20,12},{28,20},{1,9},{9,17},{13,5},{1... | collective-permute-start | bytes 2949128 | tf_op jit(solution)/shard_map/ppermute | solution.py:507
  32.4 54.0 %collective-permute-start.14 = (f32[3,256,256]{2,1,0:T(8,128)S(1)}, f32[3,256,256]{2,1,0:T(8,128)S(1)}, u32[]{:S(2)}, u32[]{:S(2)}) collective-permute-start(f32[3,256,256]{2,1,0:T(8,128)S(1)} %get-tuple-element.35), channel_id=1, source_target_pairs={{0,4},{4,0},{8,12},{12,8},{16,20},{20,16},{24,28},{28,24},{1,5},{5... | collective-permute-start | bytes 2359304 | tf_op jit(solution)/shard_map/ppermute | solution.py:507
  33.2 74.1 %copy-start = (f32[1,4,4,256,256]{4,3,2,1,0:T(8,128)S(1)}, f32[1,4,4,256,256]{4,3,2,1,0:T(8,128)}, u32[]{:S(2)}) copy-start(f32[1,4,4,256,256]{4,3,2,1,0:T(8,128)} %param.7) | copy-start | bytes 12582916
  33.2 74.1 %copy-start.2 = (f32[1,4,256,256]{3,2,1,0:T(8,128)S(1)}, f32[1,4,256,256]{3,2,1,0:T(8,128)}, u32[]{:S(2)}) copy-start(f32[1,4,256,256]{3,2,1,0:T(8,128)} %param.6) | copy-start | bytes 3145732
  33.2 64.3 %collective-permute-start.7 = (f32[4,256,256]{2,1,0:T(8,128)S(1)}, f32[4,256,256]{2,1,0:T(8,128)S(1)}, u32[]{:S(2)}, u32[]{:S(2)}) collective-permute-start(f32[4,256,256]{2,1,0:T(8,128)S(1)} %get-tuple-element.27), channel_id=1, source_target_pairs={{0,1},{1,0},{2,3},{3,2},{4,5},{5,4},{6,7},{7,6},{8,9},{9,8},{10,11... | collective-permute-start | bytes 3145736 | tf_op jit(solution)/shard_map/ppermute | solution.py:507
  33.3 64.3 %collective-permute-start.8 = (f32[4,256,256]{2,1,0:T(8,128)S(1)}, f32[4,256,256]{2,1,0:T(8,128)S(1)}, u32[]{:S(2)}, u32[]{:S(2)}) collective-permute-start(f32[4,256,256]{2,1,0:T(8,128)S(1)} %get-tuple-element.28), channel_id=1, source_target_pairs={{1,2},{2,1},{5,6},{6,5},{9,10},{10,9},{13,14},{14,13},{17,18},{18,... | collective-permute-start | bytes 3145736 | tf_op jit(solution)/shard_map/ppermute | solution.py:507
  35.8 14.9 %collective-permute-start.1 = (s32[8]{0:T(128)S(1)}, s32[8]{0:T(128)S(1)}, u32[]{:S(2)}, u32[]{:S(2)}) collective-permute-start(s32[8]{0:T(128)S(1)} %pad_add_fusion.table), channel_id=1, source_target_pairs={{0,4},{4,0},{8,12},{12,8},{16,20},{20,16},{24,28},{28,24},{1,5},{5... | collective-permute-start | bytes 104 | tf_op jit(solution)/shard_map/ppermute | solution.py:507
  50.7 3.6 %collective-permute-start.2 = (s32[8]{0:T(128)S(1)}, s32[8]{0:T(128)S(1)}, u32[]{:S(2)}, u32[]{:S(2)}) collective-permute-start(s32[8]{0:T(128)S(1)} %pad_add_fusion.table), channel_id=1, source_target_pairs={{0,8},{4,12},{8,0},{12,4},{16,24},{20,28},{24,16},{28,20},{1,9},{5... | collective-permute-start | bytes 104 | tf_op jit(solution)/shard_map/ppermute | solution.py:507
  54.3 5.5 %collective-permute-start.3 = (s32[8]{0:T(128)S(1)}, s32[8]{0:T(128)S(1)}, u32[]{:S(2)}, u32[]{:S(2)}) collective-permute-start(s32[8]{0:T(128)S(1)} %pad_add_fusion.table), channel_id=1, source_target_pairs={{8,16},{12,20},{16,8},{20,12},{9,17},{13,21},{17,9},{21,13},{10,18... | collective-permute-start | bytes 104 | tf_op jit(solution)/shard_map/ppermute | solution.py:507
  59.8 6.3 %collective-permute-start = (s32[8]{0:T(128)S(1)}, s32[8]{0:T(128)S(1)}, u32[]{:S(2)}, u32[]{:S(2)}) collective-permute-start(s32[8]{0:T(128)S(1)} %pad_add_fusion.table), channel_id=1, source_target_pairs={{4,8},{8,4},{12,16},{16,12},{20,24},{24,20},{5,9},{9,5},{13,17},{1... | collective-permute-start | bytes 104 | tf_op jit(solution)/shard_map/ppermute | solution.py:507
  66.1 18.3 %collective-permute-start.13 = (f32[1,256,256]{2,1,0:T(8,128)S(1)}, f32[1,256,256]{2,1,0:T(8,128)S(1)}, u32[]{:S(2)}, u32[]{:S(2)}) collective-permute-start(f32[1,256,256]{2,1,0:T(8,128)S(1)} %get-tuple-element.34), channel_id=1, source_target_pairs={{0,4},{4,0},{8,12},{12,8},{16,20},{20,16},{24,28},{28,24},{1,5},{5... | collective-permute-start | bytes 786440 | tf_op jit(solution)/shard_map/ppermute | solution.py:507
  84.4 35.7 %collective-permute-start.15 = (f32[4,256,256]{2,1,0:T(8,128)S(1)}, f32[4,256,256]{2,1,0:T(8,128)S(1)}, u32[]{:S(2)}, u32[]{:S(2)}) collective-permute-start(f32[4,256,256]{2,1,0:T(8,128)S(1)} %get-tuple-element.36), channel_id=1, source_target_pairs={{4,8},{8,4},{12,16},{16,12},{20,24},{24,20},{5,9},{9,5},{13,17},{1... | collective-permute-start | bytes 3145736 | tf_op jit(solution)/shard_map/ppermute | solution.py:507
  86.4 6.0 %collective-permute-start.9 = (f32[4,16,256]{2,1,0:T(8,128)S(1)}, f32[4,16,256]{2,1,0:T(8,128)S(1)}, u32[]{:S(2)}, u32[]{:S(2)}) collective-permute-start(f32[4,16,256]{2,1,0:T(8,128)S(1)} %shard_map.70), channel_id=1, source_target_pairs={{0,4},{4,0},{8,12},{12,8},{16,20},{20,16},{24,28},{28,24},{1,5},{5... | collective-permute-start | bytes 196616 | tf_op jit(solution)/shard_map/ppermute | solution.py:507
  92.5 28.4 %collective-permute-start.17 = (f32[3,256,256]{2,1,0:T(8,128)S(1)}, f32[3,256,256]{2,1,0:T(8,128)S(1)}, u32[]{:S(2)}, u32[]{:S(2)}) collective-permute-start(f32[3,256,256]{2,1,0:T(8,128)S(1)} %get-tuple-element.42), channel_id=1, source_target_pairs={{0,8},{4,12},{8,0},{12,4},{16,24},{20,28},{24,16},{28,20},{1,9},{5... | collective-permute-start | bytes 2359304 | tf_op jit(solution)/shard_map/ppermute | solution.py:507
  92.5 28.4 %collective-permute-start.18 = (f32[3,256,256]{2,1,0:T(8,128)S(1)}, f32[3,256,256]{2,1,0:T(8,128)S(1)}, u32[]{:S(2)}, u32[]{:S(2)}) collective-permute-start(f32[3,256,256]{2,1,0:T(8,128)S(1)} %get-tuple-element.43), channel_id=1, source_target_pairs={{8,16},{12,20},{16,8},{20,12},{9,17},{13,21},{17,9},{21,13},{10,18... | collective-permute-start | bytes 2359304 | tf_op jit(solution)/shard_map/ppermute | solution.py:507
  97.5 2.6 %collective-permute-start.11 = (f32[1,256,256]{2,1,0:T(8,128)S(1)}, f32[1,256,256]{2,1,0:T(8,128)S(1)}, u32[]{:S(2)}, u32[]{:S(2)}) collective-permute-start(f32[1,256,256]{2,1,0:T(8,128)S(1)} %get-tuple-element.30), channel_id=1, source_target_pairs={{0,1},{1,0},{2,3},{3,2},{4,5},{5,4},{6,7},{7,6},{8,9},{9,8},{10,11... | collective-permute-start | bytes 786440 | tf_op jit(solution)/shard_map/ppermute | solution.py:507
  97.6 7.7 %collective-permute-start.12 = (f32[1,256,256]{2,1,0:T(8,128)S(1)}, f32[1,256,256]{2,1,0:T(8,128)S(1)}, u32[]{:S(2)}, u32[]{:S(2)}) collective-permute-start(f32[1,256,256]{2,1,0:T(8,128)S(1)} %get-tuple-element.31), channel_id=1, source_target_pairs={{1,2},{2,1},{5,6},{6,5},{9,10},{10,9},{13,14},{14,13},{17,18},{18,... | collective-permute-start | bytes 786440 | tf_op jit(solution)/shard_map/ppermute | solution.py:507
  100.2 20.6 %collective-permute-start.16 = (f32[1,256,256]{2,1,0:T(8,128)S(1)}, f32[1,256,256]{2,1,0:T(8,128)S(1)}, u32[]{:S(2)}, u32[]{:S(2)}) collective-permute-start(f32[1,256,256]{2,1,0:T(8,128)S(1)} %get-tuple-element.41), channel_id=1, source_target_pairs={{0,8},{4,12},{8,0},{12,4},{16,24},{20,28},{24,16},{28,20},{1,9},{5... | collective-permute-start | bytes 786440 | tf_op jit(solution)/shard_map/ppermute | solution.py:507
  105.3 17.2 %collective-permute-start.19 = (f32[1,256,256]{2,1,0:T(8,128)S(1)}, f32[1,256,256]{2,1,0:T(8,128)S(1)}, u32[]{:S(2)}, u32[]{:S(2)}) collective-permute-start(f32[1,256,256]{2,1,0:T(8,128)S(1)} %get-tuple-element.49), channel_id=1, source_target_pairs={{8,16},{12,20},{16,8},{20,12},{9,17},{13,21},{17,9},{21,13},{10,18... | collective-permute-start | bytes 786440 | tf_op jit(solution)/shard_map/ppermute | solution.py:507

commit v6 on v4

--- a/solution.py
+++ b/solution.py
@@ -22,6 +22,7 @@
 
 LANES = 128
 STEP = 32
+SETTLE = 256
 PARTS = 2
 EDGE = 16
 RIM = 8
@@ -224,6 +225,8 @@
         slot, filled = home_slot(table, hop)
         bound = jnp.where(filled, f32(dual_bound), f32(0.0))
         _, in_filled = chosen(tables[i], -hop)
+        partner = lax.axis_index("tm") // stride + hop
+        in_filled = in_filled & (partner >= 0) & (partner < CYCLES)
         in_offset = offset_of(tables[i], -hop)
         low = jnp.where(in_filled, -in_offset, 4 * rows)
         high = rows - 1 - in_offset
@@ -366,7 +369,7 @@
     )(*images)
 
 
-def settle_kernel(terms, slices, kept, total, *refs):
+def settle_kernel(terms, slices, kept, origin, total, *refs):
     refs = list(refs)
     take = lambda k: [refs.pop(0) for _ in range(k)]
     duals = [take(len(starts)) for starts in terms]
@@ -389,16 +392,16 @@
         target = rest if z in kept else out
 
         def body(step, carry):
-            here = pl.ds(pl.multiple_of(step * STEP, STEP), STEP)
+            here = pl.ds(pl.multiple_of(step * SETTLE, SETTLE), SETTLE)
             arriving = None
             for dual, within, weight, gain in here_terms:
                 value = dual[within, here, :] + gain[z, here, :]
                 value = weight[z, here, :] * jnp.minimum(jnp.maximum(value, -dual_bound), dual_bound)
                 arriving = value if arriving is None else arriving + value
-            target[place, here, :] = total[z - slices[0], here, :] - flow * arriving
+            target[place, here, :] = total[z - origin, here, :] - flow * arriving
             return carry
 
-        lax.fori_loop(0, rows // STEP, body, 0)
+        lax.fori_loop(0, rows // SETTLE, body, 0)
         if z not in kept:
             moves.append(pltpu.make_async_copy(out.at[place], result.at[z], sems.at[place]))
             moves[-1].start()
@@ -406,7 +409,7 @@
         m.wait()
 
 
-def settle(total, terms, slices, kept, depth, result=None):
+def settle(total, terms, slices, kept, depth, result=None, origin=0):
     vmem_spec, any_spec = pl.BlockSpec(memory_space=pltpu.VMEM), pl.BlockSpec(memory_space=pl.ANY)
     rows, columns = total.shape[1:]
     f32 = jnp.float32
@@ -427,7 +430,7 @@
         out_specs.append(any_spec)
         scratch = [pltpu.VMEM((finished, rows, columns), f32), pltpu.SemaphoreType.DMA((finished,))]
     return pl.pallas_call(
-        functools.partial(settle_kernel, tuple(t[1] for t in terms), slices, kept),
+        functools.partial(settle_kernel, tuple(t[1] for t in terms), slices, kept, origin),
         in_specs=specs,
         out_specs=out_specs,
         out_shape=shapes,
@@ -440,6 +443,14 @@
     )(*operands)
 
 
+def complete(pairs_, frames, spaces):
+    return [
+        (a * spaces + s, b * spaces + s if 0 <= b < frames else a * spaces + (s ^ 1))
+        for a, b in pairs_
+        for s in range(spaces)
+    ]
+
+
 def shards(volume, prior_image, dual_pairs, pair_cycle, pair_offset):
     frames = lax.axis_size("tm")
     spaces = lax.axis_size("space")
@@ -450,10 +461,10 @@
     every = range(frames)
     swap = [(t, t + stride if cycle_of(t) % 2 == 0 else t - stride) for t in every]
     cross = [(t, t - stride if cycle_of(t) % 2 == 0 else t + stride) for t in every]
-    cross = [(a, b) for a, b in cross if 0 <= b < frames]
+    cross = complete(cross, frames, spaces)
     wide_swap = [(t, t + 2 * stride if cycle_of(t) // 2 % 2 == 0 else t - 2 * stride) for t in every]
     wide_cross = [(t, t - 2 * stride if cycle_of(t) // 2 % 2 == 0 else t + 2 * stride) for t in every]
-    wide_cross = [(a, b) for a, b in wide_cross if 0 <= b < frames]
+    wide_cross = complete(wide_cross, frames, spaces)
     relay = [(t, t + 2 * stride if cycle_of(t) % 2 == 0 else t - 2 * stride) for t in every]
     relay = [(a, b) for a, b in relay if 0 <= b < frames]
     inner = [(s, s ^ 1) for s in range(spaces)]
@@ -471,24 +482,31 @@
 
     near_image = send(image, swap)
     wide_near_image = send(image, wide_swap)
-    wide_far_image = send(image, wide_cross)
+    wide_far_image = send(image, wide_cross, ("tm", "space"))
     near_table = send(table, swap)
-    far_table = send(table, cross)
+    far_table = send(table, cross, ("tm", "space"))
     wide_near_table = send(table, wide_swap)
-    wide_far_table = send(table, wide_cross)
+    wide_far_table = send(table, wide_cross, ("tm", "space"))
     depth = image.shape[0]
     part = max(depth // 4, 1)
-    near_dual, far_dual = pack((0, 1), ((depth,),) * 2, stride, table, dual)
-    near_dual = send(near_dual, swap)
-    far_dual = send(far_dual, cross)
-    lead, rest, main, last = pack((2, 3), ((part, depth - part), (depth - part, part)), stride, table, dual)
+    both = ("tm", "space")
+    near_main, near_last, far_main, far_last = pack((0, 1), ((depth - part, part),) * 2, stride, table, dual)
+    near_main = send(near_main, swap)
+    far_main = send(far_main, cross, both)
+    lead, rest, wide_last, far_lead, main, last = pack(
+        (2, 3), ((part, depth - 2 * part, part),) * 2, stride, table, dual
+    )
     lead = send(lead, wide_swap)
+    far_lead = send(far_lead, wide_cross, ("tm", "space"))
     far_image = send(near_image, relay)
 
     within, across = halos((image, near_image, wide_near_image, wide_far_image))
-    main = send(main, wide_cross)
+    main = send(main, wide_cross, ("tm", "space"))
     rest = send(rest, wide_swap)
-    last = send(last, wide_cross)
+    near_last = send(near_last, swap)
+    far_last = send(far_last, cross, both)
+    last = send(last, wide_cross, ("tm", "space"))
+    wide_last = send(wide_last, wide_swap)
     fresh, total, w0, w2, w3, g0, g2, g3 = pairs(
         ((0, 1), (2, 2), (3, 3)), stride, table, (near_table, wide_near_table, wide_far_table),
         image, dual, prior_image[0],
@@ -499,14 +517,28 @@
         ((1, 0),), stride, table, (far_table,), image, dual, total,
         (far_image,), (far_within,), (far_across,), (within, across), fresh,
     )
-    every_slice, late = tuple(range(depth)), tuple(range(depth - part, depth))
-    (total,) = settle(
-        total, (((near_dual,), (0,), w0, g0), ((far_dual,), (0,), w1, g1)), every_slice, every_slice, depth
-    )
-    total, volume_next = settle(
-        total, (((lead, rest), (0, part), w2, g2), ((main,), (0,), w3, g3)), every_slice, late, depth
-    )
-    (volume_next,) = settle(total, (((last,), (depth - part,), w3, g3),), late, (), depth, volume_next)
+    early, late = tuple(range(depth - part)), tuple(range(depth - part, depth))
+    start = depth - part
+    (volume_next,) = settle(
+        total,
+        (
+            ((near_main,), (0,), w0, g0),
+            ((far_main,), (0,), w1, g1),
+            ((lead, rest), (0, part), w2, g2),
+            ((far_lead, main), (0, part), w3, g3),
+        ),
+        early, (), depth,
+    )
+    (volume_next,) = settle(
+        total,
+        (
+            ((near_last,), (start,), w0, g0),
+            ((far_last,), (start,), w1, g1),
+            ((wide_last,), (start,), w2, g2),
+            ((last,), (start,), w3, g3),
+        ),
+        late, (), depth, volume_next,
+    )
     return (volume_next[None], fresh[None])
 
 

time: 113 us -> 142 us (1.26)
  waiting for transfers between devices: 56.2 us -> 93.9 us
  starting transfers between devices: 32.5 us -> 24.1 us
    ppermute x18 -> x22, waiting for transfers between devices: 56.2 us -> 93.9 us  [send(): return lax.ppermute(x, axis, pairs_)]
    ppermute x18 -> x22, starting transfers between devices: 32.5 us -> 24.1 us  [send(): return lax.ppermute(x, axis, pairs_)]
  transfers between devices with their start and end apart: 18 -> 22, of which waited for: 9 -> 8; matrix products, arithmetic and copies ran while one was open for 1% -> 1% of each run, Pallas kernels for 18% -> 14%
where the time goes in v6:
time: 142 us; the launch traced here: 140 us
  waiting for transfers between devices  93.9 us (66%)
  starting transfers between devices  24.1 us (17%)
  Pallas kernels  20.1 us (14%)
    ppermute x22, waiting for transfers between devices, send(): return lax.ppermute(x, axis, pairs_)  93.9 us
    ppermute x22, starting transfers between devices, send(): return lax.ppermute(x, axis, pairs_)  24.1 us
    pallas_call x2, Pallas kernels, pairs(): pl.pallas_call(functools.partial(pair_kernel, places, first, stride), in_...  12.9 us
    pallas_call x2, Pallas kernels, pack(): pl.pallas_call(functools.partial(pack_kernel, places, pieces, stride), in...  4.5 us
  transfers between devices with their start and end apart: 22, of which 8 were waited for; matrix products, arithmetic and copies ran while one was open for 1% of the time, Pallas kernels for 14%

profile of v6, /device:TPU:10, one launch (start us, length us, event | category | flops | bytes accessed | tf_op | source)
XLA Modules:
  0.0 139.7 jit_solution(6879793720197685124)
XLA Ops:
  0.6 1.6 %collective-permute-start.4 = (f32[4,256,256]{2,1,0:T(8,128)}, f32[4,256,256]{2,1,0:T(8,128)S(1)}, u32[]{:S(2)}, u32[]{:S(2)}) collective-permute-start(f32[4,256,256]{2,1,0:T(8,128)} %bitcast.11), channel_id=1, source_target_pairs={{0,4},{4,0},{8,12},{12,8},{16,20},{20,16},{24,28},{28,24},{1,5},{5... | collective-permute-start | bytes 3145736 | tf_op jit(solution)/shard_map/ppermute | solution.py:475
  2.2 0.4 collective-permute-start.5
  2.7 2.7 %collective-permute-start.6 = (f32[4,256,256]{2,1,0:T(8,128)}, f32[4,256,256]{2,1,0:T(8,128)S(1)}, u32[]{:S(2)}, u32[]{:S(2)}) collective-permute-start(f32[4,256,256]{2,1,0:T(8,128)} %bitcast.13), channel_id=1, source_target_pairs={{0,1},{1,0},{2,3},{3,2},{4,5},{5,4},{6,7},{7,6},{8,16},{9,17},{10,... | collective-permute-start | bytes 3145736 | tf_op jit(solution)/shard_map/ppermute | solution.py:475
  5.4 20.4 %collective-permute-done.4.refs_1_.refs_6_ = f32[4,256,256]{2,1,0:T(8,128)S(1)} collective-permute-done((f32[4,256,256]{2,1,0:T(8,128)}, f32[4,256,256]{2,1,0:T(8,128)S(1)}, u32[]{:S(2)}, u32[]{:S(2)}) %collective-permute-start.4) | collective-permute-done | bytes 1048608 | tf_op jit(solution)/shard_map/ppermute | solution.py:475
  25.8 3.5 %collective-permute-start.9 = (f32[4,256,256]{2,1,0:T(8,128)S(1)}, f32[4,256,256]{2,1,0:T(8,128)S(1)}, u32[]{:S(2)}, u32[]{:S(2)}) collective-permute-start(f32[4,256,256]{2,1,0:T(8,128)S(1)} %collective-permute-done.4.refs_1_.refs_6_), channel_id=1, source_target_pairs={{0,8},{8,16},{12,4},{16,24},{20,12},{28,20},{1,9},{9,17},{13,5},{1... | collective-permute-start | bytes 3145736 | tf_op jit(solution)/shard_map/ppermute | solution.py:475
  29.3 0.7 pad_add_fusion.table
  30.0 2.3 %shard_map.73 = (f32[1,256,256]{2,1,0:T(8,128)S(1)}, f32[2,256,256]{2,1,0:T(8,128)S(1)}, f32[1,256,256]{2,1,0:T(8,128)S(1)}, f32[1,256,256]{2,1,0:T(8,128)S(1)},...) custom-call(s32[8]{0:T(128)S(1)} %pad_add_fusion.table, f32[4,4,256,256]{3,2,1,0:T(8,128)} %bitcast.7), custom_call_target="tpu_custom_call" | custom-call | bytes 4194304 | tf_op jit(solution)/shard_map/pallas_call | solution.py:115
  32.3 0.6 collective-permute-start.18
  32.9 1.5 %collective-permute-start.19 = (f32[2,256,256]{2,1,0:T(8,128)S(1)}, f32[2,256,256]{2,1,0:T(8,128)S(1)}, u32[]{:S(2)}, u32[]{:S(2)}) collective-permute-start(f32[2,256,256]{2,1,0:T(8,128)S(1)} %get-tuple-element.50), channel_id=1, source_target_pairs={{0,8},{4,12},{8,0},{12,4},{16,24},{20,28},{24,16},{28,20},{1,9},{5... | collective-permute-start | bytes 1572872 | tf_op jit(solution)/shard_map/ppermute | solution.py:475
  34.4 1.6 %collective-permute-start.20 = (f32[1,256,256]{2,1,0:T(8,128)S(1)}, f32[1,256,256]{2,1,0:T(8,128)S(1)}, u32[]{:S(2)}, u32[]{:S(2)}) collective-permute-start(f32[1,256,256]{2,1,0:T(8,128)S(1)} %get-tuple-element.51), channel_id=1, source_target_pairs={{0,1},{1,0},{2,3},{3,2},{4,5},{5,4},{6,7},{7,6},{8,16},{9,17},{10,... | collective-permute-start | bytes 786440 | tf_op jit(solution)/shard_map/ppermute | solution.py:475
  36.0 0.4 collective-permute-start.1
  36.4 0.2 shard_map.68
  36.6 3.0 %collective-permute-done.1.refs_0_ = s32[8]{0:T(128)S(1)} collective-permute-done((s32[8]{0:T(128)S(1)}, s32[8]{0:T(128)S(1)}, u32[]{:S(2)}, u32[]{:S(2)}) %collective-permute-start.1) | collective-permute-done | bytes 64 | tf_op jit(solution)/shard_map/ppermute | solution.py:475
  39.6 29.1 %collective-permute-done.2.refs_1_ = s32[8]{0:T(128)S(1)} collective-permute-done((s32[8]{0:T(128)S(1)}, s32[8]{0:T(128)S(1)}, u32[]{:S(2)}, u32[]{:S(2)}) %collective-permute-start.2) | collective-permute-done | bytes 64 | tf_op jit(solution)/shard_map/ppermute | solution.py:475
  68.7 0.6 collective-permute-start.3
  69.3 2.9 %collective-permute-done.3.refs_2_ = s32[8]{0:T(128)S(1)} collective-permute-done((s32[8]{0:T(128)S(1)}, s32[8]{0:T(128)S(1)}, u32[]{:S(2)}, u32[]{:S(2)}) %collective-permute-start.3) | collective-permute-done | bytes 64 | tf_op jit(solution)/shard_map/ppermute | solution.py:475
  72.3 4.5 %collective-permute-done.refs_0_ = s32[8]{0:T(128)S(1)} collective-permute-done((s32[8]{0:T(128)S(1)}, s32[8]{0:T(128)S(1)}, u32[]{:S(2)}, u32[]{:S(2)}) %collective-permute-start) | collective-permute-done | bytes 64 | tf_op jit(solution)/shard_map/ppermute | solution.py:475
  76.7 2.5 %collective-permute-start.8 = (f32[4,256,256]{2,1,0:T(8,128)S(1)}, f32[4,256,256]{2,1,0:T(8,128)S(1)}, u32[]{:S(2)}, u32[]{:S(2)}) collective-permute-start(f32[4,256,256]{2,1,0:T(8,128)S(1)} %get-tuple-element.29), channel_id=1, source_target_pairs={{1,2},{2,1},{5,6},{6,5},{9,10},{10,9},{13,14},{14,13},{17,18},{18,... | collective-permute-start | bytes 3145736 | tf_op jit(solution)/shard_map/ppermute | solution.py:475
  79.3 2.2 %shard_map.72 = (f32[3,256,256]{2,1,0:T(8,128)S(1)}, f32[1,256,256]{2,1,0:T(8,128)S(1)}, f32[3,256,256]{2,1,0:T(8,128)S(1)}, f32[1,256,256]{2,1,0:T(8,128)S(1)}) custom-call(s32[8]{0:T(128)S(1)} %pad_add_fusion.table, f32[4,4,256,256]{3,2,1,0:T(8,128)} %bitcast.8), custom_call_target="tpu_custom_call" | custom-call | bytes 4194304 | tf_op jit(solution)/shard_map/pallas_call | solution.py:115
  81.6 1.1 collective-permute-start.16
  82.7 2.0 %collective-permute-start.21 = (f32[2,256,256]{2,1,0:T(8,128)S(1)}, f32[2,256,256]{2,1,0:T(8,128)S(1)}, u32[]{:S(2)}, u32[]{:S(2)}) collective-permute-start(f32[2,256,256]{2,1,0:T(8,128)S(1)} %get-tuple-element.52), channel_id=1, source_target_pairs={{0,1},{1,0},{2,3},{3,2},{4,5},{5,4},{6,7},{7,6},{8,16},{9,17},{10,... | collective-permute-start | bytes 1572872 | tf_op jit(solution)/shard_map/ppermute | solution.py:475
  84.8 12.7 %collective-permute-done.21.refs_5_ = f32[2,256,256]{2,1,0:T(8,128)S(1)} collective-permute-done((f32[2,256,256]{2,1,0:T(8,128)S(1)}, f32[2,256,256]{2,1,0:T(8,128)S(1)}, u32[]{:S(2)}, u32[]{:S(2)}) %collective-permute-start.21) | collective-permute-done | bytes 524320 | tf_op jit(solution)/shard_map/ppermute | solution.py:475
  97.5 19.1 %collective-permute-done.16.refs_0_ = f32[3,256,256]{2,1,0:T(8,128)S(1)} collective-permute-done((f32[3,256,256]{2,1,0:T(8,128)S(1)}, f32[3,256,256]{2,1,0:T(8,128)S(1)}, u32[]{:S(2)}, u32[]{:S(2)}) %collective-permute-start.16) | collective-permute-done | bytes 786464 | tf_op jit(solution)/shard_map/ppermute | solution.py:475
  116.6 2.3 %collective-permute-start.11 = (f32[1,256,256]{2,1,0:T(8,128)S(1)}, f32[1,256,256]{2,1,0:T(8,128)S(1)}, u32[]{:S(2)}, u32[]{:S(2)}) collective-permute-start(f32[1,256,256]{2,1,0:T(8,128)S(1)} %get-tuple-element.32), channel_id=1, source_target_pairs={{1,2},{2,1},{5,6},{6,5},{9,10},{10,9},{13,14},{14,13},{17,18},{18,... | collective-permute-start | bytes 786440 | tf_op jit(solution)/shard_map/ppermute | solution.py:475
  118.9 0.1 collective-permute-start.14
  119.0 1.6 %collective-permute-start.15 = (f32[1,256,256]{2,1,0:T(8,128)S(1)}, f32[1,256,256]{2,1,0:T(8,128)S(1)}, u32[]{:S(2)}, u32[]{:S(2)}) collective-permute-start(f32[1,256,256]{2,1,0:T(8,128)S(1)} %get-tuple-element.38), channel_id=1, source_target_pairs={{0,1},{1,0},{2,3},{3,2},{4,5},{5,4},{6,7},{7,6},{8,16},{9,17},{10,... | collective-permute-start | bytes 786440 | tf_op jit(solution)/shard_map/ppermute | solution.py:475
  120.6 1.6 %collective-permute-start.12 = (f32[1,256,256]{2,1,0:T(8,128)S(1)}, f32[1,256,256]{2,1,0:T(8,128)S(1)}, u32[]{:S(2)}, u32[]{:S(2)}) collective-permute-start(f32[1,256,256]{2,1,0:T(8,128)S(1)} %get-tuple-element.35), channel_id=1, source_target_pairs={{0,4},{4,0},{8,12},{12,8},{16,20},{20,16},{24,28},{28,24},{1,5},{5... | collective-permute-start | bytes 786440 | tf_op jit(solution)/shard_map/ppermute | solution.py:475
  122.2 2.1 %collective-permute-done.11.refs_6_ = f32[1,256,256]{2,1,0:T(8,128)S(1)} collective-permute-done((f32[1,256,256]{2,1,0:T(8,128)S(1)}, f32[1,256,256]{2,1,0:T(8,128)S(1)}, u32[]{:S(2)}, u32[]{:S(2)}) %collective-permute-start.11) | collective-permute-done | bytes 262176 | tf_op jit(solution)/shard_map/ppermute | solution.py:475
  124.3 9.0 %shard_map.69 = (f32[4,4,256,256]{3,2,1,0:T(8,128)}, f32[4,256,256]{2,1,0:T(8,128)S(1)}, f32[4,256,256]{2,1,0:T(8,128)S(1)}, f32[4,256,256]{2,1,0:T(8,128)S(1)},...) custom-call(s32[8]{0:T(128)S(1)} %pad_add_fusion.table, ...), custom_call_target="tpu_custom_call" | custom-call | flops 47185920 | bytes 25165824 | tf_op jit(solution)/shard_map/pallas_call | solution.py:317
  133.3 3.9 %shard_map.71 = (f32[4,4,256,256]{3,2,1,0:T(8,128)}, f32[4,256,256]{2,1,0:T(8,128)S(1)}, f32[4,256,256]{2,1,0:T(8,128)S(1)}, f32[4,256,256]{2,1,0:T(8,128)S(1)}) custom-call(s32[8]{0:T(128)S(1)} %pad_add_fusion.table, s32[8]{0:T(128)S(1)} %collective-permute-done.refs_0_, f32[4,256,256]{2,1,0:T(8,128)S(1)} %bitcast.16, ...), custom_call_target="tpu_custom_call", output_to_operand_aliasing={{0}: (10, {})} | custom-call | flops 15728640 | bytes 10485760 | tf_op jit(solution)/shard_map/pallas_call | solution.py:317
  137.2 1.5 %shard_map.74.refs_12_ = f32[4,256,256]{2,1,0:T(8,128)} custom-call(f32[4,256,256]{2,1,0:T(8,128)S(1)} %get-tuple-element.34.total, f32[3,256,256]{2,1,0:T(8,128)S(1)} %collective-permute-done.16.refs_0_, f32[3,256,256]{2,1,0:T(8,128)S(1)} %collective-permute-done.17.refs_1_, f32[1,256,256]{2,1,0:T(8,128)S(1)} %collective-permute-done.18.refs_2_, ...), custom_call_target="tpu_custom_call" | custom-call | flops 5242880 | bytes 14680064 | tf_op jit(solution)/shard_map/pallas_call | solution.py:432
  138.7 1.0 shard_map.75
  (27 shorter events, 0.1 us)
Async XLA Ops:
  0.6 35.7 %copy-start.1 = (f32[1,4,256,256]{3,2,1,0:T(8,128)S(1)}, f32[1,4,256,256]{3,2,1,0:T(8,128)}, u32[]{:S(2)}) copy-start(f32[1,4,256,256]{3,2,1,0:T(8,128)} %param.5) | copy-start | bytes 3145732
  0.6 25.2 %collective-permute-start.4 = (f32[4,256,256]{2,1,0:T(8,128)}, f32[4,256,256]{2,1,0:T(8,128)S(1)}, u32[]{:S(2)}, u32[]{:S(2)}) collective-permute-start(f32[4,256,256]{2,1,0:T(8,128)} %bitcast.11), channel_id=1, source_target_pairs={{0,4},{4,0},{8,12},{12,8},{16,20},{20,16},{24,28},{28,24},{1,5},{5... | collective-permute-start | bytes 3145736 | tf_op jit(solution)/shard_map/ppermute | solution.py:475
  2.2 32.2 %collective-permute-start.5 = (f32[4,256,256]{2,1,0:T(8,128)}, f32[4,256,256]{2,1,0:T(8,128)S(1)}, u32[]{:S(2)}, u32[]{:S(2)}) collective-permute-start(f32[4,256,256]{2,1,0:T(8,128)} %bitcast.12), channel_id=1, source_target_pairs={{0,8},{4,12},{8,0},{12,4},{16,24},{20,28},{24,16},{28,20},{1,9},{5... | collective-permute-start | bytes 3145736 | tf_op jit(solution)/shard_map/ppermute | solution.py:475
  2.7 33.3 %collective-permute-start.6 = (f32[4,256,256]{2,1,0:T(8,128)}, f32[4,256,256]{2,1,0:T(8,128)S(1)}, u32[]{:S(2)}, u32[]{:S(2)}) collective-permute-start(f32[4,256,256]{2,1,0:T(8,128)} %bitcast.13), channel_id=1, source_target_pairs={{0,1},{1,0},{2,3},{3,2},{4,5},{5,4},{6,7},{7,6},{8,16},{9,17},{10,... | collective-permute-start | bytes 3145736 | tf_op jit(solution)/shard_map/ppermute | solution.py:475
  25.8 58.9 %collective-permute-start.9 = (f32[4,256,256]{2,1,0:T(8,128)S(1)}, f32[4,256,256]{2,1,0:T(8,128)S(1)}, u32[]{:S(2)}, u32[]{:S(2)}) collective-permute-start(f32[4,256,256]{2,1,0:T(8,128)S(1)} %collective-permute-done.4.refs_1_.refs_6_), channel_id=1, source_target_pairs={{0,8},{8,16},{12,4},{16,24},{20,12},{28,20},{1,9},{9,17},{13,5},{1... | collective-permute-start | bytes 3145736 | tf_op jit(solution)/shard_map/ppermute | solution.py:475
  32.3 44.4 %collective-permute-start.18 = (f32[1,256,256]{2,1,0:T(8,128)S(1)}, f32[1,256,256]{2,1,0:T(8,128)S(1)}, u32[]{:S(2)}, u32[]{:S(2)}) collective-permute-start(f32[1,256,256]{2,1,0:T(8,128)S(1)} %get-tuple-element.49), channel_id=1, source_target_pairs={{0,8},{4,12},{8,0},{12,4},{16,24},{20,28},{24,16},{28,20},{1,9},{5... | collective-permute-start | bytes 786440 | tf_op jit(solution)/shard_map/ppermute | solution.py:475
  32.9 49.8 %collective-permute-start.19 = (f32[2,256,256]{2,1,0:T(8,128)S(1)}, f32[2,256,256]{2,1,0:T(8,128)S(1)}, u32[]{:S(2)}, u32[]{:S(2)}) collective-permute-start(f32[2,256,256]{2,1,0:T(8,128)S(1)} %get-tuple-element.50), channel_id=1, source_target_pairs={{0,8},{4,12},{8,0},{12,4},{16,24},{20,28},{24,16},{28,20},{1,9},{5... | collective-permute-start | bytes 1572872 | tf_op jit(solution)/shard_map/ppermute | solution.py:475
  34.4 89.9 %copy-start = (f32[1,4,4,256,256]{4,3,2,1,0:T(8,128)S(1)}, f32[1,4,4,256,256]{4,3,2,1,0:T(8,128)}, u32[]{:S(2)}) copy-start(f32[1,4,4,256,256]{4,3,2,1,0:T(8,128)} %param.7) | copy-start | bytes 12582916
  34.4 89.9 %copy-start.2 = (f32[1,4,256,256]{3,2,1,0:T(8,128)S(1)}, f32[1,4,256,256]{3,2,1,0:T(8,128)}, u32[]{:S(2)}) copy-start(f32[1,4,256,256]{3,2,1,0:T(8,128)} %param.6) | copy-start | bytes 3145732
  34.4 47.1 %collective-permute-start.20 = (f32[1,256,256]{2,1,0:T(8,128)S(1)}, f32[1,256,256]{2,1,0:T(8,128)S(1)}, u32[]{:S(2)}, u32[]{:S(2)}) collective-permute-start(f32[1,256,256]{2,1,0:T(8,128)S(1)} %get-tuple-element.51), channel_id=1, source_target_pairs={{0,1},{1,0},{2,3},{3,2},{4,5},{5,4},{6,7},{7,6},{8,16},{9,17},{10,... | collective-permute-start | bytes 786440 | tf_op jit(solution)/shard_map/ppermute | solution.py:475
  36.0 3.6 %collective-permute-start.1 = (s32[8]{0:T(128)S(1)}, s32[8]{0:T(128)S(1)}, u32[]{:S(2)}, u32[]{:S(2)}) collective-permute-start(s32[8]{0:T(128)S(1)} %pad_add_fusion.table), channel_id=1, source_target_pairs={{0,4},{4,0},{8,12},{12,8},{16,20},{20,16},{24,28},{28,24},{1,5},{5... | collective-permute-start | bytes 104 | tf_op jit(solution)/shard_map/ppermute | solution.py:475
  39.6 29.1 %collective-permute-start.2 = (s32[8]{0:T(128)S(1)}, s32[8]{0:T(128)S(1)}, u32[]{:S(2)}, u32[]{:S(2)}) collective-permute-start(s32[8]{0:T(128)S(1)} %pad_add_fusion.table), channel_id=1, source_target_pairs={{0,8},{4,12},{8,0},{12,4},{16,24},{20,28},{24,16},{28,20},{1,9},{5... | collective-permute-start | bytes 104 | tf_op jit(solution)/shard_map/ppermute | solution.py:475
  68.7 3.6 %collective-permute-start.3 = (s32[8]{0:T(128)S(1)}, s32[8]{0:T(128)S(1)}, u32[]{:S(2)}, u32[]{:S(2)}) collective-permute-start(s32[8]{0:T(128)S(1)} %pad_add_fusion.table), channel_id=1, source_target_pairs={{0,1},{1,0},{2,3},{3,2},{4,5},{5,4},{6,7},{7,6},{8,16},{9,17},{10,... | collective-permute-start | bytes 104 | tf_op jit(solution)/shard_map/ppermute | solution.py:475
  72.3 4.5 %collective-permute-start = (s32[8]{0:T(128)S(1)}, s32[8]{0:T(128)S(1)}, u32[]{:S(2)}, u32[]{:S(2)}) collective-permute-start(s32[8]{0:T(128)S(1)} %pad_add_fusion.table), channel_id=1, source_target_pairs={{0,1},{1,0},{2,3},{3,2},{4,8},{5,9},{6,10},{7,11},{8,4},{9,5},{10,... | collective-permute-start | bytes 104 | tf_op jit(solution)/shard_map/ppermute | solution.py:475
  76.7 42.2 %collective-permute-start.7 = (f32[4,256,256]{2,1,0:T(8,128)S(1)}, f32[4,256,256]{2,1,0:T(8,128)S(1)}, u32[]{:S(2)}, u32[]{:S(2)}) collective-permute-start(f32[4,256,256]{2,1,0:T(8,128)S(1)} %get-tuple-element.28), channel_id=1, source_target_pairs={{0,1},{1,0},{2,3},{3,2},{4,5},{5,4},{6,7},{7,6},{8,9},{9,8},{10,11... | collective-permute-start | bytes 3145736 | tf_op jit(solution)/shard_map/ppermute | solution.py:475
  76.7 42.3 %collective-permute-start.8 = (f32[4,256,256]{2,1,0:T(8,128)S(1)}, f32[4,256,256]{2,1,0:T(8,128)S(1)}, u32[]{:S(2)}, u32[]{:S(2)}) collective-permute-start(f32[4,256,256]{2,1,0:T(8,128)S(1)} %get-tuple-element.29), channel_id=1, source_target_pairs={{1,2},{2,1},{5,6},{6,5},{9,10},{10,9},{13,14},{14,13},{17,18},{18,... | collective-permute-start | bytes 3145736 | tf_op jit(solution)/shard_map/ppermute | solution.py:475
  81.6 35.0 %collective-permute-start.16 = (f32[3,256,256]{2,1,0:T(8,128)S(1)}, f32[3,256,256]{2,1,0:T(8,128)S(1)}, u32[]{:S(2)}, u32[]{:S(2)}) collective-permute-start(f32[3,256,256]{2,1,0:T(8,128)S(1)} %get-tuple-element.47), channel_id=1, source_target_pairs={{0,4},{4,0},{8,12},{12,8},{16,20},{20,16},{24,28},{28,24},{1,5},{5... | collective-permute-start | bytes 2359304 | tf_op jit(solution)/shard_map/ppermute | solution.py:475
  82.7 14.8 %collective-permute-start.21 = (f32[2,256,256]{2,1,0:T(8,128)S(1)}, f32[2,256,256]{2,1,0:T(8,128)S(1)}, u32[]{:S(2)}, u32[]{:S(2)}) collective-permute-start(f32[2,256,256]{2,1,0:T(8,128)S(1)} %get-tuple-element.52), channel_id=1, source_target_pairs={{0,1},{1,0},{2,3},{3,2},{4,5},{5,4},{6,7},{7,6},{8,16},{9,17},{10,... | collective-permute-start | bytes 1572872 | tf_op jit(solution)/shard_map/ppermute | solution.py:475
  84.7 52.5 %collective-permute-start.17 = (f32[3,256,256]{2,1,0:T(8,128)S(1)}, f32[3,256,256]{2,1,0:T(8,128)S(1)}, u32[]{:S(2)}, u32[]{:S(2)}) collective-permute-start(f32[3,256,256]{2,1,0:T(8,128)S(1)} %get-tuple-element.48), channel_id=1, source_target_pairs={{0,1},{1,0},{2,3},{3,2},{4,8},{5,9},{6,10},{7,11},{8,4},{9,5},{10,... | collective-permute-start | bytes 2359304 | tf_op jit(solution)/shard_map/ppermute | solution.py:475
  97.5 23.1 %collective-permute-start.10 = (f32[1,256,256]{2,1,0:T(8,128)S(1)}, f32[1,256,256]{2,1,0:T(8,128)S(1)}, u32[]{:S(2)}, u32[]{:S(2)}) collective-permute-start(f32[1,256,256]{2,1,0:T(8,128)S(1)} %get-tuple-element.31), channel_id=1, source_target_pairs={{0,1},{1,0},{2,3},{3,2},{4,5},{5,4},{6,7},{7,6},{8,9},{9,8},{10,11... | collective-permute-start | bytes 786440 | tf_op jit(solution)/shard_map/ppermute | solution.py:475
  116.6 7.7 %collective-permute-start.11 = (f32[1,256,256]{2,1,0:T(8,128)S(1)}, f32[1,256,256]{2,1,0:T(8,128)S(1)}, u32[]{:S(2)}, u32[]{:S(2)}) collective-permute-start(f32[1,256,256]{2,1,0:T(8,128)S(1)} %get-tuple-element.32), channel_id=1, source_target_pairs={{1,2},{2,1},{5,6},{6,5},{9,10},{10,9},{13,14},{14,13},{17,18},{18,... | collective-permute-start | bytes 786440 | tf_op jit(solution)/shard_map/ppermute | solution.py:475
  118.9 19.7 %collective-permute-start.14 = (f32[1,256,256]{2,1,0:T(8,128)S(1)}, f32[1,256,256]{2,1,0:T(8,128)S(1)}, u32[]{:S(2)}, u32[]{:S(2)}) collective-permute-start(f32[1,256,256]{2,1,0:T(8,128)S(1)} %get-tuple-element.37), channel_id=1, source_target_pairs={{0,8},{4,12},{8,0},{12,4},{16,24},{20,28},{24,16},{28,20},{1,9},{5... | collective-permute-start | bytes 786440 | tf_op jit(solution)/shard_map/ppermute | solution.py:475
  119.0 19.7 %collective-permute-start.15 = (f32[1,256,256]{2,1,0:T(8,128)S(1)}, f32[1,256,256]{2,1,0:T(8,128)S(1)}, u32[]{:S(2)}, u32[]{:S(2)}) collective-permute-start(f32[1,256,256]{2,1,0:T(8,128)S(1)} %get-tuple-element.38), channel_id=1, source_target_pairs={{0,1},{1,0},{2,3},{3,2},{4,5},{5,4},{6,7},{7,6},{8,16},{9,17},{10,... | collective-permute-start | bytes 786440 | tf_op jit(solution)/shard_map/ppermute | solution.py:475
  120.6 18.1 %collective-permute-start.12 = (f32[1,256,256]{2,1,0:T(8,128)S(1)}, f32[1,256,256]{2,1,0:T(8,128)S(1)}, u32[]{:S(2)}, u32[]{:S(2)}) collective-permute-start(f32[1,256,256]{2,1,0:T(8,128)S(1)} %get-tuple-element.35), channel_id=1, source_target_pairs={{0,4},{4,0},{8,12},{12,8},{16,20},{20,16},{24,28},{28,24},{1,5},{5... | collective-permute-start | bytes 786440 | tf_op jit(solution)/shard_map/ppermute | solution.py:475
  124.3 14.4 %collective-permute-start.13 = (f32[1,256,256]{2,1,0:T(8,128)S(1)}, f32[1,256,256]{2,1,0:T(8,128)S(1)}, u32[]{:S(2)}, u32[]{:S(2)}) collective-permute-start(f32[1,256,256]{2,1,0:T(8,128)S(1)} %get-tuple-element.36), channel_id=1, source_target_pairs={{0,1},{1,0},{2,3},{3,2},{4,8},{5,9},{6,10},{7,11},{8,4},{9,5},{10,... | collective-permute-start | bytes 786440 | tf_op jit(solution)/shard_map/ppermute | solution.py:475

commit v7 on v6

--- a/solution.py
+++ b/solution.py
@@ -21,8 +21,8 @@
 
 
 LANES = 128
-STEP = 32
-SETTLE = 256
+STEP = 64
+SETTLE = 128
 PARTS = 2
 EDGE = 16
 RIM = 8
@@ -489,11 +489,10 @@
     wide_far_table = send(table, wide_cross, ("tm", "space"))
     depth = image.shape[0]
     part = max(depth // 4, 1)
-    both = ("tm", "space")
-    near_main, near_last, far_main, far_last = pack((0, 1), ((depth - part, part),) * 2, stride, table, dual)
-    near_main = send(near_main, swap)
-    far_main = send(far_main, cross, both)
-    lead, rest, wide_last, far_lead, main, last = pack(
+    near_dual, far_dual = pack((0, 1), ((depth,),) * 2, stride, table, dual)
+    near_dual = send(near_dual, swap)
+    far_dual = send(far_dual, cross, ("tm", "space"))
+    lead, rest, near_last, far_lead, main, last = pack(
         (2, 3), ((part, depth - 2 * part, part),) * 2, stride, table, dual
     )
     lead = send(lead, wide_swap)
@@ -503,10 +502,8 @@
     within, across = halos((image, near_image, wide_near_image, wide_far_image))
     main = send(main, wide_cross, ("tm", "space"))
     rest = send(rest, wide_swap)
-    near_last = send(near_last, swap)
-    far_last = send(far_last, cross, both)
     last = send(last, wide_cross, ("tm", "space"))
-    wide_last = send(wide_last, wide_swap)
+    near_last = send(near_last, wide_swap)
     fresh, total, w0, w2, w3, g0, g2, g3 = pairs(
         ((0, 1), (2, 2), (3, 3)), stride, table, (near_table, wide_near_table, wide_far_table),
         image, dual, prior_image[0],
@@ -517,27 +514,16 @@
         ((1, 0),), stride, table, (far_table,), image, dual, total,
         (far_image,), (far_within,), (far_across,), (within, across), fresh,
     )
-    early, late = tuple(range(depth - part)), tuple(range(depth - part, depth))
-    start = depth - part
+    every_slice, early, late = tuple(range(depth)), tuple(range(depth - part)), tuple(range(depth - part, depth))
+    (total,) = settle(
+        total, (((near_dual,), (0,), w0, g0), ((far_dual,), (0,), w1, g1)), every_slice, every_slice, depth
+    )
+    (volume_next,) = settle(
+        total, (((lead, rest), (0, part), w2, g2), ((far_lead, main), (0, part), w3, g3)), early, (), depth
+    )
     (volume_next,) = settle(
         total,
-        (
-            ((near_main,), (0,), w0, g0),
-            ((far_main,), (0,), w1, g1),
-            ((lead, rest), (0, part), w2, g2),
-            ((far_lead, main), (0, part), w3, g3),
-        ),
-        early, (), depth,
-    )
-    (volume_next,) = settle(
-        total,
-        (
-            ((near_last,), (start,), w0, g0),
-            ((far_last,), (start,), w1, g1),
-            ((wide_last,), (start,), w2, g2),
-            ((last,), (start,), w3, g3),
-        ),
-        late, (), depth, volume_next,
+        (((near_last,), (depth - part,), w2, g2), ((last,), (depth - part,), w3, g3)), late, (), depth, volume_next,
     )
     return (volume_next[None], fresh[None])
 

time: 142 us -> 106 us (0.75)
  waiting for transfers between devices: 93.9 us -> 59.7 us
    ppermute x22 -> x20, waiting for transfers between devices: 93.9 us -> 59.7 us  [send(): return lax.ppermute(x, axis, pairs_)]
    ppermute x22 -> x20, starting transfers between devices: 24.1 us -> 24.2 us  [send(): return lax.ppermute(x, axis, pairs_)]
  transfers between devices with their start and end apart: 22 -> 20, of which waited for: 8 -> 6; matrix products, arithmetic and copies ran while one was open for 1% -> 1% of each run, Pallas kernels for 14% -> 18%
where the time goes in v7:
time: 106 us; the launch traced here: 105 us
  waiting for transfers between devices  59.7 us (56%)
  starting transfers between devices  24.2 us (23%)
  Pallas kernels  19.4 us (18%)
    ppermute x20, waiting for transfers between devices, send(): return lax.ppermute(x, axis, pairs_)  59.7 us
    ppermute x20, starting transfers between devices, send(): return lax.ppermute(x, axis, pairs_)  24.2 us
    pallas_call x2, Pallas kernels, pairs(): pl.pallas_call(functools.partial(pair_kernel, places, first, stride), in_...  11.8 us
    pallas_call x2, Pallas kernels, pack(): pl.pallas_call(functools.partial(pack_kernel, places, pieces, stride), in...  4.76 us
    pallas_call x3, Pallas kernels, settle(): pl.pallas_call(functools.partial(settle_kernel, tuple((t[1] for t in term...  2.45 us
  transfers between devices with their start and end apart: 20, of which 6 were waited for; matrix products, arithmetic and copies ran while one was open for 1% of the time, Pallas kernels for 18%

profile of v7, /device:TPU:10, one launch (start us, length us, event | category | flops | bytes accessed | tf_op | source)
XLA Modules:
  0.0 104.9 jit_solution(10299644595644786374)
XLA Ops:
  0.6 1.6 %collective-permute-start.4 = (f32[4,256,256]{2,1,0:T(8,128)}, f32[4,256,256]{2,1,0:T(8,128)S(1)}, u32[]{:S(2)}, u32[]{:S(2)}) collective-permute-start(f32[4,256,256]{2,1,0:T(8,128)} %bitcast.11), channel_id=1, source_target_pairs={{0,4},{4,0},{8,12},{12,8},{16,20},{20,16},{24,28},{28,24},{1,5},{5... | collective-permute-start | bytes 3145736 | tf_op jit(solution)/shard_map/ppermute | solution.py:475
  2.2 0.4 collective-permute-start.5
  2.7 2.7 %collective-permute-start.6 = (f32[4,256,256]{2,1,0:T(8,128)}, f32[4,256,256]{2,1,0:T(8,128)S(1)}, u32[]{:S(2)}, u32[]{:S(2)}) collective-permute-start(f32[4,256,256]{2,1,0:T(8,128)} %bitcast.13), channel_id=1, source_target_pairs={{0,1},{1,0},{2,3},{3,2},{4,5},{5,4},{6,7},{7,6},{8,16},{9,17},{10,... | collective-permute-start | bytes 3145736 | tf_op jit(solution)/shard_map/ppermute | solution.py:475
  5.4 0.7 pad_add_fusion.table
  6.1 0.5 collective-permute-start.1
  6.6 2.2 %shard_map.72 = (f32[4,256,256]{2,1,0:T(8,128)S(1)}, f32[4,256,256]{2,1,0:T(8,128)S(1)}) custom-call(s32[8]{0:T(128)S(1)} %pad_add_fusion.table, f32[4,4,256,256]{3,2,1,0:T(8,128)} %bitcast.7), custom_call_target="tpu_custom_call" | custom-call | bytes 4194304 | tf_op jit(solution)/shard_map/pallas_call | solution.py:115
  8.9 0.0 copy-start
  8.9 0.0 copy-start.2
  8.9 2.5 %shard_map.74 = (f32[1,256,256]{2,1,0:T(8,128)S(1)}, f32[2,256,256]{2,1,0:T(8,128)S(1)}, f32[1,256,256]{2,1,0:T(8,128)S(1)}, f32[1,256,256]{2,1,0:T(8,128)S(1)},...) custom-call(s32[8]{0:T(128)S(1)} %pad_add_fusion.table, f32[4,4,256,256]{3,2,1,0:T(8,128)} %bitcast.8), custom_call_target="tpu_custom_call" | custom-call | bytes 4194304 | tf_op jit(solution)/shard_map/pallas_call | solution.py:115
  11.4 14.4 %collective-permute-done.4.refs_1_.refs_6_ = f32[4,256,256]{2,1,0:T(8,128)S(1)} collective-permute-done((f32[4,256,256]{2,1,0:T(8,128)}, f32[4,256,256]{2,1,0:T(8,128)S(1)}, u32[]{:S(2)}, u32[]{:S(2)}) %collective-permute-start.4) | collective-permute-done | bytes 1048608 | tf_op jit(solution)/shard_map/ppermute | solution.py:475
  25.8 0.4 collective-permute-start.16
  26.3 0.8 collective-permute-done.5.refs_2_.refs_7_
  27.1 0.7 collective-permute-start.12
  27.8 0.4 collective-permute-done.6.refs_3_.refs_8_
  28.2 4.2 %collective-permute-start.9 = (f32[4,256,256]{2,1,0:T(8,128)S(1)}, f32[4,256,256]{2,1,0:T(8,128)S(1)}, u32[]{:S(2)}, u32[]{:S(2)}) collective-permute-start(f32[4,256,256]{2,1,0:T(8,128)S(1)} %collective-permute-done.4.refs_1_.refs_6_), channel_id=1, source_target_pairs={{0,8},{8,16},{12,4},{16,24},{20,12},{28,20},{1,9},{9,17},{13,5},{1... | collective-permute-start | bytes 3145736 | tf_op jit(solution)/shard_map/ppermute | solution.py:475
  32.4 0.3 shard_map.68
  32.7 0.5 collective-permute-start.3
  33.2 20.2 %collective-permute-done.3.refs_2_ = s32[8]{0:T(128)S(1)} collective-permute-done((s32[8]{0:T(128)S(1)}, s32[8]{0:T(128)S(1)}, u32[]{:S(2)}, u32[]{:S(2)}) %collective-permute-start.3) | collective-permute-done | bytes 64 | tf_op jit(solution)/shard_map/ppermute | solution.py:475
  53.4 2.5 %collective-permute-start.8 = (f32[4,256,256]{2,1,0:T(8,128)S(1)}, f32[4,256,256]{2,1,0:T(8,128)S(1)}, u32[]{:S(2)}, u32[]{:S(2)}) collective-permute-start(f32[4,256,256]{2,1,0:T(8,128)S(1)} %get-tuple-element.27), channel_id=1, source_target_pairs={{1,2},{2,1},{5,6},{6,5},{9,10},{10,9},{13,14},{14,13},{17,18},{18,... | collective-permute-start | bytes 3145736 | tf_op jit(solution)/shard_map/ppermute | solution.py:475
  56.0 0.1 collective-permute-start.17
  56.1 2.8 %collective-permute-start.19 = (f32[2,256,256]{2,1,0:T(8,128)S(1)}, f32[2,256,256]{2,1,0:T(8,128)S(1)}, u32[]{:S(2)}, u32[]{:S(2)}) collective-permute-start(f32[2,256,256]{2,1,0:T(8,128)S(1)} %get-tuple-element.48), channel_id=1, source_target_pairs={{0,1},{1,0},{2,3},{3,2},{4,5},{5,4},{6,7},{7,6},{8,16},{9,17},{10,... | collective-permute-start | bytes 1572872 | tf_op jit(solution)/shard_map/ppermute | solution.py:475
  58.9 0.1 shard_map.70
  59.0 21.4 %collective-permute-done.13.refs_1_ = f32[4,256,256]{2,1,0:T(8,128)S(1)} collective-permute-done((f32[4,256,256]{2,1,0:T(8,128)S(1)}, f32[4,256,256]{2,1,0:T(8,128)S(1)}, u32[]{:S(2)}, u32[]{:S(2)}) %collective-permute-start.13) | collective-permute-done | bytes 1048608 | tf_op jit(solution)/shard_map/ppermute | solution.py:475
  80.4 2.5 %collective-permute-start.11 = (f32[1,256,256]{2,1,0:T(8,128)S(1)}, f32[1,256,256]{2,1,0:T(8,128)S(1)}, u32[]{:S(2)}, u32[]{:S(2)}) collective-permute-start(f32[1,256,256]{2,1,0:T(8,128)S(1)} %get-tuple-element.30), channel_id=1, source_target_pairs={{1,2},{2,1},{5,6},{6,5},{9,10},{10,9},{13,14},{14,13},{17,18},{18,... | collective-permute-start | bytes 786440 | tf_op jit(solution)/shard_map/ppermute | solution.py:475
  82.9 2.6 %collective-permute-start.18 = (f32[1,256,256]{2,1,0:T(8,128)S(1)}, f32[1,256,256]{2,1,0:T(8,128)S(1)}, u32[]{:S(2)}, u32[]{:S(2)}) collective-permute-start(f32[1,256,256]{2,1,0:T(8,128)S(1)} %get-tuple-element.47), channel_id=1, source_target_pairs={{0,1},{1,0},{2,3},{3,2},{4,5},{5,4},{6,7},{7,6},{8,16},{9,17},{10,... | collective-permute-start | bytes 786440 | tf_op jit(solution)/shard_map/ppermute | solution.py:475
  85.5 2.5 %collective-permute-done.11.refs_6_ = f32[1,256,256]{2,1,0:T(8,128)S(1)} collective-permute-done((f32[1,256,256]{2,1,0:T(8,128)S(1)}, f32[1,256,256]{2,1,0:T(8,128)S(1)}, u32[]{:S(2)}, u32[]{:S(2)}) %collective-permute-start.11) | collective-permute-done | bytes 262176 | tf_op jit(solution)/shard_map/ppermute | solution.py:475
  88.0 2.5 %collective-permute-start.15 = (f32[1,256,256]{2,1,0:T(8,128)S(1)}, f32[1,256,256]{2,1,0:T(8,128)S(1)}, u32[]{:S(2)}, u32[]{:S(2)}) collective-permute-start(f32[1,256,256]{2,1,0:T(8,128)S(1)} %get-tuple-element.40), channel_id=1, source_target_pairs={{0,1},{1,0},{2,3},{3,2},{4,5},{5,4},{6,7},{7,6},{8,16},{9,17},{10,... | collective-permute-start | bytes 786440 | tf_op jit(solution)/shard_map/ppermute | solution.py:475
  90.6 8.2 %shard_map.69 = (f32[4,4,256,256]{3,2,1,0:T(8,128)}, f32[4,256,256]{2,1,0:T(8,128)S(1)}, f32[4,256,256]{2,1,0:T(8,128)S(1)}, f32[4,256,256]{2,1,0:T(8,128)S(1)},...) custom-call(s32[8]{0:T(128)S(1)} %pad_add_fusion.table, ...), custom_call_target="tpu_custom_call" | custom-call | flops 47185920 | bytes 25165824 | tf_op jit(solution)/shard_map/pallas_call | solution.py:317
  98.8 3.6 %shard_map.71 = (f32[4,4,256,256]{3,2,1,0:T(8,128)}, f32[4,256,256]{2,1,0:T(8,128)S(1)}, f32[4,256,256]{2,1,0:T(8,128)S(1)}, f32[4,256,256]{2,1,0:T(8,128)S(1)}) custom-call(s32[8]{0:T(128)S(1)} %pad_add_fusion.table, s32[8]{0:T(128)S(1)} %collective-permute-done.refs_0_, f32[4,256,256]{2,1,0:T(8,128)S(1)} %bitcast.16, ...), custom_call_target="tpu_custom_call", output_to_operand_aliasing={{0}: (10, {})} | custom-call | flops 15728640 | bytes 10485760 | tf_op jit(solution)/shard_map/pallas_call | solution.py:317
  102.4 0.5 shard_map.73.total
  103.0 1.1 %shard_map.75.refs_6_ = f32[4,256,256]{2,1,0:T(8,128)} custom-call(f32[4,256,256]{2,1,0:T(8,128)S(1)} %shard_map.73.total, f32[1,256,256]{2,1,0:T(8,128)S(1)} %collective-permute-done.16.refs_0_, f32[2,256,256]{2,1,0:T(8,128)S(1)} %collective-permute-done.17.refs_1_, f32[1,256,256]{2,1,0:T(8,128)S(1)} %collective-permute-done.18.refs_2_, ...), custom_call_target="tpu_custom_call" | custom-call | flops 2621440 | bytes 8388608 | tf_op jit(solution)/shard_map/pallas_call | solution.py:432
  104.1 0.8 shard_map.76
  (24 shorter events, 0.1 us)
Async XLA Ops:
  0.6 25.2 %collective-permute-start.4 = (f32[4,256,256]{2,1,0:T(8,128)}, f32[4,256,256]{2,1,0:T(8,128)S(1)}, u32[]{:S(2)}, u32[]{:S(2)}) collective-permute-start(f32[4,256,256]{2,1,0:T(8,128)} %bitcast.11), channel_id=1, source_target_pairs={{0,4},{4,0},{8,12},{12,8},{16,20},{20,16},{24,28},{28,24},{1,5},{5... | collective-permute-start | bytes 3145736 | tf_op jit(solution)/shard_map/ppermute | solution.py:475
  2.2 24.8 %collective-permute-start.5 = (f32[4,256,256]{2,1,0:T(8,128)}, f32[4,256,256]{2,1,0:T(8,128)S(1)}, u32[]{:S(2)}, u32[]{:S(2)}) collective-permute-start(f32[4,256,256]{2,1,0:T(8,128)} %bitcast.12), channel_id=1, source_target_pairs={{0,8},{4,12},{8,0},{12,4},{16,24},{20,28},{24,16},{28,20},{1,9},{5... | collective-permute-start | bytes 3145736 | tf_op jit(solution)/shard_map/ppermute | solution.py:475
  2.7 25.5 %collective-permute-start.6 = (f32[4,256,256]{2,1,0:T(8,128)}, f32[4,256,256]{2,1,0:T(8,128)S(1)}, u32[]{:S(2)}, u32[]{:S(2)}) collective-permute-start(f32[4,256,256]{2,1,0:T(8,128)} %bitcast.13), channel_id=1, source_target_pairs={{0,1},{1,0},{2,3},{3,2},{4,5},{5,4},{6,7},{7,6},{8,16},{9,17},{10,... | collective-permute-start | bytes 3145736 | tf_op jit(solution)/shard_map/ppermute | solution.py:475
  6.1 26.6 %collective-permute-start.1 = (s32[8]{0:T(128)S(1)}, s32[8]{0:T(128)S(1)}, u32[]{:S(2)}, u32[]{:S(2)}) collective-permute-start(s32[8]{0:T(128)S(1)} %pad_add_fusion.table), channel_id=1, source_target_pairs={{0,4},{4,0},{8,12},{12,8},{16,20},{20,16},{24,28},{28,24},{1,5},{5... | collective-permute-start | bytes 104 | tf_op jit(solution)/shard_map/ppermute | solution.py:475
  6.6 26.6 %collective-permute-start.2 = (s32[8]{0:T(128)S(1)}, s32[8]{0:T(128)S(1)}, u32[]{:S(2)}, u32[]{:S(2)}) collective-permute-start(s32[8]{0:T(128)S(1)} %pad_add_fusion.table), channel_id=1, source_target_pairs={{0,8},{4,12},{8,0},{12,4},{16,24},{20,28},{24,16},{28,20},{1,9},{5... | collective-permute-start | bytes 104 | tf_op jit(solution)/shard_map/ppermute | solution.py:475
  6.6 25.8 %copy-start.1 = (f32[1,4,256,256]{3,2,1,0:T(8,128)S(1)}, f32[1,4,256,256]{3,2,1,0:T(8,128)}, u32[]{:S(2)}) copy-start(f32[1,4,256,256]{3,2,1,0:T(8,128)} %param.5) | copy-start | bytes 3145732
  8.9 81.7 %copy-start = (f32[1,4,4,256,256]{4,3,2,1,0:T(8,128)S(1)}, f32[1,4,4,256,256]{4,3,2,1,0:T(8,128)}, u32[]{:S(2)}) copy-start(f32[1,4,4,256,256]{4,3,2,1,0:T(8,128)} %param.7) | copy-start | bytes 12582916
  8.9 81.7 %copy-start.2 = (f32[1,4,256,256]{3,2,1,0:T(8,128)S(1)}, f32[1,4,256,256]{3,2,1,0:T(8,128)}, u32[]{:S(2)}) copy-start(f32[1,4,256,256]{3,2,1,0:T(8,128)} %param.6) | copy-start | bytes 3145732
  25.8 27.6 %collective-permute-start.16 = (f32[1,256,256]{2,1,0:T(8,128)S(1)}, f32[1,256,256]{2,1,0:T(8,128)S(1)}, u32[]{:S(2)}, u32[]{:S(2)}) collective-permute-start(f32[1,256,256]{2,1,0:T(8,128)S(1)} %get-tuple-element.45), channel_id=1, source_target_pairs={{0,8},{4,12},{8,0},{12,4},{16,24},{20,28},{24,16},{28,20},{1,9},{5... | collective-permute-start | bytes 786440 | tf_op jit(solution)/shard_map/ppermute | solution.py:475
  27.1 28.9 %collective-permute-start.12 = (f32[4,256,256]{2,1,0:T(8,128)S(1)}, f32[4,256,256]{2,1,0:T(8,128)S(1)}, u32[]{:S(2)}, u32[]{:S(2)}) collective-permute-start(f32[4,256,256]{2,1,0:T(8,128)S(1)} %get-tuple-element.33), channel_id=1, source_target_pairs={{0,4},{4,0},{8,12},{12,8},{16,20},{20,16},{24,28},{28,24},{1,5},{5... | collective-permute-start | bytes 3145736 | tf_op jit(solution)/shard_map/ppermute | solution.py:475
  28.2 27.9 %collective-permute-start.9 = (f32[4,256,256]{2,1,0:T(8,128)S(1)}, f32[4,256,256]{2,1,0:T(8,128)S(1)}, u32[]{:S(2)}, u32[]{:S(2)}) collective-permute-start(f32[4,256,256]{2,1,0:T(8,128)S(1)} %collective-permute-done.4.refs_1_.refs_6_), channel_id=1, source_target_pairs={{0,8},{8,16},{12,4},{16,24},{20,12},{28,20},{1,9},{9,17},{13,5},{1... | collective-permute-start | bytes 3145736 | tf_op jit(solution)/shard_map/ppermute | solution.py:475
  32.7 20.7 %collective-permute-start.3 = (s32[8]{0:T(128)S(1)}, s32[8]{0:T(128)S(1)}, u32[]{:S(2)}, u32[]{:S(2)}) collective-permute-start(s32[8]{0:T(128)S(1)} %pad_add_fusion.table), channel_id=1, source_target_pairs={{0,1},{1,0},{2,3},{3,2},{4,5},{5,4},{6,7},{7,6},{8,16},{9,17},{10,... | collective-permute-start | bytes 104 | tf_op jit(solution)/shard_map/ppermute | solution.py:475
  33.2 20.2 %collective-permute-start = (s32[8]{0:T(128)S(1)}, s32[8]{0:T(128)S(1)}, u32[]{:S(2)}, u32[]{:S(2)}) collective-permute-start(s32[8]{0:T(128)S(1)} %pad_add_fusion.table), channel_id=1, source_target_pairs={{0,1},{1,0},{2,3},{3,2},{4,8},{5,9},{6,10},{7,11},{8,4},{9,5},{10,... | collective-permute-start | bytes 104 | tf_op jit(solution)/shard_map/ppermute | solution.py:475
  53.4 26.9 %collective-permute-start.13 = (f32[4,256,256]{2,1,0:T(8,128)S(1)}, f32[4,256,256]{2,1,0:T(8,128)S(1)}, u32[]{:S(2)}, u32[]{:S(2)}) collective-permute-start(f32[4,256,256]{2,1,0:T(8,128)S(1)} %get-tuple-element.34), channel_id=1, source_target_pairs={{0,1},{1,0},{2,3},{3,2},{4,8},{5,9},{6,10},{7,11},{8,4},{9,5},{10,... | collective-permute-start | bytes 3145736 | tf_op jit(solution)/shard_map/ppermute | solution.py:475
  53.4 26.9 %collective-permute-start.7 = (f32[4,256,256]{2,1,0:T(8,128)S(1)}, f32[4,256,256]{2,1,0:T(8,128)S(1)}, u32[]{:S(2)}, u32[]{:S(2)}) collective-permute-start(f32[4,256,256]{2,1,0:T(8,128)S(1)} %get-tuple-element.26), channel_id=1, source_target_pairs={{0,1},{1,0},{2,3},{3,2},{4,5},{5,4},{6,7},{7,6},{8,9},{9,8},{10,11... | collective-permute-start | bytes 3145736 | tf_op jit(solution)/shard_map/ppermute | solution.py:475
  53.4 29.5 %collective-permute-start.8 = (f32[4,256,256]{2,1,0:T(8,128)S(1)}, f32[4,256,256]{2,1,0:T(8,128)S(1)}, u32[]{:S(2)}, u32[]{:S(2)}) collective-permute-start(f32[4,256,256]{2,1,0:T(8,128)S(1)} %get-tuple-element.27), channel_id=1, source_target_pairs={{1,2},{2,1},{5,6},{6,5},{9,10},{10,9},{13,14},{14,13},{17,18},{18,... | collective-permute-start | bytes 3145736 | tf_op jit(solution)/shard_map/ppermute | solution.py:475
  56.0 47.0 %collective-permute-start.17 = (f32[2,256,256]{2,1,0:T(8,128)S(1)}, f32[2,256,256]{2,1,0:T(8,128)S(1)}, u32[]{:S(2)}, u32[]{:S(2)}) collective-permute-start(f32[2,256,256]{2,1,0:T(8,128)S(1)} %get-tuple-element.46), channel_id=1, source_target_pairs={{0,8},{4,12},{8,0},{12,4},{16,24},{20,28},{24,16},{28,20},{1,9},{5... | collective-permute-start | bytes 1572872 | tf_op jit(solution)/shard_map/ppermute | solution.py:475
  56.1 46.9 %collective-permute-start.19 = (f32[2,256,256]{2,1,0:T(8,128)S(1)}, f32[2,256,256]{2,1,0:T(8,128)S(1)}, u32[]{:S(2)}, u32[]{:S(2)}) collective-permute-start(f32[2,256,256]{2,1,0:T(8,128)S(1)} %get-tuple-element.48), channel_id=1, source_target_pairs={{0,1},{1,0},{2,3},{3,2},{4,5},{5,4},{6,7},{7,6},{8,16},{9,17},{10,... | collective-permute-start | bytes 1572872 | tf_op jit(solution)/shard_map/ppermute | solution.py:475
  80.3 5.2 %collective-permute-start.10 = (f32[1,256,256]{2,1,0:T(8,128)S(1)}, f32[1,256,256]{2,1,0:T(8,128)S(1)}, u32[]{:S(2)}, u32[]{:S(2)}) collective-permute-start(f32[1,256,256]{2,1,0:T(8,128)S(1)} %get-tuple-element.29), channel_id=1, source_target_pairs={{0,1},{1,0},{2,3},{3,2},{4,5},{5,4},{6,7},{7,6},{8,9},{9,8},{10,11... | collective-permute-start | bytes 786440 | tf_op jit(solution)/shard_map/ppermute | solution.py:475
  80.4 7.7 %collective-permute-start.11 = (f32[1,256,256]{2,1,0:T(8,128)S(1)}, f32[1,256,256]{2,1,0:T(8,128)S(1)}, u32[]{:S(2)}, u32[]{:S(2)}) collective-permute-start(f32[1,256,256]{2,1,0:T(8,128)S(1)} %get-tuple-element.30), channel_id=1, source_target_pairs={{1,2},{2,1},{5,6},{6,5},{9,10},{10,9},{13,14},{14,13},{17,18},{18,... | collective-permute-start | bytes 786440 | tf_op jit(solution)/shard_map/ppermute | solution.py:475
  82.9 20.1 %collective-permute-start.18 = (f32[1,256,256]{2,1,0:T(8,128)S(1)}, f32[1,256,256]{2,1,0:T(8,128)S(1)}, u32[]{:S(2)}, u32[]{:S(2)}) collective-permute-start(f32[1,256,256]{2,1,0:T(8,128)S(1)} %get-tuple-element.47), channel_id=1, source_target_pairs={{0,1},{1,0},{2,3},{3,2},{4,5},{5,4},{6,7},{7,6},{8,16},{9,17},{10,... | collective-permute-start | bytes 786440 | tf_op jit(solution)/shard_map/ppermute | solution.py:475
  85.5 18.6 %collective-permute-start.14 = (f32[1,256,256]{2,1,0:T(8,128)S(1)}, f32[1,256,256]{2,1,0:T(8,128)S(1)}, u32[]{:S(2)}, u32[]{:S(2)}) collective-permute-start(f32[1,256,256]{2,1,0:T(8,128)S(1)} %get-tuple-element.39), channel_id=1, source_target_pairs={{0,8},{4,12},{8,0},{12,4},{16,24},{20,28},{24,16},{28,20},{1,9},{5... | collective-permute-start | bytes 786440 | tf_op jit(solution)/shard_map/ppermute | solution.py:475
  88.0 16.1 %collective-permute-start.15 = (f32[1,256,256]{2,1,0:T(8,128)S(1)}, f32[1,256,256]{2,1,0:T(8,128)S(1)}, u32[]{:S(2)}, u32[]{:S(2)}) collective-permute-start(f32[1,256,256]{2,1,0:T(8,128)S(1)} %get-tuple-element.40), channel_id=1, source_target_pairs={{0,1},{1,0},{2,3},{3,2},{4,5},{5,4},{6,7},{7,6},{8,16},{9,17},{10,... | collective-permute-start | bytes 786440 | tf_op jit(solution)/shard_map/ppermute | solution.py:475
